TPU v7x, 32 devices: a whole 2x2x4 slice. The times are simulated.
32 devices in a mesh: grp: 2 (over x), ev: 4 (over y, core), hd: 4 (over z).
Axes of the slice: x: 2, y: 2, z: 4, core: 2. Of those that a mesh axis runs over, the one named last changes fastest.
Arguments:
- hist_keys: bfloat16 [8, 16384, 1024], P('grp', 'ev', 'hd'), parts along dimension 0, may hold values from -6 to 6
- hist_values: bfloat16 [8, 16384, 1024], P('grp', 'ev', 'hd'), parts along dimension 0, may hold values from -6 to 6
- hist_len: int32 [8], P('grp'), parts along dimension 0, may hold values from 4096 to 16384
- new_queries: bfloat16 [8, 1024, 1024], P('grp', 'ev', 'hd'), parts along dimension 0, may hold values from -6 to 6
- event_gate: bfloat16 [8, 1024, 1024], P('grp', 'ev', 'hd'), parts along dimension 0, may hold values from -6 to 6
- key_weight: bfloat16 [1024, 1024], P(None, 'hd'), may hold values from -0.1875 to 0.1875
- value_weight: bfloat16 [1024, 1024], P(None, 'hd'), may hold values from -0.1875 to 0.1875
- event_gain: float32 [1024], P('hd'), may hold values from 0.25 to 1.75
- cand_queries: bfloat16 [4096, 1024], P(('grp', 'ev'), 'hd'), parts along dimension 0, may hold values from -6 to 6
- cand_gate: bfloat16 [4096, 1024], P(('grp', 'ev'), 'hd'), parts along dimension 0, may hold values from -6 to 6
- cand_gain: float32 [1024], P('hd'), may hold values from 0.25 to 1.75
- block_user: int32 [32], P(('grp', 'ev')), parts along dimension 0, may hold values from 0 to 3, as said below
- cand_count: int32 [8], P('grp'), parts along dimension 0, may hold values from 1 to 1024, as said below
Outputs:
- event_out: bfloat16 [8, 1024, 1024], P('grp', 'ev', 'hd'), parts along dimension 0
- cand_out: bfloat16 [4096, 1024], P(('grp', 'ev'), 'hd'), parts along dimension 0
There are 2 independent parts, one for each index of `grp`. A program takes and returns all parts, laid end to end along the dimension named above; an argument that names none is the same for every part. Nothing has to cross between parts.
Inputs may be any that keep to these rules, and one draw needn't show every extreme that they name: `block_user`: blocks belong to users in order: the first ceil(cand_count[0] / 128) blocks to user 0, the next ceil(cand_count[1] / 128) to user 1, and so on; every user has at least one block and all 16 blocks are used. `cand_count`: the blocks of users add up to 16 as stated for block_user; one user has exactly 8 full blocks.
All inputs are finite; a program needn't handle non-finite values.
Results may differ from a plain program's by a relative error of at most 0.0072.
Values may be sent and summed in bfloat16 or wider, within the bound.
No kernel may reach another device: no remote copies, remote signals or barrier semaphores. Data moves between devices by JAX's collectives and lax.ppermute only.
A program may use at most 128 MiB of HBM per device.

v0:
```python
import jax
import jax.numpy as jnp
from jax import lax
from jax.sharding import PartitionSpec as P

HEAD = 128
BLOCK = 128


EPSILON = 1e-05


def head_norm(values, gain):
    centre = jnp.mean(values, axis=-1, keepdims=True)
    shifted = values - centre
    spread = jnp.mean(shifted * shifted, axis=-1, keepdims=True)
    return shifted * lax.rsqrt(spread + EPSILON) * gain


def local(
    hist_keys,
    hist_values,
    hist_len,
    new_queries,
    event_gate,
    key_weight,
    value_weight,
    event_gain,
    cand_queries,
    cand_gate,
    cand_gain,
    block_user,
    cand_count,
):
    n_users, hist_rows, col_width = hist_keys.shape
    n_heads = col_width // HEAD
    score_scale = HEAD ** (-0.5)
    key_block = min(1024, hist_rows)
    n_blocks = hist_rows // key_block
    keys_split = hist_keys.reshape(n_users, n_blocks, key_block, n_heads, HEAD)
    values_split = hist_values.reshape(n_users, n_blocks, key_block, n_heads, HEAD)
    event_base = lax.axis_index("ev") * hist_rows
    pieces = lax.all_gather(new_queries, "ev", axis=1, tiled=True)
    n_rows = pieces.shape[1]
    queries_here = pieces.reshape(n_users, n_rows, n_heads, HEAD)

    def history_step(total, block_idx):
        keys_here = lax.dynamic_index_in_dim(keys_split, block_idx, 1, keepdims=False)
        values_here = lax.dynamic_index_in_dim(values_split, block_idx, 1, keepdims=False)
        scores = (
            jnp.einsum(
                "unhd,ukhd->uhnk", queries_here, keys_here, preferred_element_type=jnp.float32
            )
            * score_scale
        )
        position = event_base + block_idx * key_block + jnp.arange(key_block, dtype=jnp.int32)
        alive = (position[None, :] < hist_len[:, None]).astype(jnp.float32)
        weights = (jax.nn.silu(scores) * alive[:, None, None, :]).astype(jnp.bfloat16)
        return (
            total
            + jnp.einsum(
                "uhnk,ukhd->unhd", weights, values_here, preferred_element_type=jnp.float32
            ),
            None,
        )

    total, _ = lax.scan(
        history_step,
        jnp.zeros((n_users, n_rows, n_heads, HEAD), jnp.float32),
        jnp.arange(n_blocks, dtype=jnp.int32),
    )
    partial_sum = total.reshape(n_users, n_rows, col_width)
    blocks_here = block_user.shape[0]
    cand_split = cand_queries.reshape(blocks_here, BLOCK, n_heads, HEAD)
    user_ids = jnp.arange(n_users, dtype=jnp.int32)
    owner_table = block_user[:, None] == user_ids[None, :]
    owner_pick = owner_table.astype(jnp.bfloat16)
    attended = lax.psum_scatter(partial_sum, "ev", scatter_dimension=1, tiled=True)
    rows_here = attended.shape[1]
    shaped = attended.reshape(n_users, rows_here, n_heads, HEAD)
    gate_f = event_gate.astype(jnp.float32).reshape(n_users, rows_here, n_heads, HEAD)
    event_out = (
        (head_norm(shaped, event_gain.reshape(n_heads, HEAD)) * gate_f)
        .astype(jnp.bfloat16)
        .reshape(n_users, rows_here, col_width)
    )
    rows_here = event_out.shape[1]
    flat = event_out.reshape(n_users * rows_here, col_width)
    pieces = lax.all_gather(flat, "hd", axis=1, tiled=True)
    key_sum = jnp.dot(pieces, key_weight, preferred_element_type=jnp.float32)
    value_sum = jnp.dot(pieces, value_weight, preferred_element_type=jnp.float32)
    fresh_keys = key_sum.astype(jnp.bfloat16).reshape(n_users, rows_here, col_width)
    fresh_values = value_sum.astype(jnp.bfloat16).reshape(n_users, rows_here, col_width)
    keys_piece = lax.all_gather(fresh_keys, "ev", axis=1, tiled=True)
    values_piece = lax.all_gather(fresh_values, "ev", axis=1, tiled=True)
    n_rows = keys_piece.shape[1]
    keys_own = jnp.dot(
        owner_pick,
        keys_piece.reshape(n_users, n_rows * col_width),
        preferred_element_type=jnp.float32,
    )
    keys_own = keys_own.astype(jnp.bfloat16).reshape(blocks_here, n_rows, n_heads, HEAD)
    values_own = jnp.dot(
        owner_pick,
        values_piece.reshape(n_users, n_rows * col_width),
        preferred_element_type=jnp.float32,
    )
    values_own = values_own.astype(jnp.bfloat16).reshape(blocks_here, n_rows, n_heads, HEAD)
    scores = (
        jnp.einsum("bchd,brhd->bhcr", cand_split, keys_own, preferred_element_type=jnp.float32)
        * score_scale
    )
    weights = jax.nn.silu(scores).astype(jnp.bfloat16)
    cand_attn = jnp.einsum(
        "bhcr,brhd->bchd", weights, values_own, preferred_element_type=jnp.float32
    )
    block_count = (cand_count + BLOCK - 1) // BLOCK
    first_block = jnp.cumsum(block_count) - block_count
    owner_int = owner_table.astype(jnp.int32)
    own_first = jnp.sum(owner_int * first_block[None, :], axis=1)
    own_limit = jnp.sum(owner_int * cand_count[None, :], axis=1)
    block_global = lax.axis_index("ev") * blocks_here + jnp.arange(blocks_here, dtype=jnp.int32)
    row_pos = (block_global - own_first)[:, None] * BLOCK + jnp.arange(BLOCK, dtype=jnp.int32)[
        None, :
    ]
    valid = (row_pos < own_limit[:, None]).astype(jnp.float32)
    gate_c = cand_gate.astype(jnp.float32).reshape(blocks_here, BLOCK, n_heads, HEAD)
    cand_out = (
        head_norm(cand_attn, cand_gain.reshape(n_heads, HEAD)) * gate_c * valid[:, :, None, None]
    ).astype(jnp.bfloat16)
    return (event_out, cand_out.reshape(blocks_here * BLOCK, col_width))


def solution(mesh):
    return jax.shard_map(
        local,
        mesh=mesh,
        in_specs=(
            P("grp", "ev", "hd"),
            P("grp", "ev", "hd"),
            P("grp"),
            P("grp", "ev", "hd"),
            P("grp", "ev", "hd"),
            P(None, "hd"),
            P(None, "hd"),
            P("hd"),
            P(("grp", "ev"), "hd"),
            P(("grp", "ev"), "hd"),
            P("hd"),
            P(("grp", "ev")),
            P("grp"),
        ),
        out_specs=(P("grp", "ev", "hd"), P(("grp", "ev"), "hd")),
        check_vma=False,
    )
```

profile of v0, /device:TPU:0, one launch (start us, length us, event | category | flops | bytes accessed | tf_op | source)
XLA Modules:
  0.0 361.0 jit_solution(16850112253524450805)
XLA Ops:
  7.2 2.1 copy.34
  9.4 12.8 %reshape.194 = bf16[4,4,1024,2,128]{4,3,2,1,0:T(2,128)(2,1)} reshape(bf16[4,4096,256]{2,1,0:T(8,128)(2,1)} %param.16) | data formatting | bytes 16777216 | tf_op jit(solution)/shard_map/reshape | solution.py:41
  22.2 12.5 %reshape.195 = bf16[4,4,1024,2,128]{4,3,2,1,0:T(2,128)(2,1)} reshape(bf16[4,4096,256]{2,1,0:T(8,128)(2,1)} %param.15) | data formatting | bytes 16777216 | tf_op jit(solution)/shard_map/reshape | solution.py:40
  35.7 4.0 %copy.37 = bf16[4,1024,2,128]{3,1,2,0:T(8,128)(2,1)} copy(bf16[4,1024,2,128]{1,3,2,0:T(8,128)(2,1)} %bitcast.111) | data formatting | bytes 4194304
  39.7 132.6 %while.11 = (s32[]{:T(128)}, f32[4,1024,2,128]{1,3,2,0:T(8,128)}, s32[4]{0:T(128)S(1)}, bf16[4,4,1024,2,128]{4,3,2,1,0:T(2,128)(2,1)}, bf16[4,4,1024,2,128]{4,3,...) while((s32[]{:T(128)}, f32[4,1024,2,128]{1,3,2,0:T(8,128)}, ...), condition=%wide.region_1.2_spmd.clone, body=%wide.region_0.1_spmd.clone.sunk | while | flops 4355793920 | bytes 27304156 | solution.py:67
  42.2 6.5 %constant_dynamic-slice_fusion.3 = (bf16[4,1,1024,2,128]{4,3,2,1,0:T(2,128)(2,1)}, bf16[4,1,1024,2,128]{4,3,2,1,0:T(2,128)(2,1)S(1)}) fusion(bf16[4,4,1024,2,128]{4,3,2,1,0:T(2,128)(2,1)} %get-tuple-element.191, s32[]{:T(128)S(6)} %select_n.18, bf16[4,4,1024,2,128]{4,3,2,1,0:T(2,128)(2,1)} %get-tuple-element.190), kind=kLoop, calls=%fused_computation.14.clone.1 | loop fusion | bytes 8388612 | tf_op jit(solution)/shard_map/while/body/eval_jaxpr/jit(dynamic_index_in_dim)/dynamic_slice | solution.py:48
  48.7 3.9 %copy.82 = bf16[4,1,1024,2,128]{2,4,3,0,1:T(8,128)(2,1)} copy(bf16[4,1,1024,2,128]{4,3,2,1,0:T(2,128)(2,1)S(1)} %get-tuple-element.162) | data formatting | bytes 4194304 | tf_op jit(solution)/shard_map/while/body/eval_jaxpr/jit(dynamic_index_in_dim)/dynamic_slice | solution.py:49
  53.3 19.0 %bitcast_add_fusion.2 = f32[4,1024,2,128]{1,3,2,0:T(8,128)} fusion(f32[4,1024,2,128]{1,3,2,0:T(8,128)} %get-tuple-element.176, f32[4,1024]{1,0:T(4,128)S(1)} %compare_convert_fusion.2, bf16[4,1024,2,128]{3,1,2,0:T(8,128)(2,1)} %get-tuple-element.192, bf16[4,1,1024,2,128]{4,3,2,1,0:T(2,128)(2,1)} %get-tuple-element.161, ...), kind=kOutput, calls=%fused_computation.8.clone.1 | convolution fusion | flops 4355784704 | bytes 14696449 | tf_op jit(solution)/shard_map/while/body/eval_jaxpr/uhnk,ukhd->unhd/dot_general | solution.py:61
  74.8 6.5 %constant_dynamic-slice_fusion.3 = (bf16[4,1,1024,2,128]{4,3,2,1,0:T(2,128)(2,1)}, bf16[4,1,1024,2,128]{4,3,2,1,0:T(2,128)(2,1)S(1)}) fusion(bf16[4,4,1024,2,128]{4,3,2,1,0:T(2,128)(2,1)} %get-tuple-element.191, s32[]{:T(128)S(6)} %select_n.18, bf16[4,4,1024,2,128]{4,3,2,1,0:T(2,128)(2,1)} %get-tuple-element.190), kind=kLoop, calls=%fused_computation.14.clone.1 | loop fusion | bytes 8388612 | tf_op jit(solution)/shard_map/while/body/eval_jaxpr/jit(dynamic_index_in_dim)/dynamic_slice | solution.py:48
  81.3 3.9 %copy.82 = bf16[4,1,1024,2,128]{2,4,3,0,1:T(8,128)(2,1)} copy(bf16[4,1,1024,2,128]{4,3,2,1,0:T(2,128)(2,1)S(1)} %get-tuple-element.162) | data formatting | bytes 4194304 | tf_op jit(solution)/shard_map/while/body/eval_jaxpr/jit(dynamic_index_in_dim)/dynamic_slice | solution.py:49
  85.9 19.7 %bitcast_add_fusion.2 = f32[4,1024,2,128]{1,3,2,0:T(8,128)} fusion(f32[4,1024,2,128]{1,3,2,0:T(8,128)} %get-tuple-element.176, f32[4,1024]{1,0:T(4,128)S(1)} %compare_convert_fusion.2, bf16[4,1024,2,128]{3,1,2,0:T(8,128)(2,1)} %get-tuple-element.192, bf16[4,1,1024,2,128]{4,3,2,1,0:T(2,128)(2,1)} %get-tuple-element.161, ...), kind=kOutput, calls=%fused_computation.8.clone.1 | convolution fusion | flops 4355784704 | bytes 14696449 | tf_op jit(solution)/shard_map/while/body/eval_jaxpr/uhnk,ukhd->unhd/dot_general | solution.py:61
  108.1 6.5 %constant_dynamic-slice_fusion.3 = (bf16[4,1,1024,2,128]{4,3,2,1,0:T(2,128)(2,1)}, bf16[4,1,1024,2,128]{4,3,2,1,0:T(2,128)(2,1)S(1)}) fusion(bf16[4,4,1024,2,128]{4,3,2,1,0:T(2,128)(2,1)} %get-tuple-element.191, s32[]{:T(128)S(6)} %select_n.18, bf16[4,4,1024,2,128]{4,3,2,1,0:T(2,128)(2,1)} %get-tuple-element.190), kind=kLoop, calls=%fused_computation.14.clone.1 | loop fusion | bytes 8388612 | tf_op jit(solution)/shard_map/while/body/eval_jaxpr/jit(dynamic_index_in_dim)/dynamic_slice | solution.py:48
  114.6 3.9 %copy.82 = bf16[4,1,1024,2,128]{2,4,3,0,1:T(8,128)(2,1)} copy(bf16[4,1,1024,2,128]{4,3,2,1,0:T(2,128)(2,1)S(1)} %get-tuple-element.162) | data formatting | bytes 4194304 | tf_op jit(solution)/shard_map/while/body/eval_jaxpr/jit(dynamic_index_in_dim)/dynamic_slice | solution.py:49
  119.2 19.7 %bitcast_add_fusion.2 = f32[4,1024,2,128]{1,3,2,0:T(8,128)} fusion(f32[4,1024,2,128]{1,3,2,0:T(8,128)} %get-tuple-element.176, f32[4,1024]{1,0:T(4,128)S(1)} %compare_convert_fusion.2, bf16[4,1024,2,128]{3,1,2,0:T(8,128)(2,1)} %get-tuple-element.192, bf16[4,1,1024,2,128]{4,3,2,1,0:T(2,128)(2,1)} %get-tuple-element.161, ...), kind=kOutput, calls=%fused_computation.8.clone.1 | convolution fusion | flops 4355784704 | bytes 14696449 | tf_op jit(solution)/shard_map/while/body/eval_jaxpr/uhnk,ukhd->unhd/dot_general | solution.py:61
  141.5 6.5 %constant_dynamic-slice_fusion.3 = (bf16[4,1,1024,2,128]{4,3,2,1,0:T(2,128)(2,1)}, bf16[4,1,1024,2,128]{4,3,2,1,0:T(2,128)(2,1)S(1)}) fusion(bf16[4,4,1024,2,128]{4,3,2,1,0:T(2,128)(2,1)} %get-tuple-element.191, s32[]{:T(128)S(6)} %select_n.18, bf16[4,4,1024,2,128]{4,3,2,1,0:T(2,128)(2,1)} %get-tuple-element.190), kind=kLoop, calls=%fused_computation.14.clone.1 | loop fusion | bytes 8388612 | tf_op jit(solution)/shard_map/while/body/eval_jaxpr/jit(dynamic_index_in_dim)/dynamic_slice | solution.py:48
  147.9 3.9 %copy.82 = bf16[4,1,1024,2,128]{2,4,3,0,1:T(8,128)(2,1)} copy(bf16[4,1,1024,2,128]{4,3,2,1,0:T(2,128)(2,1)S(1)} %get-tuple-element.162) | data formatting | bytes 4194304 | tf_op jit(solution)/shard_map/while/body/eval_jaxpr/jit(dynamic_index_in_dim)/dynamic_slice | solution.py:49
  152.6 19.7 %bitcast_add_fusion.2 = f32[4,1024,2,128]{1,3,2,0:T(8,128)} fusion(f32[4,1024,2,128]{1,3,2,0:T(8,128)} %get-tuple-element.176, f32[4,1024]{1,0:T(4,128)S(1)} %compare_convert_fusion.2, bf16[4,1024,2,128]{3,1,2,0:T(8,128)(2,1)} %get-tuple-element.192, bf16[4,1,1024,2,128]{4,3,2,1,0:T(2,128)(2,1)} %get-tuple-element.161, ...), kind=kOutput, calls=%fused_computation.8.clone.1 | convolution fusion | flops 4355784704 | bytes 14696449 | tf_op jit(solution)/shard_map/while/body/eval_jaxpr/uhnk,ukhd->unhd/dot_general | solution.py:61
  172.2 5.4 %copy.47 = f32[4,1024,256]{2,1,0:T(8,128)} copy(f32[4,1024,256]{1,2,0:T(8,128)} %bitcast.108) | data formatting | bytes 8388608 | tf_op jit(solution)/shard_map/reshape | solution.py:72
  177.7 46.4 %reduce-scatter.2.cloned.1.call-done = f32[4,256,256]{2,1,0:T(8,128)} async-done(((f32[4,1024,256]{2,1,0:T(8,128)}), f32[4,256,256]{2,1,0:T(8,128)}) %reduce-scatter.2.cloned.1.call-update) | async-done | bytes 1048592 | tf_op jit(solution)/shard_map/reduce_scatter | solution.py:78
  227.0 14.6 %multiply_reduce_fusion = f32[4,256,2]{2,1,0:T(8,128)S(1)} fusion(f32[4,256,2,128]{3,2,1,0:T(2,128)S(1)} %reshape.198, f32[4,256,2]{2,1,0:T(8,128)S(1)} %broadcast_multiply_fusion), kind=kLoop, calls=%fused_computation.38 | loop fusion | flops 784384 | bytes 1064960 | tf_op jit(solution)/shard_map/reduce_sum | solution.py:16
  246.3 46.4 %all-gather.7.cloned.1.call-done = bf16[1024,1024]{1,0:T(8,128)(2,1)} async-done(((bf16[1024,256]{1,0:T(8,128)(2,1)}), bf16[1024,1024]{1,0:T(8,128)(2,1)}) %all-gather.7.cloned.1.call-update) | async-done | bytes 2097168 | tf_op jit(solution)/shard_map/all_gather | solution.py:89
  292.6 3.1 convolution_convert_fusion.3
  295.9 3.3 convolution_convert_fusion.2
  306.3 3.1 sub.46
  309.5 2.3 multiply_convert_fusion
  311.7 5.0 %all-gather.9.cloned.1.call-done = bf16[4,1024,256]{2,1,0:T(8,128)(2,1)} async-done(((bf16[4,256,256]{2,1,0:T(8,128)(2,1)}), bf16[4,1024,256]{2,1,0:T(8,128)(2,1)}) %all-gather.9.cloned.1.call-update) | async-done | bytes 2097168 | tf_op jit(solution)/shard_map/all_gather | solution.py:95
  316.7 3.2 copy.52
  321.2 3.4 reshape.203
  324.7 16.0 %all-gather.11.cloned.1.call-done = bf16[4,1024,256]{2,1,0:T(8,128)(2,1)} async-done(((bf16[4,256,256]{2,1,0:T(8,128)(2,1)}), bf16[4,1024,256]{2,1,0:T(8,128)(2,1)}) %all-gather.11.cloned.1.call-update) | async-done | bytes 2097168 | tf_op jit(solution)/shard_map/all_gather | solution.py:94
  340.7 3.2 copy.53
  345.2 3.6 %reshape.206 = bf16[4,1024,2,128]{3,2,1,0:T(2,128)(2,1)} reshape(bf16[4,262144]{1,0:T(4,128)(2,1)S(1)} %convolution_convert_fusion) | data formatting | bytes 4194304 | tf_op jit(solution)/shard_map/reshape | solution.py:102
  348.9 4.4 %fusion.36 = (f32[4,128,2]{1,2,0:T(2,128)S(1)}, f32[4,128,2,128]{1,3,2,0:T(8,128)S(1)}) fusion(bf16[4,1024,2,128]{3,2,1,0:T(2,128)(2,1)} %reshape.206, bf16[4,128,2,128]{3,2,1,0:T(2,128)(2,1)S(1)} %copy-done.7, bf16[4,1024,2,128]{3,2,1,0:T(2,128)(2,1)} %reshape.203), kind=kOutput, calls=%fused_computation.62 | convolution fusion | flops 543292416 | bytes 4984832 | tf_op jit(solution)/shard_map/bhcr,brhd->bchd/dot_general | solution.py:114
  (76 shorter events, 22.4 us)
Async XLA Ops:
  7.2 285.5 %copy-start = (bf16[1024,256]{1,0:T(8,128)(2,1)S(1)}, bf16[1024,256]{1,0:T(8,128)(2,1)}, u32[]{:S(2)}) copy-start(bf16[1024,256]{1,0:T(8,128)(2,1)} %param.21) | copy-start | bytes 1572868
  7.2 28.5 %all-gather.5.cloned.1.call-start = ((), (), s32[]{:S(2)}) async-start(), calls=%async_computation.1 | async-start | bytes 2621440 | tf_op jit(solution)/shard_map/all_gather | solution.py:43
  9.3 214.7 %reduce-scatter.2.cloned.1.call-start = ((), (), s32[]{:S(2)}) async-start(), calls=%async_computation.2 | async-start | bytes 5242880 | tf_op jit(solution)/shard_map/reduce_scatter | solution.py:78
  35.7 4.0 %copy-start.8 = (s32[4]{0:T(128)S(1)}, s32[4]{0:T(128)}, u32[]{:S(2)}) copy-start(s32[4]{0:T(128)} %param.17) | copy-start | bytes 52
  177.6 115.0 %all-gather.7.cloned.1.call-start = ((), (), s32[]{:S(2)}) async-start(), calls=%async_computation.3 | async-start | bytes 2621440 | tf_op jit(solution)/shard_map/all_gather | solution.py:89
  241.5 3.6 copy-start.1
  241.5 3.6 copy-start.4
  241.6 3.6 copy-start.10
  244.1 1.0 copy-start.2
  246.2 70.5 %all-gather.9.cloned.1.call-start = ((), (), s32[]{:S(2)}) async-start(), calls=%async_computation.4 | async-start | bytes 2621440 | tf_op jit(solution)/shard_map/all_gather | solution.py:95
  295.8 5.1 %copy-start.12 = (s32[4]{0:T(128)S(1)}, s32[4]{0:T(128)}, u32[]{:S(2)}) copy-start(s32[4]{0:T(128)} %param.27) | copy-start | bytes 52
  295.8 5.3 %copy-start.6 = (bf16[512,256]{1,0:T(8,128)(2,1)S(1)}, bf16[512,256]{1,0:T(8,128)(2,1)}, u32[]{:S(2)}) copy-start(bf16[512,256]{1,0:T(8,128)(2,1)} %param.24) | copy-start | bytes 786436
  295.8 44.9 %all-gather.11.cloned.1.call-start = ((), (), s32[]{:S(2)}) async-start(), calls=%async_computation.5 | async-start | bytes 2621440 | tf_op jit(solution)/shard_map/all_gather | solution.py:94
  299.1 5.0 %copy-start.9 = (s32[4]{0:T(128)S(1)}, s32[4]{0:T(128)}, u32[]{:S(2)}) copy-start(s32[4]{0:T(128)} %param.26) | copy-start | bytes 52
  306.3 3.1 copy-start.3
  345.2 3.6 %copy-start.7 = (bf16[4,128,2,128]{3,2,1,0:T(2,128)(2,1)S(1)}, bf16[4,128,2,128]{3,2,1,0:T(2,128)(2,1)}, u32[]{:S(2)}) copy-start(bf16[4,128,2,128]{3,2,1,0:T(2,128)(2,1)} %reshape.207) | copy-start | bytes 786436
  348.9 4.6 %copy-start.5 = (f32[4,128,2,128]{1,3,2,0:T(8,128)S(1)}, f32[4,128,2,128]{1,3,2,0:T(8,128)}, u32[]{:S(2)}) copy-start(f32[4,128,2,128]{1,3,2,0:T(8,128)} %copy.43) | copy-start | bytes 1572868
  348.9 4.6 %copy-start.11 = (f32[256]{0:T(256)S(1)}, f32[256]{0:T(256)}, u32[]{:S(2)}) copy-start(f32[256]{0:T(256)} %param.25) | copy-start | bytes 3076
Sparse Core Ops, SparseCore 0:
  10.1 25.5 all-gather.4
  177.8 46.2 reduce-scatter.1
  246.4 46.2 all-gather.6
  295.9 20.7 all-gather.8
  318.1 22.5 all-gather.10
where the time goes:
time: 362 us; the launch traced here: 361 us
  waiting for transfers between devices  115 us (32%)
  local copies, waits for them, and re-layouts  110 us (30%)
  matrix products  91.5 us (25%)
  other arithmetic  20.2 us (6%)
  between operations  14 us (4%)
  loops' own time  10.4 us (3%)
    dot_general x4, matrix products, history_step(): jnp.einsum('uhnk,ukhd->unhd', weights, values_here, preferred_element_typ...  78 us
    all_gather x1, waiting for transfers between devices, local(): pieces = lax.all_gather(flat, 'hd', axis=1, tiled=True)  46.4 us
    reduce_scatter x1, waiting for transfers between devices, local(): lax.psum_scatter(partial_sum, 'ev', scatter_dimension=1, tiled=True)  46.4 us
    dynamic_slice x4, local copies, waits for them, and re-layouts, history_step(): lax.dynamic_index_in_dim(keys_split, block_idx, 1, keepdims=False)  25.9 us
    all_gather x1, waiting for transfers between devices, local(): keys_piece = lax.all_gather(fresh_keys, 'ev', axis=1, tiled=True)  16 us
    dynamic_slice x4, local copies, waits for them, and re-layouts, history_step(): lax.dynamic_index_in_dim(values_split, block_idx, 1, keepdims=False)  15.6 us
    reduce_sum x2, other arithmetic, head_norm(): spread = jnp.mean(shifted * shifted, axis=-1, keepdims=True)  14.6 us
    unnamed x31, local copies, waits for them, and re-layouts  14.3 us
  transfers between devices with their start and end apart: 5, of which 5 were waited for; matrix products, arithmetic and copies ran while one was open for 14% of the time, Pallas kernels for 0%

commit v1 on v0

v1 whole, which is shorter than its diff:
```python
import functools

import jax
import jax.numpy as jnp
from jax import lax
from jax.experimental import pallas as pl
from jax.experimental.pallas import tpu as pltpu
from jax.sharding import PartitionSpec as P

HEAD = 128
BLOCK = 128
EPSILON = 1e-05
SCALE = HEAD ** (-0.5)
HALF = 0.5 * SCALE
BF16 = jnp.bfloat16
F32 = jnp.float32


def qk(q, k):
    return lax.dot_general(q, k, (((1,), (1,)), ((), ())), preferred_element_type=F32)


def head_norm(values, gain):
    centre = jnp.mean(values, axis=-1, keepdims=True)
    shifted = values - centre
    spread = jnp.mean(shifted * shifted, axis=-1, keepdims=True)
    return shifted * lax.rsqrt(spread + EPSILON) * gain


def swap(x, axis, size, j):
    return lax.ppermute(x, axis, [(i, i ^ j) for i in range(size)])


def attend(user, q_list, odd, hist_len, place, keys, values):
    n = len(q_list)
    rows, width = q_list[0].shape
    hist_rows = keys.shape[1]
    tile = min(2048, hist_rows)
    steps = hist_rows // tile

    def kern(len_ref, place_ref, *refs):
        q_refs, (k_ref, v_ref), o_refs, acc = refs[:n], refs[n : n + 2], refs[n + 2 : 2 * n + 2], refs[-1]
        step = pl.program_id(1)
        left = len_ref[user] - place_ref[0] * hist_rows - step * tile

        @pl.when(step == 0)
        def _():
            acc[...] = jnp.zeros_like(acc)

        @pl.when(left > 0)
        def _():
            k = k_ref[0]
            row = lax.broadcasted_iota(jnp.int32, (tile, HEAD), 0)
            v = jnp.where(row < left, v_ref[0], jnp.zeros((tile, HEAD), BF16))
            for i in range(n):
                s = qk(q_refs[i][...], k).astype(BF16)
                w = s + s * jnp.tanh(s * BF16(HALF))
                acc[i] += jnp.dot(w, v, preferred_element_type=F32)

        @pl.when(step == steps - 1)
        def _():
            for i in range(n):
                o_refs[i][...] = (acc[i] * HALF).astype(o_refs[i].dtype)

    piece = pl.BlockSpec((rows, HEAD), lambda h, s, *_: (0, h))
    hist = pl.BlockSpec((1, tile, HEAD), lambda h, s, *_: (user, s, h))
    return pl.pallas_call(
        kern,
        grid_spec=pltpu.PrefetchScalarGridSpec(
            num_scalar_prefetch=2,
            grid=(width // HEAD, steps),
            in_specs=[piece] * n + [hist, hist],
            out_specs=[piece] * n,
            scratch_shapes=[pltpu.VMEM((n, rows, HEAD), F32)],
        ),
        out_shape=[jax.ShapeDtypeStruct((rows, width), BF16 if o else F32) for o in odd],
        name=f"attend{user}_{n}",
    )(hist_len, place, *q_list, keys, values)


def gate_events(user, parts, gain, gate):
    n = len(parts)
    rows, width = parts[0].shape

    def kern(*refs):
        p_refs, gain_ref, gate_ref, o_ref = refs[:n], refs[n], refs[n + 1], refs[n + 2]
        for h in range(width // HEAD):
            cols = slice(h * HEAD, (h + 1) * HEAD)
            total = p_refs[0][:, cols].astype(F32)
            for p in p_refs[1:]:
                total = total + p[:, cols].astype(F32)
            o_ref[:, cols] = (
                head_norm(total, gain_ref[:, cols]) * gate_ref[0, :, cols].astype(F32)
            ).astype(BF16)

    whole = pl.BlockSpec((rows, width), lambda i: (0, 0))
    return pl.pallas_call(
        kern,
        grid=(1,),
        in_specs=[whole] * n
        + [pl.BlockSpec((1, width), lambda i: (0, 0)), pl.BlockSpec((1, rows, width), lambda i: (user, 0, 0))],
        out_specs=whole,
        out_shape=jax.ShapeDtypeStruct((rows, width), BF16),
        name=f"gate{user}",
    )(*parts, gain, gate)


def project(user, n_users, pieces, column, key_weight, value_weight, fresh):
    n = len(pieces)
    rows, part = pieces[0].shape
    width = key_weight.shape[1]

    def kern(col_ref, *refs):
        p_refs, wk, wv = refs[:n], refs[n], refs[n + 1]
        k_ref, v_ref = refs[-2:]
        k = jnp.zeros((rows, width), F32)
        v = jnp.zeros((rows, width), F32)
        for j in range(n):
            from_row = pl.ds(pl.multiple_of((col_ref[0] ^ j) * part, part), part)
            k += jnp.dot(p_refs[j][...], wk[from_row, :], preferred_element_type=F32)
            v += jnp.dot(p_refs[j][...], wv[from_row, :], preferred_element_type=F32)
        k_ref[0] = k.astype(BF16)
        v_ref[0] = v.astype(BF16)

    full = lambda s: pl.BlockSpec(s, lambda i, *_: (0,) * len(s))
    slot = pl.BlockSpec((1, rows, width), lambda i, *_: (user, 0, 0))
    shape = jax.ShapeDtypeStruct((n_users, rows, width), BF16)
    extra = [] if fresh is None else list(fresh)
    return pl.pallas_call(
        kern,
        grid_spec=pltpu.PrefetchScalarGridSpec(
            num_scalar_prefetch=1,
            grid=(1,),
            in_specs=[full((rows, part))] * n
            + [full(key_weight.shape)] * 2
            + [pl.BlockSpec(memory_space=pl.ANY)] * len(extra),
            out_specs=[slot, slot],
        ),
        out_shape=[shape, shape],
        input_output_aliases={} if fresh is None else {n + 3: 0, n + 4: 1},
        name=f"project{user}",
    )(column, *pieces, key_weight, value_weight, *extra)


def user_of(block, count_ref, n_users):
    end = jnp.int32(0)
    user = jnp.int32(0)
    first = jnp.int32(0)
    for u in range(n_users - 1):
        end = end + lax.shift_right_logical(count_ref[u] + (BLOCK - 1), 7)
        past = block >= end
        user = jnp.where(past, u + 1, user)
        first = jnp.where(past, end, first)
    return user, first


def cand_sums(pieces, cand_count, place, keys, values):
    n = len(pieces)
    n_users, rows, width = keys.shape
    blocks = pieces[0].shape[0] // BLOCK

    def kern(count_ref, place_ref, *refs):
        q_refs, k_ref, v_ref, o_refs = refs[:n], refs[n], refs[n + 1], refs[n + 2 :]
        for j in range(n):
            for i in range(blocks):
                user, _ = user_of((place_ref[0] ^ j) * blocks + i, count_ref, n_users)
                for h in range(width // HEAD):
                    cols = slice(h * HEAD, (h + 1) * HEAD)
                    rws = slice(i * BLOCK, (i + 1) * BLOCK)
                    t = qk(q_refs[j][rws, cols], k_ref[user, :, cols]) * HALF
                    w = (t + t * jnp.tanh(t)).astype(BF16)
                    o = jnp.dot(w, v_ref[user, :, cols], preferred_element_type=F32)
                    o_refs[j][rws, cols] = o.astype(o_refs[j].dtype)

    full = lambda s: pl.BlockSpec(s, lambda i, *_: (0,) * len(s))
    piece = full(pieces[0].shape)
    return pl.pallas_call(
        kern,
        grid_spec=pltpu.PrefetchScalarGridSpec(
            num_scalar_prefetch=2,
            grid=(1,),
            in_specs=[piece] * n + [full(keys.shape)] * 2,
            out_specs=[piece] * n,
        ),
        out_shape=[jax.ShapeDtypeStruct(pieces[0].shape, BF16 if j & 1 else F32) for j in range(n)],
        name="cand_sums",
    )(cand_count, place, *pieces, keys, values)


def gate_cands(parts, cand_count, place, gain, gate):
    n = len(parts)
    n_users = cand_count.shape[0]
    rows, width = parts[0].shape

    def kern(count_ref, place_ref, *refs):
        p_refs, gain_ref, gate_ref, o_ref = refs[:n], refs[n], refs[n + 1], refs[n + 2]
        for i in range(rows // BLOCK):
            block = place_ref[0] * (rows // BLOCK) + i
            user, first = user_of(block, count_ref, n_users)
            limit = count_ref[user] - (block - first) * BLOCK
            live = lax.broadcasted_iota(jnp.int32, (BLOCK, HEAD), 0) < limit
            rws = slice(i * BLOCK, (i + 1) * BLOCK)
            for h in range(width // HEAD):
                cols = slice(h * HEAD, (h + 1) * HEAD)
                total = p_refs[0][rws, cols].astype(F32)
                for p in p_refs[1:]:
                    total = total + p[rws, cols].astype(F32)
                out = head_norm(total, gain_ref[:, cols]) * gate_ref[rws, cols].astype(F32)
                o_ref[rws, cols] = jnp.where(live, out, 0.0).astype(BF16)

    full = lambda s: pl.BlockSpec(s, lambda i, *_: (0,) * len(s))
    return pl.pallas_call(
        kern,
        grid_spec=pltpu.PrefetchScalarGridSpec(
            num_scalar_prefetch=2,
            grid=(1,),
            in_specs=[full((rows, width))] * n + [full((1, width)), full((rows, width))],
            out_specs=full((rows, width)),
        ),
        out_shape=jax.ShapeDtypeStruct((rows, width), BF16),
        name="gate_cands",
    )(cand_count, place, *parts, gain, gate)


def gather_pieces(x, axis, size):
    pieces = {0: x}
    for j in range(1, size):
        low = j & -j
        pieces[j] = None
    bit = size // 2
    while bit:
        for j in list(pieces):
            if pieces[j] is not None and pieces.get(j ^ bit, 0) is None:
                pieces[j ^ bit] = swap(pieces[j], axis, size, bit)
        bit //= 2
    return [pieces[j] for j in range(size)]


def scatter_sums(parts, axis, size):
    held = {j: [p] for j, p in enumerate(parts)}
    bit = 1
    while bit < size:
        for j in sorted(held):
            if j & bit:
                addends = held.pop(j)
                total = addends[0]
                if len(addends) > 1:
                    total = sum(a.astype(F32) for a in addends)
                held[j ^ bit].append(swap(total.astype(BF16), axis, size, bit))
        bit *= 2
    return held[0]


def make_local(n_ev, n_hd):
    def local(
        hist_keys,
        hist_values,
        hist_len,
        new_queries,
        event_gate,
        key_weight,
        value_weight,
        event_gain,
        cand_queries,
        cand_gate,
        cand_gain,
        block_user,
        cand_count,
    ):
        n_users, rows, width = new_queries.shape
        place = lax.axis_index("ev").astype(jnp.int32).reshape(1)
        column = lax.axis_index("hd").astype(jnp.int32).reshape(1)
        event_gain = event_gain.reshape(1, width)
        cand_gain = cand_gain.reshape(1, width)
        queries = [gather_pieces(new_queries[u], "ev", n_ev) for u in range(n_users)]
        cands = gather_pieces(cand_queries, "ev", n_ev)
        odd = [bool(j & 1) for j in range(n_ev)]
        event_out = []
        fresh = None
        for u in range(n_users):
            args = (hist_len, place, hist_keys, hist_values)
            if u == 0:
                parts = attend(u, queries[u][:1], odd[:1], *args)
                if n_ev > 1:
                    parts = parts + attend(u, queries[u][1:], odd[1:], *args)
            else:
                parts = attend(u, queries[u], odd, *args)
            gated = gate_events(u, scatter_sums(parts, "ev", n_ev), event_gain, event_gate)
            event_out.append(gated)
            pieces = [gated] + [swap(gated, "hd", n_hd, j) for j in range(1, n_hd)]
            fresh = project(u, n_users, pieces, column, key_weight, value_weight, fresh)
        sums = cand_sums(cands, cand_count, place, *fresh)
        cand_out = gate_cands(scatter_sums(sums, "ev", n_ev), cand_count, place, cand_gain, cand_gate)
        return jnp.stack(event_out), cand_out

    return local


def solution(mesh):
    return jax.shard_map(
        make_local(mesh.shape["ev"], mesh.shape["hd"]),
        mesh=mesh,
        in_specs=(
            P("grp", "ev", "hd"),
            P("grp", "ev", "hd"),
            P("grp"),
            P("grp", "ev", "hd"),
            P("grp", "ev", "hd"),
            P(None, "hd"),
            P(None, "hd"),
            P("hd"),
            P(("grp", "ev"), "hd"),
            P(("grp", "ev"), "hd"),
            P("hd"),
            P(("grp", "ev")),
            P("grp"),
        ),
        out_specs=(P("grp", "ev", "hd"), P(("grp", "ev"), "hd")),
        check_vma=False,
    )
```

time: 362 us -> 164 us (0.45)
  local copies, waits for them, and re-layouts: 110 us -> 4.82 us
  matrix products: 91.5 us -> 0 us
  waiting for transfers between devices: 115 us -> 26.4 us
  Pallas kernels: 0 us -> 82.2 us
  starting transfers between devices: 0.21 us -> 44.6 us
  other arithmetic: 20.2 us -> 3.02 us
  between operations: 14 us -> 1.13 us
  loops' own time: 10.4 us -> 0 us
    dot_general x9 -> x0, matrix products: 91.5 us -> none  [the longest x4 78 us: history_step(): jnp.einsum('uhnk,ukhd->unhd', weights, values_here, preferred_element_typ...]
    pallas_call x0 -> x15, Pallas kernels: none -> 82.2 us  [the longest x5 56.1 us: attend(): pl.pallas_call(kern, grid_spec=pltpu.PrefetchScalarGridSpec(num_scalar_pr...]
    all_gather x4 -> x0, waiting for transfers between devices: 68.3 us -> none  [the longest x1 46.4 us: local(): pieces = lax.all_gather(flat, 'hd', axis=1, tiled=True)]
    reduce_scatter x1 -> x0, waiting for transfers between devices: 46.4 us -> none  [local(): lax.psum_scatter(partial_sum, 'ev', scatter_dimension=1, tiled=True)]
    ppermute x0 -> x42, starting transfers between devices: none -> 44.6 us  [swap(): return lax.ppermute(x, axis, [(i, i ^ j) for i in range(size)])]
    reshape x9 -> x0, local copies, waits for them, and re-layouts: 44.3 us -> none  [the longest x1 12.8 us: local(): hist_values.reshape(n_users, n_blocks, key_block, n_heads, HEAD)]
    dynamic_slice x12 -> x0, local copies, waits for them, and re-layouts: 43.8 us -> none  [the longest x4 25.9 us: history_step(): lax.dynamic_index_in_dim(keys_split, block_idx, 1, keepdims=False)]
    ppermute x0 -> x42, waiting for transfers between devices: none -> 26.4 us  [swap(): return lax.ppermute(x, axis, [(i, i ^ j) for i in range(size)])]
  transfers between devices with their start and end apart: 5 -> 42, of which waited for: 5 -> 12; matrix products, arithmetic and copies ran while one was open for 14% -> 2% of each run, Pallas kernels for 0% -> 46%
where the time goes in v1:
time: 164 us; the launch traced here: 162 us
  Pallas kernels  82.2 us (50%)
  starting transfers between devices  44.6 us (27%)
  waiting for transfers between devices  26.4 us (16%)
  local copies, waits for them, and re-layouts  4.82 us (3%)
  other arithmetic  3.02 us (2%)
    pallas_call x5, Pallas kernels, attend(): pl.pallas_call(kern, grid_spec=pltpu.PrefetchScalarGridSpec(num_scalar_pr...  56.1 us
    ppermute x42, starting transfers between devices, swap(): return lax.ppermute(x, axis, [(i, i ^ j) for i in range(size)])  44.6 us
    ppermute x42, waiting for transfers between devices, swap(): return lax.ppermute(x, axis, [(i, i ^ j) for i in range(size)])  26.4 us
    pallas_call x4, Pallas kernels, project(): pl.pallas_call(kern, grid_spec=pltpu.PrefetchScalarGridSpec(num_scalar_pr...  10.4 us
    pallas_call x4, Pallas kernels, gate_events(): pl.pallas_call(kern, grid=(1,), in_specs=[whole] * n + [pl.BlockSpec((1,...  8.08 us
    pallas_call x1, Pallas kernels, cand_sums(): pl.pallas_call(kern, grid_spec=pltpu.PrefetchScalarGridSpec(num_scalar_pr...  4.42 us
    unnamed x108, local copies, waits for them, and re-layouts  3.69 us
  transfers between devices with their start and end apart: 42, of which 12 were waited for; matrix products, arithmetic and copies ran while one was open for 2% of the time, Pallas kernels for 46%

profile of v1, /device:TPU:0, one launch (start us, length us, event | category | flops | bytes accessed | tf_op | source)
XLA Modules:
  0.0 162.2 jit_solution(12635968785372750077)
XLA Ops:
  1.8 3.1 %collective-permute-start.1 = (bf16[256,256]{1,0:T(8,128)(2,1)S(1)}, bf16[256,256]{1,0:T(8,128)(2,1)S(1)}, u32[]{:S(2)}, u32[]{:S(2)}) collective-permute-start(bf16[256,256]{1,0:T(8,128)(2,1)S(1)} %get-tuple-element.56.refs_0_), channel_id=1, source_target_pairs={{0,8},{4,12},{8,0},{12,4},{1,9},{5,13},{9,1},{13,5},{2,10},{6,14},... | collective-permute-start | bytes 393224 | tf_op jit(solution)/shard_map/ppermute | solution.py:31
  5.4 1.7 %collective-permute-start.13 = (bf16[256,256]{1,0:T(8,128)(2,1)S(1)}, bf16[256,256]{1,0:T(8,128)(2,1)S(1)}, u32[]{:S(2)}, u32[]{:S(2)}) collective-permute-start(bf16[256,256]{1,0:T(8,128)(2,1)S(1)} %get-tuple-element.59.refs_0_), channel_id=1, source_target_pairs={{0,8},{4,12},{8,0},{12,4},{1,9},{5,13},{9,1},{13,5},{2,10},{6,14},... | collective-permute-start | bytes 393224 | tf_op jit(solution)/shard_map/ppermute | solution.py:31
  7.1 1.6 %collective-permute-done.1.refs_1_ = bf16[256,256]{1,0:T(8,128)(2,1)S(1)} collective-permute-done((bf16[256,256]{1,0:T(8,128)(2,1)S(1)}, bf16[256,256]{1,0:T(8,128)(2,1)S(1)}, u32[]{:S(2)}, u32[]{:S(2)}) %collective-permute-start.1) | collective-permute-done | bytes 131104 | tf_op jit(solution)/shard_map/ppermute | solution.py:31
  8.8 2.5 %collective-permute-start.19 = (bf16[256,256]{1,0:T(8,128)(2,1)S(1)}, bf16[256,256]{1,0:T(8,128)(2,1)S(1)}, u32[]{:S(2)}, u32[]{:S(2)}) collective-permute-start(bf16[256,256]{1,0:T(8,128)(2,1)S(1)} %get-tuple-element.58.refs_0_), channel_id=1, source_target_pairs={{0,8},{4,12},{8,0},{12,4},{1,9},{5,13},{9,1},{13,5},{2,10},{6,14},... | collective-permute-start | bytes 393224 | tf_op jit(solution)/shard_map/ppermute | solution.py:31
  12.1 2.3 %collective-permute-done.13.refs_2_ = bf16[256,256]{1,0:T(8,128)(2,1)S(1)} collective-permute-done((bf16[256,256]{1,0:T(8,128)(2,1)S(1)}, bf16[256,256]{1,0:T(8,128)(2,1)S(1)}, u32[]{:S(2)}, u32[]{:S(2)}) %collective-permute-start.13) | collective-permute-done | bytes 131104 | tf_op jit(solution)/shard_map/ppermute | solution.py:31
  14.4 2.4 %collective-permute-done.19.refs_2_ = bf16[256,256]{1,0:T(8,128)(2,1)S(1)} collective-permute-done((bf16[256,256]{1,0:T(8,128)(2,1)S(1)}, bf16[256,256]{1,0:T(8,128)(2,1)S(1)}, u32[]{:S(2)}, u32[]{:S(2)}) %collective-permute-start.19) | collective-permute-done | bytes 131104 | tf_op jit(solution)/shard_map/ppermute | solution.py:31
  17.5 10.6 %attend0_3.1 = (bf16[256,256]{1,0:T(8,128)(2,1)}, f32[256,256]{1,0:T(8,128)}, bf16[256,256]{1,0:T(8,128)(2,1)}) custom-call(s32[4]{0:T(128)} %len_ref.9, s32[1]{0:T(128)} %bitcast.place_ref, bf16[256,256]{1,0:T(8,128)(2,1)} %copy-done.23, bf16[256,256]{1,0:T(8,128)(2,1)} %copy-done.21, bf16[256,256]{1,0:T(8,128)(2,1)} %copy-done.28, ...), custom_call_target="tpu_custom_call" | custom-call | tf_op jit(solution)/shard_map/attend0_3/pallas_call | solution.py:67
  28.3 6.4 %attend0_1.1.refs_0_ = f32[256,256]{1,0:T(8,128)} custom-call(s32[4]{0:T(128)} %len_ref.9, s32[1]{0:T(128)} %bitcast.place_ref, bf16[256,256]{1,0:T(8,128)(2,1)} %copy-done.7, bf16[4,4096,256]{2,1,0:T(8,128)(2,1)} %refs_4_.19, bf16[4,4096,256]{2,1,0:T(8,128)(2,1)} %refs_5_.9), custom_call_target="tpu_custom_call" | custom-call | tf_op jit(solution)/shard_map/attend0_1/pallas_call | solution.py:67
  34.7 13.1 %attend1_4.1 = (f32[256,256]{1,0:T(8,128)}, bf16[256,256]{1,0:T(8,128)(2,1)}, f32[256,256]{1,0:T(8,128)}, bf16[256,256]{1,0:T(8,128)(2,1)}) custom-call(s32[4]{0:T(128)} %len_ref.9, s32[1]{0:T(128)} %bitcast.place_ref, bf16[256,256]{1,0:T(8,128)(2,1)} %copy-done.6, bf16[256,256]{1,0:T(8,128)(2,1)} %copy-done.20, bf16[256,256]{1,0:T(8,128)(2,1)} %copy-done.19, ...), custom_call_target="tpu_custom_call" | custom-call | tf_op jit(solution)/shard_map/attend1_4/pallas_call | solution.py:67
  48.6 13.0 %attend2_4.1 = (f32[256,256]{1,0:T(8,128)}, bf16[256,256]{1,0:T(8,128)(2,1)}, f32[256,256]{1,0:T(8,128)}, bf16[256,256]{1,0:T(8,128)(2,1)}) custom-call(s32[4]{0:T(128)} %len_ref.9, s32[1]{0:T(128)} %bitcast.place_ref, bf16[256,256]{1,0:T(8,128)(2,1)} %copy-done.5, bf16[256,256]{1,0:T(8,128)(2,1)} %copy-done.25, bf16[256,256]{1,0:T(8,128)(2,1)} %copy-done.18, ...), custom_call_target="tpu_custom_call" | custom-call | tf_op jit(solution)/shard_map/attend2_4/pallas_call | solution.py:67
  62.3 12.9 %attend3_4.1 = (f32[256,256]{1,0:T(8,128)}, bf16[256,256]{1,0:T(8,128)(2,1)}, f32[256,256]{1,0:T(8,128)}, bf16[256,256]{1,0:T(8,128)(2,1)}) custom-call(s32[4]{0:T(128)} %len_ref.9, s32[1]{0:T(128)} %bitcast.place_ref, bf16[256,256]{1,0:T(8,128)(2,1)} %copy-done.4, bf16[256,256]{1,0:T(8,128)(2,1)} %copy-done.22, bf16[256,256]{1,0:T(8,128)(2,1)} %copy-done.17, ...), custom_call_target="tpu_custom_call" | custom-call | tf_op jit(solution)/shard_map/attend3_4/pallas_call | solution.py:67
  80.5 2.6 %collective-permute-done.5.refs_2_ = bf16[256,256]{1,0:T(8,128)(2,1)S(1)} collective-permute-done((bf16[256,256]{1,0:T(8,128)(2,1)S(1)}, bf16[256,256]{1,0:T(8,128)(2,1)S(1)}, u32[]{:S(2)}, u32[]{:S(2)}) %collective-permute-start.5) | collective-permute-done | bytes 131104 | tf_op jit(solution)/shard_map/ppermute | solution.py:31
  83.8 2.0 %gate0.1.refs_0_ = bf16[256,256]{1,0:T(8,128)(2,1)} custom-call(f32[256,256]{1,0:T(8,128)} %attend0_1.1.refs_0_, bf16[256,256]{1,0:T(8,128)(2,1)} %copy-done.42, bf16[256,256]{1,0:T(8,128)(2,1)} %copy-done.48, f32[1,256]{1,0:T(1,128)} %bitcast.20, bf16[4,256,256]{2,1,0:T(8,128)(2,1)} %refs_4_.20), custom_call_target="tpu_custom_call" | custom-call | tf_op jit(solution)/shard_map/gate0/pallas_call | solution.py:97
  87.3 1.8 %collective-permute-start.36 = (bf16[256,256]{1,0:T(8,128)(2,1)}, bf16[256,256]{1,0:T(8,128)(2,1)S(1)}, u32[]{:S(2)}, u32[]{:S(2)}) collective-permute-start(bf16[256,256]{1,0:T(8,128)(2,1)} %gate0.1.refs_0_), channel_id=1, source_target_pairs={{0,1},{1,0},{2,3},{3,2},{4,5},{5,4},{6,7},{7,6},{8,9},{9,8},{10,11... | collective-permute-start | bytes 393224 | tf_op jit(solution)/shard_map/ppermute | solution.py:31
  89.1 2.0 %gate1.1.refs_0_ = bf16[256,256]{1,0:T(8,128)(2,1)} custom-call(f32[256,256]{1,0:T(8,128)} %get-tuple-element.32.refs_0_, bf16[256,256]{1,0:T(8,128)(2,1)} %copy-done.43, bf16[256,256]{1,0:T(8,128)(2,1)} %copy-done.47, f32[1,256]{1,0:T(1,128)} %bitcast.21, bf16[4,256,256]{2,1,0:T(8,128)(2,1)} %refs_4_.20), custom_call_target="tpu_custom_call" | custom-call | tf_op jit(solution)/shard_map/gate1/pallas_call | solution.py:97
  91.1 2.7 %collective-permute-start.37 = (bf16[256,256]{1,0:T(8,128)(2,1)}, bf16[256,256]{1,0:T(8,128)(2,1)S(1)}, u32[]{:S(2)}, u32[]{:S(2)}) collective-permute-start(bf16[256,256]{1,0:T(8,128)(2,1)} %gate0.1.refs_0_), channel_id=1, source_target_pairs={{0,2},{1,3},{2,0},{3,1},{4,6},{5,7},{6,4},{7,5},{8,10},{9,11},{10,... | collective-permute-start | bytes 393224 | tf_op jit(solution)/shard_map/ppermute | solution.py:31
  94.7 3.5 %collective-permute-start.34 = (bf16[256,256]{1,0:T(8,128)(2,1)}, bf16[256,256]{1,0:T(8,128)(2,1)S(1)}, u32[]{:S(2)}, u32[]{:S(2)}) collective-permute-start(bf16[256,256]{1,0:T(8,128)(2,1)} %gate1.1.refs_0_), channel_id=1, source_target_pairs={{0,2},{1,3},{2,0},{3,1},{4,6},{5,7},{6,4},{7,5},{8,10},{9,11},{10,... | collective-permute-start | bytes 393224 | tf_op jit(solution)/shard_map/ppermute | solution.py:31
  98.6 2.0 %gate2.1.refs_0_ = bf16[256,256]{1,0:T(8,128)(2,1)} custom-call(f32[256,256]{1,0:T(8,128)} %get-tuple-element.36.refs_0_, bf16[256,256]{1,0:T(8,128)(2,1)} %copy-done.45, bf16[256,256]{1,0:T(8,128)(2,1)} %copy-done.46, f32[1,256]{1,0:T(1,128)} %bitcast.22, bf16[4,256,256]{2,1,0:T(8,128)(2,1)} %refs_4_.20), custom_call_target="tpu_custom_call" | custom-call | tf_op jit(solution)/shard_map/gate2/pallas_call | solution.py:97
  100.6 4.1 %collective-permute-done.37.refs_2_ = bf16[256,256]{1,0:T(8,128)(2,1)S(1)} collective-permute-done((bf16[256,256]{1,0:T(8,128)(2,1)}, bf16[256,256]{1,0:T(8,128)(2,1)S(1)}, u32[]{:S(2)}, u32[]{:S(2)}) %collective-permute-start.37) | collective-permute-done | bytes 131104 | tf_op jit(solution)/shard_map/ppermute | solution.py:31
  104.8 7.8 %collective-permute-start.31 = (bf16[256,256]{1,0:T(8,128)(2,1)}, bf16[256,256]{1,0:T(8,128)(2,1)S(1)}, u32[]{:S(2)}, u32[]{:S(2)}) collective-permute-start(bf16[256,256]{1,0:T(8,128)(2,1)} %gate2.1.refs_0_), channel_id=1, source_target_pairs={{0,2},{1,3},{2,0},{3,1},{4,6},{5,7},{6,4},{7,5},{8,10},{9,11},{10,... | collective-permute-start | bytes 393224 | tf_op jit(solution)/shard_map/ppermute | solution.py:31
  112.6 2.3 %collective-permute-start.32 = (bf16[256,256]{1,0:T(8,128)(2,1)}, bf16[256,256]{1,0:T(8,128)(2,1)S(1)}, u32[]{:S(2)}, u32[]{:S(2)}) collective-permute-start(bf16[256,256]{1,0:T(8,128)(2,1)} %gate2.1.refs_0_), channel_id=1, source_target_pairs={{0,3},{1,2},{2,1},{3,0},{4,7},{5,6},{6,5},{7,4},{8,11},{9,10},{10,... | collective-permute-start | bytes 393224 | tf_op jit(solution)/shard_map/ppermute | solution.py:31
  116.2 2.0 %gate3.1.refs_0_ = bf16[256,256]{1,0:T(8,128)(2,1)} custom-call(f32[256,256]{1,0:T(8,128)} %get-tuple-element.40.refs_0_, bf16[256,256]{1,0:T(8,128)(2,1)} %copy-done.41, bf16[256,256]{1,0:T(8,128)(2,1)} %copy-done.44, f32[1,256]{1,0:T(1,128)} %bitcast.23, bf16[4,256,256]{2,1,0:T(8,128)(2,1)} %refs_4_.20), custom_call_target="tpu_custom_call" | custom-call | tf_op jit(solution)/shard_map/gate3/pallas_call | solution.py:97
  118.2 7.2 %collective-permute-start.27 = (bf16[256,256]{1,0:T(8,128)(2,1)}, bf16[256,256]{1,0:T(8,128)(2,1)S(1)}, u32[]{:S(2)}, u32[]{:S(2)}) collective-permute-start(bf16[256,256]{1,0:T(8,128)(2,1)} %gate3.1.refs_0_), channel_id=1, source_target_pairs={{0,1},{1,0},{2,3},{3,2},{4,5},{5,4},{6,7},{7,6},{8,9},{9,8},{10,11... | collective-permute-start | bytes 393224 | tf_op jit(solution)/shard_map/ppermute | solution.py:31
  126.1 1.8 %collective-permute-start.29 = (bf16[256,256]{1,0:T(8,128)(2,1)}, bf16[256,256]{1,0:T(8,128)(2,1)S(1)}, u32[]{:S(2)}, u32[]{:S(2)}) collective-permute-start(bf16[256,256]{1,0:T(8,128)(2,1)} %gate3.1.refs_0_), channel_id=1, source_target_pairs={{0,3},{1,2},{2,1},{3,0},{4,7},{5,6},{6,5},{7,4},{8,11},{9,10},{10,... | collective-permute-start | bytes 393224 | tf_op jit(solution)/shard_map/ppermute | solution.py:31
  127.9 2.6 %project0.1 = (bf16[4,256,256]{2,1,0:T(8,128)(2,1)}, bf16[4,256,256]{2,1,0:T(8,128)(2,1)}) custom-call(s32[1]{0:T(128)} %bitcast.10.col_ref, bf16[256,256]{1,0:T(8,128)(2,1)} %gate0.1.refs_0_, bf16[256,256]{1,0:T(8,128)(2,1)} %copy-done.29, bf16[256,256]{1,0:T(8,128)(2,1)} %copy-done.30, bf16[256,256]{1,0:T(8,128)(2,1)} %copy-done.31, ...), custom_call_target="tpu_custom_call" | custom-call | tf_op jit(solution)/shard_map/project0/pallas_call | solution.py:129
  130.5 2.6 %project1.1 = (bf16[4,256,256]{2,1,0:T(8,128)(2,1)}, bf16[4,256,256]{2,1,0:T(8,128)(2,1)}) custom-call(s32[1]{0:T(128)} %bitcast.10.col_ref, bf16[256,256]{1,0:T(8,128)(2,1)} %gate1.1.refs_0_, bf16[256,256]{1,0:T(8,128)(2,1)} %copy-done.32, bf16[256,256]{1,0:T(8,128)(2,1)} %copy-done.33, ...), custom_call_target="tpu_custom_call", output_to_operand_aliasing={{0}: (7, {}), {1}: (8, {})} | custom-call | tf_op jit(solution)/shard_map/project1/pallas_call | solution.py:129
  133.1 2.6 %project2.1 = (bf16[4,256,256]{2,1,0:T(8,128)(2,1)}, bf16[4,256,256]{2,1,0:T(8,128)(2,1)}) custom-call(s32[1]{0:T(128)} %bitcast.10.col_ref, bf16[256,256]{1,0:T(8,128)(2,1)} %gate2.1.refs_0_, bf16[256,256]{1,0:T(8,128)(2,1)} %copy-done.35, bf16[256,256]{1,0:T(8,128)(2,1)} %copy-done.36, ...), custom_call_target="tpu_custom_call", output_to_operand_aliasing={{0}: (7, {}), {1}: (8, {})} | custom-call | tf_op jit(solution)/shard_map/project2/pallas_call | solution.py:129
  135.7 2.8 %collective-permute-done.28.refs_2_ = bf16[256,256]{1,0:T(8,128)(2,1)S(1)} collective-permute-done((bf16[256,256]{1,0:T(8,128)(2,1)}, bf16[256,256]{1,0:T(8,128)(2,1)S(1)}, u32[]{:S(2)}, u32[]{:S(2)}) %collective-permute-start.28) | collective-permute-done | bytes 131104 | tf_op jit(solution)/shard_map/ppermute | solution.py:31
  139.2 2.6 %project3.1 = (bf16[4,256,256]{2,1,0:T(8,128)(2,1)}, bf16[4,256,256]{2,1,0:T(8,128)(2,1)}) custom-call(s32[1]{0:T(128)} %bitcast.10.col_ref, bf16[256,256]{1,0:T(8,128)(2,1)} %gate3.1.refs_0_, bf16[256,256]{1,0:T(8,128)(2,1)} %copy-done.38, bf16[256,256]{1,0:T(8,128)(2,1)} %copy-done.39, ...), custom_call_target="tpu_custom_call", output_to_operand_aliasing={{0}: (7, {}), {1}: (8, {})} | custom-call | tf_op jit(solution)/shard_map/project3/pallas_call | solution.py:129
  142.6 4.4 %cand_sums.1 = (f32[512,256]{1,0:T(8,128)}, bf16[512,256]{1,0:T(8,128)(2,1)}, f32[512,256]{1,0:T(8,128)}, bf16[512,256]{1,0:T(8,128)(2,1)}) custom-call(s32[4]{0:T(128)} %count_ref.3, s32[1]{0:T(128)} %bitcast.place_ref, bf16[512,256]{1,0:T(8,128)(2,1)} %refs_0_.1, bf16[512,256]{1,0:T(8,128)(2,1)} %copy-done.15, bf16[512,256]{1,0:T(8,128)(2,1)} %copy-done.14, ...), custom_call_target="tpu_custom_call" | custom-call | tf_op jit(solution)/shard_map/cand_sums/pallas_call | solution.py:177
  151.6 6.7 %collective-permute-done.41.refs_2_ = bf16[512,256]{1,0:T(8,128)(2,1)S(1)} collective-permute-done((bf16[512,256]{1,0:T(8,128)(2,1)S(1)}, bf16[512,256]{1,0:T(8,128)(2,1)S(1)}, u32[]{:S(2)}, u32[]{:S(2)}) %collective-permute-start.41) | collective-permute-done | bytes 262176 | tf_op jit(solution)/shard_map/ppermute | solution.py:31
  159.0 3.2 %gate_cands.1 = bf16[512,256]{1,0:T(8,128)(2,1)} custom-call(s32[4]{0:T(128)} %count_ref.3, s32[1]{0:T(128)} %bitcast.place_ref, f32[512,256]{1,0:T(8,128)} %get-tuple-element.52.refs_0_, bf16[512,256]{1,0:T(8,128)(2,1)} %copy-done.11, bf16[512,256]{1,0:T(8,128)(2,1)} %copy-done.12, f32[1,256]{1,0:T(1,128)} %bitcast.24, bf16[512,256]{1,0:T(8,128)(2,1)} %refs_4_.25), custom_call_target="tpu_custom_call" | custom-call | tf_op jit(solution)/shard_map/gate_cands/pallas_call | solution.py:212
  (182 shorter events, 22.0 us)
Async XLA Ops:
  5.4 9.0 %collective-permute-start.13 = (bf16[256,256]{1,0:T(8,128)(2,1)S(1)}, bf16[256,256]{1,0:T(8,128)(2,1)S(1)}, u32[]{:S(2)}, u32[]{:S(2)}) collective-permute-start(bf16[256,256]{1,0:T(8,128)(2,1)S(1)} %get-tuple-element.59.refs_0_), channel_id=1, source_target_pairs={{0,8},{4,12},{8,0},{12,4},{1,9},{5,13},{9,1},{13,5},{2,10},{6,14},... | collective-permute-start | bytes 393224 | tf_op jit(solution)/shard_map/ppermute | solution.py:31
  8.8 8.0 %collective-permute-start.19 = (bf16[256,256]{1,0:T(8,128)(2,1)S(1)}, bf16[256,256]{1,0:T(8,128)(2,1)S(1)}, u32[]{:S(2)}, u32[]{:S(2)}) collective-permute-start(bf16[256,256]{1,0:T(8,128)(2,1)S(1)} %get-tuple-element.58.refs_0_), channel_id=1, source_target_pairs={{0,8},{4,12},{8,0},{12,4},{1,9},{5,13},{9,1},{13,5},{2,10},{6,14},... | collective-permute-start | bytes 393224 | tf_op jit(solution)/shard_map/ppermute | solution.py:31
  11.6 16.6 %collective-permute-start.8 = (bf16[256,256]{1,0:T(8,128)(2,1)S(1)}, bf16[256,256]{1,0:T(8,128)(2,1)S(1)}, u32[]{:S(2)}, u32[]{:S(2)}) collective-permute-start(bf16[256,256]{1,0:T(8,128)(2,1)S(1)} %collective-permute-done.7.refs_2_), channel_id=1, source_target_pairs={{0,4},{4,0},{8,12},{12,8},{1,5},{5,1},{9,13},{13,9},{2,6},{6,2},{1... | collective-permute-start | bytes 393224 | tf_op jit(solution)/shard_map/ppermute | solution.py:31
  11.8 36.0 %collective-permute-start.12 = (bf16[256,256]{1,0:T(8,128)(2,1)S(1)}, bf16[256,256]{1,0:T(8,128)(2,1)S(1)}, u32[]{:S(2)}, u32[]{:S(2)}) collective-permute-start(bf16[256,256]{1,0:T(8,128)(2,1)S(1)} %get-tuple-element.59.refs_0_), channel_id=1, source_target_pairs={{0,4},{4,0},{8,12},{12,8},{1,5},{5,1},{9,13},{13,9},{2,6},{6,2},{1... | collective-permute-start | bytes 393224 | tf_op jit(solution)/shard_map/ppermute | solution.py:31
  14.4 33.5 %collective-permute-start.14 = (bf16[256,256]{1,0:T(8,128)(2,1)S(1)}, bf16[256,256]{1,0:T(8,128)(2,1)S(1)}, u32[]{:S(2)}, u32[]{:S(2)}) collective-permute-start(bf16[256,256]{1,0:T(8,128)(2,1)S(1)} %collective-permute-done.13.refs_2_), channel_id=1, source_target_pairs={{0,4},{4,0},{8,12},{12,8},{1,5},{5,1},{9,13},{13,9},{2,6},{6,2},{1... | collective-permute-start | bytes 393224 | tf_op jit(solution)/shard_map/ppermute | solution.py:31
  16.8 44.8 %collective-permute-start.18 = (bf16[256,256]{1,0:T(8,128)(2,1)S(1)}, bf16[256,256]{1,0:T(8,128)(2,1)S(1)}, u32[]{:S(2)}, u32[]{:S(2)}) collective-permute-start(bf16[256,256]{1,0:T(8,128)(2,1)S(1)} %get-tuple-element.58.refs_0_), channel_id=1, source_target_pairs={{0,4},{4,0},{8,12},{12,8},{1,5},{5,1},{9,13},{13,9},{2,6},{6,2},{1... | collective-permute-start | bytes 393224 | tf_op jit(solution)/shard_map/ppermute | solution.py:31
  16.8 44.9 %collective-permute-start.20 = (bf16[256,256]{1,0:T(8,128)(2,1)S(1)}, bf16[256,256]{1,0:T(8,128)(2,1)S(1)}, u32[]{:S(2)}, u32[]{:S(2)}) collective-permute-start(bf16[256,256]{1,0:T(8,128)(2,1)S(1)} %collective-permute-done.19.refs_2_), channel_id=1, source_target_pairs={{0,4},{4,0},{8,12},{12,8},{1,5},{5,1},{9,13},{13,9},{2,6},{6,2},{1... | collective-permute-start | bytes 393224 | tf_op jit(solution)/shard_map/ppermute | solution.py:31
  28.2 47.1 %collective-permute-start.4 = (bf16[256,256]{1,0:T(8,128)(2,1)}, bf16[256,256]{1,0:T(8,128)(2,1)S(1)}, u32[]{:S(2)}, u32[]{:S(2)}) collective-permute-start(bf16[256,256]{1,0:T(8,128)(2,1)} %get-tuple-element.31), channel_id=1, source_target_pairs={{0,4},{4,0},{8,12},{12,8},{1,5},{5,1},{9,13},{13,9},{2,6},{6,2},{1... | collective-permute-start | bytes 393224 | tf_op jit(solution)/shard_map/ppermute | solution.py:31
  47.8 32.1 %collective-permute-start.25 = (bf16[512,256]{1,0:T(8,128)(2,1)S(1)}, bf16[512,256]{1,0:T(8,128)(2,1)S(1)}, u32[]{:S(2)}, u32[]{:S(2)}) collective-permute-start(bf16[512,256]{1,0:T(8,128)(2,1)S(1)} %copy-done.13), channel_id=1, source_target_pairs={{0,8},{4,12},{8,0},{12,4},{1,9},{5,13},{9,1},{13,5},{2,10},{6,14},... | collective-permute-start | bytes 786440 | tf_op jit(solution)/shard_map/ppermute | solution.py:31
  48.0 32.1 %collective-permute-start.3 = (bf16[256,256]{1,0:T(8,128)(2,1)S(1)}, bf16[256,256]{1,0:T(8,128)(2,1)S(1)}, u32[]{:S(2)}, u32[]{:S(2)}) collective-permute-start(bf16[256,256]{1,0:T(8,128)(2,1)S(1)} %copy-done.51), channel_id=1, source_target_pairs={{0,4},{4,0},{8,12},{12,8},{1,5},{5,1},{9,13},{13,9},{2,6},{6,2},{1... | collective-permute-start | bytes 393224 | tf_op jit(solution)/shard_map/ppermute | solution.py:31
  61.6 14.3 %collective-permute-start.10 = (bf16[256,256]{1,0:T(8,128)(2,1)S(1)}, bf16[256,256]{1,0:T(8,128)(2,1)S(1)}, u32[]{:S(2)}, u32[]{:S(2)}) collective-permute-start(bf16[256,256]{1,0:T(8,128)(2,1)S(1)} %copy-done.52), channel_id=1, source_target_pairs={{0,4},{4,0},{8,12},{12,8},{1,5},{5,1},{9,13},{13,9},{2,6},{6,2},{1... | collective-permute-start | bytes 393224 | tf_op jit(solution)/shard_map/ppermute | solution.py:31
  61.7 24.1 %collective-permute-start.9 = (bf16[256,256]{1,0:T(8,128)(2,1)S(1)}, bf16[256,256]{1,0:T(8,128)(2,1)S(1)}, u32[]{:S(2)}, u32[]{:S(2)}) collective-permute-start(bf16[256,256]{1,0:T(8,128)(2,1)S(1)} %copy-done.49), channel_id=1, source_target_pairs={{0,4},{4,0},{8,12},{12,8},{1,5},{5,1},{9,13},{13,9},{2,6},{6,2},{1... | collective-permute-start | bytes 393224 | tf_op jit(solution)/shard_map/ppermute | solution.py:31
  77.5 9.8 %collective-permute-start.11 = (bf16[256,256]{1,0:T(8,128)(2,1)S(1)}, bf16[256,256]{1,0:T(8,128)(2,1)S(1)}, u32[]{:S(2)}, u32[]{:S(2)}) collective-permute-start(bf16[256,256]{1,0:T(8,128)(2,1)S(1)} %add_convert_fusion.3), channel_id=1, source_target_pairs={{0,8},{4,12},{8,0},{12,4},{1,9},{5,13},{9,1},{13,5},{2,10},{6,14},... | collective-permute-start | bytes 393224 | tf_op jit(solution)/shard_map/ppermute | solution.py:31
  80.0 11.2 %collective-permute-start.15 = (bf16[256,256]{1,0:T(8,128)(2,1)S(1)}, bf16[256,256]{1,0:T(8,128)(2,1)S(1)}, u32[]{:S(2)}, u32[]{:S(2)}) collective-permute-start(bf16[256,256]{1,0:T(8,128)(2,1)S(1)} %copy-done.50), channel_id=1, source_target_pairs={{0,4},{4,0},{8,12},{12,8},{1,5},{5,1},{9,13},{13,9},{2,6},{6,2},{1... | collective-permute-start | bytes 393224 | tf_op jit(solution)/shard_map/ppermute | solution.py:31
  80.1 13.7 %collective-permute-start.21 = (bf16[256,256]{1,0:T(8,128)(2,1)}, bf16[256,256]{1,0:T(8,128)(2,1)S(1)}, u32[]{:S(2)}, u32[]{:S(2)}) collective-permute-start(bf16[256,256]{1,0:T(8,128)(2,1)} %get-tuple-element.41), channel_id=1, source_target_pairs={{0,4},{4,0},{8,12},{12,8},{1,5},{5,1},{9,13},{13,9},{2,6},{6,2},{1... | collective-permute-start | bytes 393224 | tf_op jit(solution)/shard_map/ppermute | solution.py:31
  83.2 11.0 %collective-permute-start.17 = (bf16[256,256]{1,0:T(8,128)(2,1)S(1)}, bf16[256,256]{1,0:T(8,128)(2,1)S(1)}, u32[]{:S(2)}, u32[]{:S(2)}) collective-permute-start(bf16[256,256]{1,0:T(8,128)(2,1)S(1)} %add_convert_fusion.2), channel_id=1, source_target_pairs={{0,8},{4,12},{8,0},{12,4},{1,9},{5,13},{9,1},{13,5},{2,10},{6,14},... | collective-permute-start | bytes 393224 | tf_op jit(solution)/shard_map/ppermute | solution.py:31
  85.8 8.9 %collective-permute-start.23 = (bf16[256,256]{1,0:T(8,128)(2,1)S(1)}, bf16[256,256]{1,0:T(8,128)(2,1)S(1)}, u32[]{:S(2)}, u32[]{:S(2)}) collective-permute-start(bf16[256,256]{1,0:T(8,128)(2,1)S(1)} %add_convert_fusion.1), channel_id=1, source_target_pairs={{0,8},{4,12},{8,0},{12,4},{1,9},{5,13},{9,1},{13,5},{2,10},{6,14},... | collective-permute-start | bytes 393224 | tf_op jit(solution)/shard_map/ppermute | solution.py:31
  87.3 10.9 %collective-permute-start.36 = (bf16[256,256]{1,0:T(8,128)(2,1)}, bf16[256,256]{1,0:T(8,128)(2,1)S(1)}, u32[]{:S(2)}, u32[]{:S(2)}) collective-permute-start(bf16[256,256]{1,0:T(8,128)(2,1)} %gate0.1.refs_0_), channel_id=1, source_target_pairs={{0,1},{1,0},{2,3},{3,2},{4,5},{5,4},{6,7},{7,6},{8,9},{9,8},{10,11... | collective-permute-start | bytes 393224 | tf_op jit(solution)/shard_map/ppermute | solution.py:31
  91.1 13.6 %collective-permute-start.37 = (bf16[256,256]{1,0:T(8,128)(2,1)}, bf16[256,256]{1,0:T(8,128)(2,1)S(1)}, u32[]{:S(2)}, u32[]{:S(2)}) collective-permute-start(bf16[256,256]{1,0:T(8,128)(2,1)} %gate0.1.refs_0_), channel_id=1, source_target_pairs={{0,2},{1,3},{2,0},{3,1},{4,6},{5,7},{6,4},{7,5},{8,10},{9,11},{10,... | collective-permute-start | bytes 393224 | tf_op jit(solution)/shard_map/ppermute | solution.py:31
  93.8 11.0 %collective-permute-start.38 = (bf16[256,256]{1,0:T(8,128)(2,1)}, bf16[256,256]{1,0:T(8,128)(2,1)S(1)}, u32[]{:S(2)}, u32[]{:S(2)}) collective-permute-start(bf16[256,256]{1,0:T(8,128)(2,1)} %gate0.1.refs_0_), channel_id=1, source_target_pairs={{0,3},{1,2},{2,1},{3,0},{4,7},{5,6},{6,5},{7,4},{8,11},{9,10},{10,... | collective-permute-start | bytes 393224 | tf_op jit(solution)/shard_map/ppermute | solution.py:31
  94.2 18.4 %collective-permute-start.33 = (bf16[256,256]{1,0:T(8,128)(2,1)}, bf16[256,256]{1,0:T(8,128)(2,1)S(1)}, u32[]{:S(2)}, u32[]{:S(2)}) collective-permute-start(bf16[256,256]{1,0:T(8,128)(2,1)} %gate1.1.refs_0_), channel_id=1, source_target_pairs={{0,1},{1,0},{2,3},{3,2},{4,5},{5,4},{6,7},{7,6},{8,9},{9,8},{10,11... | collective-permute-start | bytes 393224 | tf_op jit(solution)/shard_map/ppermute | solution.py:31
  94.7 20.9 %collective-permute-start.34 = (bf16[256,256]{1,0:T(8,128)(2,1)}, bf16[256,256]{1,0:T(8,128)(2,1)S(1)}, u32[]{:S(2)}, u32[]{:S(2)}) collective-permute-start(bf16[256,256]{1,0:T(8,128)(2,1)} %gate1.1.refs_0_), channel_id=1, source_target_pairs={{0,2},{1,3},{2,0},{3,1},{4,6},{5,7},{6,4},{7,5},{8,10},{9,11},{10,... | collective-permute-start | bytes 393224 | tf_op jit(solution)/shard_map/ppermute | solution.py:31
  98.2 17.4 %collective-permute-start.35 = (bf16[256,256]{1,0:T(8,128)(2,1)}, bf16[256,256]{1,0:T(8,128)(2,1)S(1)}, u32[]{:S(2)}, u32[]{:S(2)}) collective-permute-start(bf16[256,256]{1,0:T(8,128)(2,1)} %gate1.1.refs_0_), channel_id=1, source_target_pairs={{0,3},{1,2},{2,1},{3,0},{4,7},{5,6},{6,5},{7,4},{8,11},{9,10},{10,... | collective-permute-start | bytes 393224 | tf_op jit(solution)/shard_map/ppermute | solution.py:31
  104.7 13.5 %collective-permute-start.30 = (bf16[256,256]{1,0:T(8,128)(2,1)}, bf16[256,256]{1,0:T(8,128)(2,1)S(1)}, u32[]{:S(2)}, u32[]{:S(2)}) collective-permute-start(bf16[256,256]{1,0:T(8,128)(2,1)} %gate2.1.refs_0_), channel_id=1, source_target_pairs={{0,1},{1,0},{2,3},{3,2},{4,5},{5,4},{6,7},{7,6},{8,9},{9,8},{10,11... | collective-permute-start | bytes 393224 | tf_op jit(solution)/shard_map/ppermute | solution.py:31
  104.8 20.6 %collective-permute-start.31 = (bf16[256,256]{1,0:T(8,128)(2,1)}, bf16[256,256]{1,0:T(8,128)(2,1)S(1)}, u32[]{:S(2)}, u32[]{:S(2)}) collective-permute-start(bf16[256,256]{1,0:T(8,128)(2,1)} %gate2.1.refs_0_), channel_id=1, source_target_pairs={{0,2},{1,3},{2,0},{3,1},{4,6},{5,7},{6,4},{7,5},{8,10},{9,11},{10,... | collective-permute-start | bytes 393224 | tf_op jit(solution)/shard_map/ppermute | solution.py:31
  112.6 13.5 %collective-permute-start.32 = (bf16[256,256]{1,0:T(8,128)(2,1)}, bf16[256,256]{1,0:T(8,128)(2,1)S(1)}, u32[]{:S(2)}, u32[]{:S(2)}) collective-permute-start(bf16[256,256]{1,0:T(8,128)(2,1)} %gate2.1.refs_0_), channel_id=1, source_target_pairs={{0,3},{1,2},{2,1},{3,0},{4,7},{5,6},{6,5},{7,4},{8,11},{9,10},{10,... | collective-permute-start | bytes 393224 | tf_op jit(solution)/shard_map/ppermute | solution.py:31
  115.7 26.2 %collective-permute-start.24 = (bf16[512,256]{1,0:T(8,128)(2,1)S(1)}, bf16[512,256]{1,0:T(8,128)(2,1)S(1)}, u32[]{:S(2)}, u32[]{:S(2)}) collective-permute-start(bf16[512,256]{1,0:T(8,128)(2,1)S(1)} %copy-done.13), channel_id=1, source_target_pairs={{0,4},{4,0},{8,12},{12,8},{1,5},{5,1},{9,13},{13,9},{2,6},{6,2},{1... | collective-permute-start | bytes 786440 | tf_op jit(solution)/shard_map/ppermute | solution.py:31
  115.7 26.2 %collective-permute-start.26 = (bf16[512,256]{1,0:T(8,128)(2,1)S(1)}, bf16[512,256]{1,0:T(8,128)(2,1)S(1)}, u32[]{:S(2)}, u32[]{:S(2)}) collective-permute-start(bf16[512,256]{1,0:T(8,128)(2,1)S(1)} %collective-permute-done.25.refs_2_), channel_id=1, source_target_pairs={{0,4},{4,0},{8,12},{12,8},{1,5},{5,1},{9,13},{13,9},{2,6},{6,2},{1... | collective-permute-start | bytes 786440 | tf_op jit(solution)/shard_map/ppermute | solution.py:31
  118.2 17.5 %collective-permute-start.27 = (bf16[256,256]{1,0:T(8,128)(2,1)}, bf16[256,256]{1,0:T(8,128)(2,1)S(1)}, u32[]{:S(2)}, u32[]{:S(2)}) collective-permute-start(bf16[256,256]{1,0:T(8,128)(2,1)} %gate3.1.refs_0_), channel_id=1, source_target_pairs={{0,1},{1,0},{2,3},{3,2},{4,5},{5,4},{6,7},{7,6},{8,9},{9,8},{10,11... | collective-permute-start | bytes 393224 | tf_op jit(solution)/shard_map/ppermute | solution.py:31
  125.4 13.1 %collective-permute-start.28 = (bf16[256,256]{1,0:T(8,128)(2,1)}, bf16[256,256]{1,0:T(8,128)(2,1)S(1)}, u32[]{:S(2)}, u32[]{:S(2)}) collective-permute-start(bf16[256,256]{1,0:T(8,128)(2,1)} %gate3.1.refs_0_), channel_id=1, source_target_pairs={{0,2},{1,3},{2,0},{3,1},{4,6},{5,7},{6,4},{7,5},{8,10},{9,11},{10,... | collective-permute-start | bytes 393224 | tf_op jit(solution)/shard_map/ppermute | solution.py:31
  126.1 12.5 %collective-permute-start.29 = (bf16[256,256]{1,0:T(8,128)(2,1)}, bf16[256,256]{1,0:T(8,128)(2,1)S(1)}, u32[]{:S(2)}, u32[]{:S(2)}) collective-permute-start(bf16[256,256]{1,0:T(8,128)(2,1)} %gate3.1.refs_0_), channel_id=1, source_target_pairs={{0,3},{1,2},{2,1},{3,0},{4,7},{5,6},{6,5},{7,4},{8,11},{9,10},{10,... | collective-permute-start | bytes 393224 | tf_op jit(solution)/shard_map/ppermute | solution.py:31
  149.9 8.4 %collective-permute-start.41 = (bf16[512,256]{1,0:T(8,128)(2,1)S(1)}, bf16[512,256]{1,0:T(8,128)(2,1)S(1)}, u32[]{:S(2)}, u32[]{:S(2)}) collective-permute-start(bf16[512,256]{1,0:T(8,128)(2,1)S(1)} %add_convert_fusion), channel_id=1, source_target_pairs={{0,8},{4,12},{8,0},{12,4},{1,9},{5,13},{9,1},{13,5},{2,10},{6,14},... | collective-permute-start | bytes 786440 | tf_op jit(solution)/shard_map/ppermute | solution.py:31
  (64 other events, 864.8 us)

commit v2 on v1

v2 whole, which is shorter than its diff:
```python
import jax
import jax.numpy as jnp
from jax import lax
from jax.experimental import pallas as pl
from jax.experimental.pallas import tpu as pltpu
from jax.sharding import PartitionSpec as P


HEAD = 128
BLOCK = 128
EPSILON = 1e-05
SCALE = HEAD ** (-0.5)
HALF = 0.5 * SCALE
BF16 = jnp.bfloat16
F32 = jnp.float32
ANY = pl.BlockSpec(memory_space=pl.ANY)


def qk(q, k):
    return lax.dot_general(q, k, (((1,), (1,)), ((), ())), preferred_element_type=F32)


def head_norm(values, gain):
    centre = jnp.mean(values, axis=-1, keepdims=True)
    shifted = values - centre
    spread = jnp.mean(shifted * shifted, axis=-1, keepdims=True)
    return shifted * lax.rsqrt(spread + EPSILON) * gain


def swap(x, axis, size, j):
    return lax.ppermute(x, axis, [(i, i ^ j) for i in range(size)])


def full(shape):
    return pl.BlockSpec(shape, lambda *_: (0,) * len(shape))


def attend(first_user, counts, half_rows, start, queries, own_first, hist_len, place, keys, values, after):
    n = len(queries)
    width = queries[0][0].shape[2]
    hist_rows = keys.shape[1]
    users = len(counts)
    take = max(counts)
    total = sum(counts) * half_rows
    group = max(1, 256 // (take * half_rows))
    n_after = len(after)

    def kern(len_ref, place_ref, *refs):
        q_refs, k_ref, v_ref = refs[:n], refs[n], refs[n + 1]
        o_refs = refs[n + 2 + n_after :]
        for g in range(users):
            rows = counts[g] * half_rows
            at = sum(counts[:g]) * half_rows

            def run(g=g, rows=rows, at=at):
                left = len_ref[first_user + g] - place_ref[0] * hist_rows

                @pl.when(left > 0)
                def _():
                    k = k_ref[0]
                    row = lax.broadcasted_iota(jnp.int32, (hist_rows, HEAD), 0)
                    v = jnp.where(row < left, v_ref[0], jnp.zeros((hist_rows, HEAD), BF16))
                    for i in range(0, n, group):
                        some = q_refs[i : i + group]
                        q = [r[0, :rows, :] for r in some]
                        q = q[0] if len(q) == 1 else jnp.concatenate(q, axis=0)
                        s = qk(q, k)
                        w = (s + s * jnp.tanh(s * HALF)).astype(BF16)
                        o = jnp.dot(w, v, preferred_element_type=F32) * HALF
                        for m, o_ref in enumerate(o_refs[i : i + group]):
                            o_ref[at : at + rows, :] = o[m * rows : (m + 1) * rows].astype(o_ref.dtype)

                @pl.when(left <= 0)
                def _():
                    for o_ref in o_refs:
                        o_ref[at : at + rows, :] = jnp.zeros((rows, HEAD), o_ref.dtype)

            if users == 1:
                run()
            else:
                pl.when(pl.program_id(1) == g)(run)

    def q_spec(offset):
        return pl.BlockSpec((1, take * half_rows, HEAD), lambda h, g, *_: (offset + g, start, h))

    hist = pl.BlockSpec((1, hist_rows, HEAD), lambda h, g, *_: (first_user + g, 0, h))
    kinds = [F32 if own_first and i == 0 else BF16 for i in range(n)]
    return pl.pallas_call(
        kern,
        grid_spec=pltpu.PrefetchScalarGridSpec(
            num_scalar_prefetch=2,
            grid=(width // HEAD, users),
            in_specs=[q_spec(off) for _, off in queries] + [hist, hist] + [ANY] * n_after,
            out_specs=[pl.BlockSpec((total, HEAD), lambda h, g, *_: (0, h))] * n,
        ),
        out_shape=[jax.ShapeDtypeStruct((total, width), kind) for kind in kinds],
        cost_estimate=pl.CostEstimate(
            flops=8 * n * total * hist_rows * width,
            transcendentals=n * total * hist_rows * width // HEAD,
            bytes_accessed=4 * users * hist_rows * width,
        ),
    )(hist_len, place, *[q for q, _ in queries], keys, values, *after)


def gate_events(own, own_at, others, tile, tiles, gate_at, gain, gate):
    n = len(others)
    width = own.shape[1]

    def kern(own_ref, *refs):
        p_refs, gain_ref, gate_ref, o_ref = refs[:n], refs[n], refs[n + 1], refs[n + 2]
        for h in range(width // HEAD):
            cols = slice(h * HEAD, (h + 1) * HEAD)
            total = own_ref[:, cols]
            for p in p_refs:
                total = total + p[:, cols].astype(F32)
            o_ref[:, cols] = (
                head_norm(total, gain_ref[:, cols]) * gate_ref[:, cols].astype(F32)
            ).astype(BF16)

    def at(offset):
        return pl.BlockSpec((tile, width), lambda i: (offset + i, 0))

    return pl.pallas_call(
        kern,
        grid=(tiles,),
        in_specs=[at(own_at)] + [at(0)] * n + [full((1, width)), at(gate_at)],
        out_specs=at(0),
        out_shape=jax.ShapeDtypeStruct((tile * tiles, width), BF16),
    )(own, *others, gain, gate)


def user_of(block, count_ref, n_users):
    end = jnp.int32(0)
    user = jnp.int32(0)
    first = jnp.int32(0)
    for u in range(n_users - 1):
        end = end + lax.shift_right_logical(count_ref[u] + (BLOCK - 1), 7)
        past = block >= end
        user = jnp.where(past, u + 1, user)
        first = jnp.where(past, end, first)
    return user, first


def cand_sums(users, n_users, chunks, cands, cand_count, place, column, key_weight, value_weight, earlier):
    n = len(cands)
    n_hd = len(chunks[0])
    part = chunks[0][0].shape[1]
    width = key_weight.shape[1]
    rows = sum(c[0].shape[0] for c in chunks) // len(users)
    blocks = cands[0].shape[0] // BLOCK
    flat = [p for c in chunks for p in c]
    lo, hi = users[0], users[-1]

    def kern(count_ref, place_ref, col_ref, *refs):
        e_refs = refs[: len(flat)]
        wk, wv = refs[len(flat) : len(flat) + 2]
        q_refs = refs[len(flat) + 2 : len(flat) + 2 + n]
        early = refs[len(flat) + 2 + n : -4]
        keep_ref, send_ref, k_ref, v_ref = refs[-4:]
        at = 0
        for c in range(len(chunks)):
            size = chunks[c][0].shape[0]
            k = jnp.zeros((size, width), F32)
            v = jnp.zeros((size, width), F32)
            for j in range(n_hd):
                from_row = pl.ds(pl.multiple_of((col_ref[0] ^ j) * part, part), part)
                e = e_refs[c * n_hd + j][...]
                k += jnp.dot(e, wk[from_row, :], preferred_element_type=F32)
                v += jnp.dot(e, wv[from_row, :], preferred_element_type=F32)
            k_ref[at : at + size, :] = k.astype(BF16)
            v_ref[at : at + size, :] = v.astype(BF16)
            at += size
        for j in range(n):
            o_ref = send_ref if j & 1 else keep_ref
            for i in range(blocks):
                user, _ = user_of((place_ref[0] ^ j) * blocks + i, count_ref, n_users)
                mine = (user >= lo) & (user <= hi)
                rws = slice(i * BLOCK, (i + 1) * BLOCK)

                @pl.when(mine)
                def _(j=j, o_ref=o_ref, user=user, rws=rws):
                    own = pl.ds(pl.multiple_of((user - lo) * rows, rows), rows)
                    for h in range(width // HEAD):
                        cols = slice(h * HEAD, (h + 1) * HEAD)
                        t = qk(q_refs[j][rws, cols], k_ref[own, cols]) * HALF
                        w = (t + t * jnp.tanh(t)).astype(BF16)
                        o = jnp.dot(w, v_ref[own, cols], preferred_element_type=F32)
                        o_ref[j // 2, rws, cols] = o.astype(o_ref.dtype)

                if early:

                    @pl.when(jnp.logical_not(mine))
                    def _(j=j, o_ref=o_ref, rws=rws):
                        o_ref[j // 2, rws, :] = early[j & 1][j // 2, rws, :]

    shape = (max(n // 2, 1), blocks * BLOCK, width)
    return pl.pallas_call(
        kern,
        grid_spec=pltpu.PrefetchScalarGridSpec(
            num_scalar_prefetch=3,
            grid=(1,),
            in_specs=[full(e.shape) for e in flat]
            + [full(key_weight.shape)] * 2
            + [full(c.shape) for c in cands]
            + [full(shape) for _ in earlier],
            out_specs=[full(shape)] * 2,
            scratch_shapes=[pltpu.VMEM((rows * len(users), width), BF16)] * 2,
        ),
        out_shape=[jax.ShapeDtypeStruct(shape, F32), jax.ShapeDtypeStruct(shape, BF16)],
    )(cand_count, place, column, *flat, key_weight, value_weight, *cands, *earlier)


def gate_cands(own, others, cand_count, place, gain, gate):
    n = 1 + len(others)
    n_users = cand_count.shape[0]
    rows, width = gate.shape

    def kern(count_ref, place_ref, *refs):
        p_refs, gain_ref, gate_ref, o_ref = refs[:n], refs[n], refs[n + 1], refs[n + 2]
        i = pl.program_id(0)
        block = place_ref[0] * (rows // BLOCK) + i
        user, first = user_of(block, count_ref, n_users)
        limit = count_ref[user] - (block - first) * BLOCK
        live = lax.broadcasted_iota(jnp.int32, (BLOCK, HEAD), 0) < limit
        for h in range(width // HEAD):
            cols = slice(h * HEAD, (h + 1) * HEAD)
            total = p_refs[0][0, :, cols].astype(F32)
            for p in p_refs[1:]:
                total = total + p[0, :, cols].astype(F32)
            out = head_norm(total, gain_ref[:, cols]) * gate_ref[:, cols].astype(F32)
            o_ref[:, cols] = jnp.where(live, out, 0.0).astype(BF16)

    part = pl.BlockSpec((1, BLOCK, width), lambda i, *_: (0, i, 0))
    block = pl.BlockSpec((BLOCK, width), lambda i, *_: (i, 0))
    return pl.pallas_call(
        kern,
        grid_spec=pltpu.PrefetchScalarGridSpec(
            num_scalar_prefetch=2,
            grid=(rows // BLOCK,),
            in_specs=[part] * n + [full((1, width)), block],
            out_specs=block,
        ),
        out_shape=jax.ShapeDtypeStruct((rows, width), BF16),
        name="gate_cands",
    )(cand_count, place, own, *others, gain, gate)


def gather_pieces(x, axis, size, skip=()):
    pieces = [x] + [None] * (size - 1)
    bit = size // 2
    while bit:
        for j in range(0, size, 2 * bit):
            if pieces[j] is not None and j + bit not in skip:
                pieces[j + bit] = swap(pieces[j], axis, size, bit)
        bit //= 2
    return pieces


def make_local(n_ev, n_hd):
    def local(
        hist_keys,
        hist_values,
        hist_len,
        new_queries,
        event_gate,
        key_weight,
        value_weight,
        event_gain,
        cand_queries,
        cand_gate,
        cand_gain,
        block_user,
        cand_count,
    ):
        n_users, rows, width = new_queries.shape
        half = rows // 2
        place = lax.axis_index("ev").astype(jnp.int32).reshape(1)
        column = lax.axis_index("hd").astype(jnp.int32).reshape(1)
        event_gain = event_gain.reshape(1, width)
        cand_gain = cand_gain.reshape(1, width)
        gates = event_gate.reshape(n_users * rows, width)
        early_q = gather_pieces(new_queries[:1], "ev", n_ev, skip=(1,))
        queries = gather_pieces(new_queries, "ev", n_ev)
        early_q[1] = queries[1]
        cands = gather_pieces(cand_queries, "ev", n_ev)
        hist = (hist_len, place, hist_keys, hist_values)

        own01 = attend(0, (2, 2), half, 0, [(new_queries, 0)], True, *hist, ())[0]

        def reduce(own, own_at, outs, tiles, gate_at):
            others = [swap(o, "ev", n_ev, j + 1) for j, o in enumerate(outs)]
            return gate_events(own, own_at, others, half, tiles, gate_at, event_gain, gates)


        out0 = attend(0, (2,), half, 0, [(q, 0) for q in early_q[1:]], False, *hist, (own01,))
        out1 = attend(1, (2,), half, 0, [(q, 1) for q in queries[1:]], False, *hist, (out0[0],))
        gated0 = reduce(own01, 0, out0, 2, 0)
        out2 = attend(2, (2, 1), half, 0, [(q, 2) for q in queries], True, *hist, (gated0, out1[0]))
        gated1 = reduce(own01, 2, out1, 2, 2)
        out3 = attend(3, (1,), half, 1, [(q, 3) for q in queries], True, *hist, (gated1, out2[0]))
        gated2 = reduce(out2[0], 0, out2[1:], 3, 4)
        gated3 = reduce(out3[0], 0, out3[1:], 1, 7)
        gated = [gated0, gated1, gated2, gated3]
        all_columns = [gather_pieces(g, "hd", n_hd) for g in gated]
        common = (cands, cand_count, place, column, key_weight, value_weight)
        first = cand_sums((0, 1), n_users, all_columns[:2], *common, ())
        keep, send = cand_sums((2, 3), n_users, all_columns[2:], *common, first)
        if n_ev == 1:
            cand_out = gate_cands(keep, [], cand_count, place, cand_gain, cand_gate)
        else:
            came = swap(send, "ev", n_ev, 1)
            bit = 2
            while bit < n_ev:
                total = keep + came.astype(F32)
                keep = total[0::2]
                came = swap(total[1::2].astype(BF16), "ev", n_ev, bit)
                bit *= 2
            cand_out = gate_cands(keep, [came], cand_count, place, cand_gain, cand_gate)
        event_out = jnp.concatenate(gated, axis=0)
        return event_out.reshape(n_users, rows, width), cand_out

    return local


def solution(mesh):
    return jax.shard_map(
        make_local(mesh.shape["ev"], mesh.shape["hd"]),
        mesh=mesh,
        in_specs=(
            P("grp", "ev", "hd"),
            P("grp", "ev", "hd"),
            P("grp"),
            P("grp", "ev", "hd"),
            P("grp", "ev", "hd"),
            P(None, "hd"),
            P(None, "hd"),
            P("hd"),
            P(("grp", "ev"), "hd"),
            P(("grp", "ev"), "hd"),
            P("hd"),
            P(("grp", "ev")),
            P("grp"),
        ),
        out_specs=(P("grp", "ev", "hd"), P(("grp", "ev"), "hd")),
        check_vma=False,
    )
```

time: 164 us -> 173 us (1.055)
  waiting for transfers between devices: 26.4 us -> 46.9 us
  starting transfers between devices: 44.6 us -> 26.7 us
  Pallas kernels: 82.2 us -> 86.8 us
  local copies, waits for them, and re-layouts: 4.82 us -> 7.8 us
    ppermute x42 -> x34, waiting for transfers between devices: 26.4 us -> 46.9 us  [swap(): return lax.ppermute(x, axis, [(i, i ^ j) for i in range(size)])]
    ppermute x42 -> x34, starting transfers between devices: 44.6 us -> 26.7 us  [swap(): return lax.ppermute(x, axis, [(i, i ^ j) for i in range(size)])]
    pallas_call x1 -> x2, Pallas kernels: 4.42 us -> 17.3 us  [cand_sums(): pl.pallas_call(kern, grid_spec=pltpu.PrefetchScalarGridSpec(num_scalar_pr...]
    pallas_call x8 -> x4, Pallas kernels: 18.5 us -> 9.08 us  [gate_events(): pl.pallas_call(kern, grid=(tiles,), in_specs=[at(own_at)] + [at(0)] * n +...]
    unnamed x108 -> x82, local copies, waits for them, and re-layouts: 3.69 us -> 6 us
    convert_element_type x5 -> x0, other arithmetic: 2.15 us -> none  [scatter_sums(): held[j ^ bit].append(swap(total.astype(BF16), axis, size, bit))]
    slice x0 -> x3, local copies, waits for them, and re-layouts: none -> 1.8 us  [the longest x1 0.92 us: local(): early_q = gather_pieces(new_queries[:1], 'ev', n_ev, skip=(1,))]
    concatenate x0 -> x1, other arithmetic: none -> 1.73 us  [local(): event_out = jnp.concatenate(gated, axis=0)]
  transfers between devices with their start and end apart: 42 -> 34, of which waited for: 12 -> 11; matrix products, arithmetic and copies ran while one was open for 2% -> 2% of each run, Pallas kernels for 46% -> 42%
where the time goes in v2:
time: 173 us; the launch traced here: 172 us
  Pallas kernels  86.8 us (50%)
  waiting for transfers between devices  46.9 us (27%)
  starting transfers between devices  26.7 us (15%)
  local copies, waits for them, and re-layouts  7.8 us (5%)
  other arithmetic  3.06 us (2%)
    pallas_call x5, Pallas kernels, attend(): pl.pallas_call(kern, grid_spec=pltpu.PrefetchScalarGridSpec(num_scalar_pr...  56.2 us
    ppermute x34, waiting for transfers between devices, swap(): return lax.ppermute(x, axis, [(i, i ^ j) for i in range(size)])  46.9 us
    ppermute x34, starting transfers between devices, swap(): return lax.ppermute(x, axis, [(i, i ^ j) for i in range(size)])  26.7 us
    pallas_call x2, Pallas kernels, cand_sums(): pl.pallas_call(kern, grid_spec=pltpu.PrefetchScalarGridSpec(num_scalar_pr...  17.3 us
    pallas_call x4, Pallas kernels, gate_events(): pl.pallas_call(kern, grid=(tiles,), in_specs=[at(own_at)] + [at(0)] * n +...  9.08 us
    unnamed x82, local copies, waits for them, and re-layouts  6 us
    pallas_call x1, Pallas kernels, gate_cands(): pl.pallas_call(kern, grid_spec=pltpu.PrefetchScalarGridSpec(num_scalar_pr...  4.26 us
  transfers between devices with their start and end apart: 34, of which 11 were waited for; matrix products, arithmetic and copies ran while one was open for 2% of the time, Pallas kernels for 42%

profile of v2, /device:TPU:0, one launch (start us, length us, event | category | flops | bytes accessed | tf_op | source)
XLA Modules:
  0.0 172.2 jit_solution(3835990934059013731)
XLA Ops:
  1.5 3.1 %collective-permute-start.1 = (bf16[1,256,256]{2,1,0:T(8,128)(2,1)S(1)}, bf16[1,256,256]{2,1,0:T(8,128)(2,1)S(1)}, u32[]{:S(2)}, u32[]{:S(2)}) collective-permute-start(bf16[1,256,256]{2,1,0:T(8,128)(2,1)S(1)} %slice.12), channel_id=1, source_target_pairs={{0,8},{4,12},{8,0},{12,4},{1,9},{5,13},{9,1},{13,5},{2,10},{6,14},... | collective-permute-start | bytes 393224 | tf_op jit(solution)/shard_map/ppermute | solution.py:31
  4.7 4.3 %collective-permute-done.1.refs_1_ = bf16[1,256,256]{2,1,0:T(8,128)(2,1)S(1)} collective-permute-done((bf16[1,256,256]{2,1,0:T(8,128)(2,1)S(1)}, bf16[1,256,256]{2,1,0:T(8,128)(2,1)S(1)}, u32[]{:S(2)}, u32[]{:S(2)}) %collective-permute-start.1) | collective-permute-done | bytes 131104 | tf_op jit(solution)/shard_map/ppermute | solution.py:31
  9.0 8.9 %shard_map.131.refs_5_.own_ref = f32[512,256]{1,0:T(8,128)} custom-call(s32[4]{0:T(128)} %len_ref.9, s32[1]{0:T(128)} %bitcast.place_ref, bf16[4,256,256]{2,1,0:T(8,128)(2,1)} %refs_0_.5, bf16[4,4096,256]{2,1,0:T(8,128)(2,1)} %refs_4_.7, bf16[4,4096,256]{2,1,0:T(8,128)(2,1)} %refs_5_.3), custom_call_target="tpu_custom_call" | custom-call | flops 4294967296 | bytes 8388608 | tf_op jit(solution)/shard_map/pallas_call | solution.py:88
  17.9 1.5 collective-permute-done.6.refs_1_.refs_2_
  20.9 10.3 %shard_map.132 = (bf16[256,256]{1,0:T(8,128)(2,1)}, bf16[256,256]{1,0:T(8,128)(2,1)}, bf16[256,256]{1,0:T(8,128)(2,1)}) custom-call(s32[4]{0:T(128)} %len_ref.9, s32[1]{0:T(128)} %bitcast.place_ref, bf16[4,256,256]{2,1,0:T(8,128)(2,1)} %copy-done.10, bf16[1,256,256]{2,1,0:T(8,128)(2,1)} %copy-done.38, bf16[1,256,256]{2,1,0:T(8,128)(2,1)} %copy-done.40, ...), custom_call_target="tpu_custom_call" | custom-call | flops 6442450944 | bytes 4194304 | tf_op jit(solution)/shard_map/pallas_call | solution.py:88
  31.3 1.8 %collective-permute-start.5 = (bf16[256,256]{1,0:T(8,128)(2,1)}, bf16[256,256]{1,0:T(8,128)(2,1)S(1)}, u32[]{:S(2)}, u32[]{:S(2)}) collective-permute-start(bf16[256,256]{1,0:T(8,128)(2,1)} %get-tuple-element.22), channel_id=1, source_target_pairs={{0,12},{4,8},{8,4},{12,0},{1,13},{5,9},{9,5},{13,1},{2,14},{6,10},... | collective-permute-start | bytes 393224 | tf_op jit(solution)/shard_map/ppermute | solution.py:31
  33.4 4.5 %collective-permute-done.4.refs_1_ = bf16[256,256]{1,0:T(8,128)(2,1)S(1)} collective-permute-done((bf16[256,256]{1,0:T(8,128)(2,1)}, bf16[256,256]{1,0:T(8,128)(2,1)S(1)}, u32[]{:S(2)}, u32[]{:S(2)}) %collective-permute-start.4) | collective-permute-done | bytes 131104 | tf_op jit(solution)/shard_map/ppermute | solution.py:31
  37.9 1.7 %collective-permute-done.5.refs_2_ = bf16[256,256]{1,0:T(8,128)(2,1)S(1)} collective-permute-done((bf16[256,256]{1,0:T(8,128)(2,1)}, bf16[256,256]{1,0:T(8,128)(2,1)S(1)}, u32[]{:S(2)}, u32[]{:S(2)}) %collective-permute-start.5) | collective-permute-done | bytes 131104 | tf_op jit(solution)/shard_map/ppermute | solution.py:31
  40.3 2.1 %shard_map.133.refs_6_.refs_0_ = bf16[256,256]{1,0:T(8,128)(2,1)} custom-call(f32[512,256]{1,0:T(8,128)} %shard_map.131.refs_5_.own_ref, bf16[256,256]{1,0:T(8,128)(2,1)} %copy-done.27, bf16[256,256]{1,0:T(8,128)(2,1)} %copy-done.28, bf16[256,256]{1,0:T(8,128)(2,1)} %copy-done.30, f32[1,256]{1,0:T(1,128)} %bitcast.11, bf16[1024,256]{1,0:T(8,128)(2,1)} %bitcast.6), custom_call_target="tpu_custom_call" | custom-call | tf_op jit(solution)/shard_map/pallas_call | solution.py:123
  43.2 10.3 %shard_map.134 = (bf16[256,256]{1,0:T(8,128)(2,1)}, bf16[256,256]{1,0:T(8,128)(2,1)}, bf16[256,256]{1,0:T(8,128)(2,1)}) custom-call(s32[4]{0:T(128)} %len_ref.9, s32[1]{0:T(128)} %bitcast.place_ref, bf16[4,256,256]{2,1,0:T(8,128)(2,1)} %copy-done.10, bf16[4,256,256]{2,1,0:T(8,128)(2,1)} %copy-done.9, bf16[4,256,256]{2,1,0:T(8,128)(2,1)} %copy-done.11, ...), custom_call_target="tpu_custom_call" | custom-call | flops 6442450944 | bytes 4194304 | tf_op jit(solution)/shard_map/pallas_call | solution.py:88
  54.5 18.5 %shard_map.136 = (f32[384,256]{1,0:T(8,128)}, bf16[384,256]{1,0:T(8,128)(2,1)}, bf16[384,256]{1,0:T(8,128)(2,1)}, bf16[384,256]{1,0:T(8,128)(2,1)}) custom-call(s32[4]{0:T(128)} %len_ref.9, s32[1]{0:T(128)} %bitcast.place_ref, bf16[4,256,256]{2,1,0:T(8,128)(2,1)} %refs_0_.5, bf16[4,256,256]{2,1,0:T(8,128)(2,1)} %copy-done.10, ...), custom_call_target="tpu_custom_call" | custom-call | flops 12884901888 | bytes 8388608 | tf_op jit(solution)/shard_map/pallas_call | solution.py:88
  73.4 1.5 collective-permute-start.13
  75.3 1.5 collective-permute-start.10
  76.8 11.4 %collective-permute-done.9.refs_1_ = bf16[256,256]{1,0:T(8,128)(2,1)S(1)} collective-permute-done((bf16[256,256]{1,0:T(8,128)(2,1)S(1)}, bf16[256,256]{1,0:T(8,128)(2,1)S(1)}, u32[]{:S(2)}, u32[]{:S(2)}) %collective-permute-start.9) | collective-permute-done | bytes 131104 | tf_op jit(solution)/shard_map/ppermute | solution.py:31
  88.2 1.6 collective-permute-done.10.refs_2_
  90.4 2.1 %shard_map.135.refs_6_.refs_4_ = bf16[256,256]{1,0:T(8,128)(2,1)} custom-call(f32[512,256]{1,0:T(8,128)} %shard_map.131.refs_5_.own_ref, bf16[256,256]{1,0:T(8,128)(2,1)} %copy-done.25, bf16[256,256]{1,0:T(8,128)(2,1)} %copy-done.26, bf16[256,256]{1,0:T(8,128)(2,1)} %copy-done.29, f32[1,256]{1,0:T(1,128)} %bitcast.12, bf16[1024,256]{1,0:T(8,128)(2,1)} %bitcast.7), custom_call_target="tpu_custom_call" | custom-call | tf_op jit(solution)/shard_map/pallas_call | solution.py:123
  92.5 1.9 %collective-permute-start.26 = (bf16[256,256]{1,0:T(8,128)(2,1)}, bf16[256,256]{1,0:T(8,128)(2,1)S(1)}, u32[]{:S(2)}, u32[]{:S(2)}) collective-permute-start(bf16[256,256]{1,0:T(8,128)(2,1)} %shard_map.133.refs_6_.refs_0_), channel_id=1, source_target_pairs={{0,1},{1,0},{2,3},{3,2},{4,5},{5,4},{6,7},{7,6},{8,9},{9,8},{10,11... | collective-permute-start | bytes 393224 | tf_op jit(solution)/shard_map/ppermute | solution.py:31
  94.4 2.6 %collective-permute-start.27 = (bf16[256,256]{1,0:T(8,128)(2,1)}, bf16[256,256]{1,0:T(8,128)(2,1)S(1)}, u32[]{:S(2)}, u32[]{:S(2)}) collective-permute-start(bf16[256,256]{1,0:T(8,128)(2,1)} %shard_map.133.refs_6_.refs_0_), channel_id=1, source_target_pairs={{0,2},{1,3},{2,0},{3,1},{4,6},{5,7},{6,4},{7,5},{8,10},{9,11},{10,... | collective-permute-start | bytes 393224 | tf_op jit(solution)/shard_map/ppermute | solution.py:31
  97.7 3.1 %shard_map.137.refs_0_ = bf16[384,256]{1,0:T(8,128)(2,1)} custom-call(f32[384,256]{1,0:T(8,128)} %get-tuple-element.26.own_ref.refs_7_, bf16[384,256]{1,0:T(8,128)(2,1)} %copy-done.16, bf16[384,256]{1,0:T(8,128)(2,1)} %copy-done.17, bf16[384,256]{1,0:T(8,128)(2,1)} %copy-done.18, f32[1,256]{1,0:T(1,128)} %bitcast.13, bf16[1024,256]{1,0:T(8,128)(2,1)} %bitcast.8), custom_call_target="tpu_custom_call" | custom-call | tf_op jit(solution)/shard_map/pallas_call | solution.py:123
  101.1 8.1 %shard_map.138 = (f32[128,256]{1,0:T(8,128)}, bf16[128,256]{1,0:T(8,128)(2,1)}, bf16[128,256]{1,0:T(8,128)(2,1)}, bf16[128,256]{1,0:T(8,128)(2,1)}) custom-call(s32[4]{0:T(128)} %len_ref.9, s32[1]{0:T(128)} %bitcast.place_ref, bf16[4,256,256]{2,1,0:T(8,128)(2,1)} %refs_0_.5, bf16[4,256,256]{2,1,0:T(8,128)(2,1)} %copy-done.10, ...), custom_call_target="tpu_custom_call" | custom-call | flops 4294967296 | bytes 4194304 | tf_op jit(solution)/shard_map/pallas_call | solution.py:88
  109.4 2.6 %collective-permute-start.30 = (bf16[256,256]{1,0:T(8,128)(2,1)S(1)}, bf16[256,256]{1,0:T(8,128)(2,1)S(1)}, u32[]{:S(2)}, u32[]{:S(2)}) collective-permute-start(bf16[256,256]{1,0:T(8,128)(2,1)S(1)} %copy-done), channel_id=1, source_target_pairs={{0,2},{1,3},{2,0},{3,1},{4,6},{5,7},{6,4},{7,5},{8,10},{9,11},{10,... | collective-permute-start | bytes 393224 | tf_op jit(solution)/shard_map/ppermute | solution.py:31
  113.8 3.7 %collective-permute-done.15.refs_1_ = bf16[128,256]{1,0:T(8,128)(2,1)S(1)} collective-permute-done((bf16[128,256]{1,0:T(8,128)(2,1)}, bf16[128,256]{1,0:T(8,128)(2,1)S(1)}, u32[]{:S(2)}, u32[]{:S(2)}) %collective-permute-start.15) | collective-permute-done | bytes 65568 | tf_op jit(solution)/shard_map/ppermute | solution.py:31
  117.5 1.6 collective-permute-start.29
  119.6 1.6 collective-permute-start.19
  121.6 1.8 %shard_map.139.refs_4_ = bf16[128,256]{1,0:T(8,128)(2,1)} custom-call(f32[128,256]{1,0:T(8,128)} %get-tuple-element.30.own_ref, bf16[128,256]{1,0:T(8,128)(2,1)} %copy-done.34, bf16[128,256]{1,0:T(8,128)(2,1)} %copy-done.35, bf16[128,256]{1,0:T(8,128)(2,1)} %copy-done.36, f32[1,256]{1,0:T(1,128)} %bitcast.14, bf16[1024,256]{1,0:T(8,128)(2,1)} %bitcast.9), custom_call_target="tpu_custom_call" | custom-call | tf_op jit(solution)/shard_map/pallas_call | solution.py:123
  125.5 10.1 %collective-permute-done.21.refs_6_ = bf16[128,256]{1,0:T(8,128)(2,1)S(1)} collective-permute-done((bf16[128,256]{1,0:T(8,128)(2,1)}, bf16[128,256]{1,0:T(8,128)(2,1)S(1)}, u32[]{:S(2)}, u32[]{:S(2)}) %collective-permute-start.21) | collective-permute-done | bytes 65568 | tf_op jit(solution)/shard_map/ppermute | solution.py:31
  137.2 7.0 %shard_map.140 = (f32[2,512,256]{2,1,0:T(8,128)}, bf16[2,512,256]{2,1,0:T(8,128)(2,1)}) custom-call(s32[4]{0:T(128)} %count_ref.5, s32[1]{0:T(128)} %bitcast.place_ref, s32[1]{0:T(128)} %bitcast.4.col_ref, bf16[256,256]{1,0:T(8,128)(2,1)} %shard_map.133.refs_6_.refs_0_, bf16[256,256]{1,0:T(8,128)(2,1)} %copy-done.19, bf16[256,256]{1,0:T(8,128)(2,1)} %copy-done.20, ...), custom_call_target="tpu_custom_call" | custom-call | tf_op jit(solution)/shard_map/pallas_call | solution.py:197
  145.0 10.3 %shard_map.141 = (f32[2,512,256]{2,1,0:T(8,128)}, bf16[2,512,256]{2,1,0:T(8,128)(2,1)}) custom-call(s32[4]{0:T(128)} %count_ref.5, s32[1]{0:T(128)} %bitcast.place_ref, s32[1]{0:T(128)} %bitcast.4.col_ref, bf16[384,256]{1,0:T(8,128)(2,1)} %shard_map.137.refs_0_, bf16[384,256]{1,0:T(8,128)(2,1)} %copy-done.14, bf16[384,256]{1,0:T(8,128)(2,1)} %copy-done.13, ...), custom_call_target="tpu_custom_call" | custom-call | tf_op jit(solution)/shard_map/pallas_call | solution.py:197
  155.4 2.1 %collective-permute-done.32 = bf16[2,512,256]{2,1,0:T(8,128)(2,1)S(1)} collective-permute-done((bf16[2,512,256]{2,1,0:T(8,128)(2,1)}, bf16[2,512,256]{2,1,0:T(8,128)(2,1)S(1)}, u32[]{:S(2)}, u32[]{:S(2)}) %collective-permute-start.32) | collective-permute-done | bytes 524320 | tf_op jit(solution)/shard_map/ppermute | solution.py:31
  159.3 1.7 %pad_maximum_fusion = bf16[1024,256]{1,0:T(8,128)(2,1)} fusion(bf16[128,256]{1,0:T(8,128)(2,1)S(1)} %copy-done.8, bf16[384,256]{1,0:T(8,128)(2,1)S(1)} %copy-done.3, bf16[256,256]{1,0:T(8,128)(2,1)S(1)} %copy-done.1, bf16[256,256]{1,0:T(8,128)(2,1)} %shard_map.133.refs_6_.refs_0_), kind=kLoop, calls=%fused_computation.2 | loop fusion | flops 2097152 | bytes 1048576 | tf_op jit(solution)/shard_map/concatenate | solution.py:319
  161.9 5.4 %collective-permute-done.33.refs_1_ = bf16[1,512,256]{2,1,0:T(8,128)(2,1)S(1)} collective-permute-done((bf16[1,512,256]{2,1,0:T(8,128)(2,1)S(1)}, bf16[1,512,256]{2,1,0:T(8,128)(2,1)S(1)}, u32[]{:S(2)}, u32[]{:S(2)}) %collective-permute-start.33) | collective-permute-done | bytes 262176 | tf_op jit(solution)/shard_map/ppermute | solution.py:31
  168.0 4.3 %gate_cands.1 = bf16[512,256]{1,0:T(8,128)(2,1)} custom-call(s32[4]{0:T(128)} %count_ref.5, s32[1]{0:T(128)} %bitcast.place_ref, f32[1,512,256]{2,1,0:T(8,128)} %slice.15.refs_0_, bf16[1,512,256]{2,1,0:T(8,128)(2,1)} %copy-done.12, f32[1,256]{1,0:T(1,128)} %bitcast.15, bf16[512,256]{1,0:T(8,128)(2,1)} %refs_3_.5), custom_call_target="tpu_custom_call" | custom-call | tf_op jit(solution)/shard_map/gate_cands/pallas_call | solution.py:235
  (135 shorter events, 18.5 us)
Async XLA Ops:
  1.5 7.4 %collective-permute-start.1 = (bf16[1,256,256]{2,1,0:T(8,128)(2,1)S(1)}, bf16[1,256,256]{2,1,0:T(8,128)(2,1)S(1)}, u32[]{:S(2)}, u32[]{:S(2)}) collective-permute-start(bf16[1,256,256]{2,1,0:T(8,128)(2,1)S(1)} %slice.12), channel_id=1, source_target_pairs={{0,8},{4,12},{8,0},{12,4},{1,9},{5,13},{9,1},{13,5},{2,10},{6,14},... | collective-permute-start | bytes 393224 | tf_op jit(solution)/shard_map/ppermute | solution.py:31
  4.6 14.7 %collective-permute-start.6 = (bf16[4,256,256]{2,1,0:T(8,128)(2,1)}, bf16[4,256,256]{2,1,0:T(8,128)(2,1)S(1)}, u32[]{:S(2)}, u32[]{:S(2)}) collective-permute-start(bf16[4,256,256]{2,1,0:T(8,128)(2,1)} %refs_0_.5), channel_id=1, source_target_pairs={{0,8},{4,12},{8,0},{12,4},{1,9},{5,13},{9,1},{13,5},{2,10},{6,14},... | collective-permute-start | bytes 1572872 | tf_op jit(solution)/shard_map/ppermute | solution.py:31
  4.7 14.7 %collective-permute-start = (bf16[4,256,256]{2,1,0:T(8,128)(2,1)}, bf16[4,256,256]{2,1,0:T(8,128)(2,1)S(1)}, u32[]{:S(2)}, u32[]{:S(2)}) collective-permute-start(bf16[4,256,256]{2,1,0:T(8,128)(2,1)} %refs_0_.5), channel_id=1, source_target_pairs={{0,4},{4,0},{8,12},{12,8},{1,5},{5,1},{9,13},{13,9},{2,6},{6,2},{1... | collective-permute-start | bytes 1572872 | tf_op jit(solution)/shard_map/ppermute | solution.py:31
  9.0 10.4 %collective-permute-start.2 = (bf16[1,256,256]{2,1,0:T(8,128)(2,1)S(1)}, bf16[1,256,256]{2,1,0:T(8,128)(2,1)S(1)}, u32[]{:S(2)}, u32[]{:S(2)}) collective-permute-start(bf16[1,256,256]{2,1,0:T(8,128)(2,1)S(1)} %collective-permute-done.1.refs_1_), channel_id=1, source_target_pairs={{0,4},{4,0},{8,12},{12,8},{1,5},{5,1},{9,13},{13,9},{2,6},{6,2},{1... | collective-permute-start | bytes 393224 | tf_op jit(solution)/shard_map/ppermute | solution.py:31
  19.3 23.0 %collective-permute-start.7 = (bf16[4,256,256]{2,1,0:T(8,128)(2,1)S(1)}, bf16[4,256,256]{2,1,0:T(8,128)(2,1)S(1)}, u32[]{:S(2)}, u32[]{:S(2)}) collective-permute-start(bf16[4,256,256]{2,1,0:T(8,128)(2,1)S(1)} %collective-permute-done.6.refs_1_.refs_2_), channel_id=1, source_target_pairs={{0,4},{4,0},{8,12},{12,8},{1,5},{5,1},{9,13},{13,9},{2,6},{6,2},{1... | collective-permute-start | bytes 1572872 | tf_op jit(solution)/shard_map/ppermute | solution.py:31
  31.3 6.6 %collective-permute-start.4 = (bf16[256,256]{1,0:T(8,128)(2,1)}, bf16[256,256]{1,0:T(8,128)(2,1)S(1)}, u32[]{:S(2)}, u32[]{:S(2)}) collective-permute-start(bf16[256,256]{1,0:T(8,128)(2,1)} %get-tuple-element.21), channel_id=1, source_target_pairs={{0,8},{4,12},{8,0},{12,4},{1,9},{5,13},{9,1},{13,5},{2,10},{6,14},... | collective-permute-start | bytes 393224 | tf_op jit(solution)/shard_map/ppermute | solution.py:31
  31.3 8.3 %collective-permute-start.5 = (bf16[256,256]{1,0:T(8,128)(2,1)}, bf16[256,256]{1,0:T(8,128)(2,1)S(1)}, u32[]{:S(2)}, u32[]{:S(2)}) collective-permute-start(bf16[256,256]{1,0:T(8,128)(2,1)} %get-tuple-element.22), channel_id=1, source_target_pairs={{0,12},{4,8},{8,4},{12,0},{1,13},{5,9},{9,5},{13,1},{2,14},{6,10},... | collective-permute-start | bytes 393224 | tf_op jit(solution)/shard_map/ppermute | solution.py:31
  33.1 41.8 %collective-permute-start.24 = (bf16[512,256]{1,0:T(8,128)(2,1)S(1)}, bf16[512,256]{1,0:T(8,128)(2,1)S(1)}, u32[]{:S(2)}, u32[]{:S(2)}) collective-permute-start(bf16[512,256]{1,0:T(8,128)(2,1)S(1)} %copy-done.4), channel_id=1, source_target_pairs={{0,8},{4,12},{8,0},{12,4},{1,9},{5,13},{9,1},{13,5},{2,10},{6,14},... | collective-permute-start | bytes 786440 | tf_op jit(solution)/shard_map/ppermute | solution.py:31
  53.5 21.8 %collective-permute-start.8 = (bf16[256,256]{1,0:T(8,128)(2,1)}, bf16[256,256]{1,0:T(8,128)(2,1)S(1)}, u32[]{:S(2)}, u32[]{:S(2)}) collective-permute-start(bf16[256,256]{1,0:T(8,128)(2,1)} %get-tuple-element.23.refs_7_), channel_id=1, source_target_pairs={{0,4},{4,0},{8,12},{12,8},{1,5},{5,1},{9,13},{13,9},{2,6},{6,2},{1... | collective-permute-start | bytes 393224 | tf_op jit(solution)/shard_map/ppermute | solution.py:31
  73.0 19.5 %collective-permute-start.11 = (bf16[384,256]{1,0:T(8,128)(2,1)}, bf16[384,256]{1,0:T(8,128)(2,1)S(1)}, u32[]{:S(2)}, u32[]{:S(2)}) collective-permute-start(bf16[384,256]{1,0:T(8,128)(2,1)} %get-tuple-element.27), channel_id=1, source_target_pairs={{0,4},{4,0},{8,12},{12,8},{1,5},{5,1},{9,13},{13,9},{2,6},{6,2},{1... | collective-permute-start | bytes 589832 | tf_op jit(solution)/shard_map/ppermute | solution.py:31
  73.2 21.2 %collective-permute-start.12 = (bf16[384,256]{1,0:T(8,128)(2,1)}, bf16[384,256]{1,0:T(8,128)(2,1)S(1)}, u32[]{:S(2)}, u32[]{:S(2)}) collective-permute-start(bf16[384,256]{1,0:T(8,128)(2,1)} %get-tuple-element.28), channel_id=1, source_target_pairs={{0,8},{4,12},{8,0},{12,4},{1,9},{5,13},{9,1},{13,5},{2,10},{6,14},... | collective-permute-start | bytes 589832 | tf_op jit(solution)/shard_map/ppermute | solution.py:31
  73.4 23.6 %collective-permute-start.13 = (bf16[384,256]{1,0:T(8,128)(2,1)}, bf16[384,256]{1,0:T(8,128)(2,1)S(1)}, u32[]{:S(2)}, u32[]{:S(2)}) collective-permute-start(bf16[384,256]{1,0:T(8,128)(2,1)} %get-tuple-element.29), channel_id=1, source_target_pairs={{0,12},{4,8},{8,4},{12,0},{1,13},{5,9},{9,5},{13,1},{2,14},{6,10},... | collective-permute-start | bytes 589832 | tf_op jit(solution)/shard_map/ppermute | solution.py:31
  74.9 13.3 %collective-permute-start.9 = (bf16[256,256]{1,0:T(8,128)(2,1)S(1)}, bf16[256,256]{1,0:T(8,128)(2,1)S(1)}, u32[]{:S(2)}, u32[]{:S(2)}) collective-permute-start(bf16[256,256]{1,0:T(8,128)(2,1)S(1)} %copy-done.39), channel_id=1, source_target_pairs={{0,8},{4,12},{8,0},{12,4},{1,9},{5,13},{9,1},{13,5},{2,10},{6,14},... | collective-permute-start | bytes 393224 | tf_op jit(solution)/shard_map/ppermute | solution.py:31
  75.3 14.5 %collective-permute-start.10 = (bf16[256,256]{1,0:T(8,128)(2,1)S(1)}, bf16[256,256]{1,0:T(8,128)(2,1)S(1)}, u32[]{:S(2)}, u32[]{:S(2)}) collective-permute-start(bf16[256,256]{1,0:T(8,128)(2,1)S(1)} %copy-done.37), channel_id=1, source_target_pairs={{0,12},{4,8},{8,4},{12,0},{1,13},{5,9},{9,5},{13,1},{2,14},{6,10},... | collective-permute-start | bytes 393224 | tf_op jit(solution)/shard_map/ppermute | solution.py:31
  88.2 21.0 %collective-permute-start.23 = (bf16[512,256]{1,0:T(8,128)(2,1)S(1)}, bf16[512,256]{1,0:T(8,128)(2,1)S(1)}, u32[]{:S(2)}, u32[]{:S(2)}) collective-permute-start(bf16[512,256]{1,0:T(8,128)(2,1)S(1)} %copy-done.4), channel_id=1, source_target_pairs={{0,4},{4,0},{8,12},{12,8},{1,5},{5,1},{9,13},{13,9},{2,6},{6,2},{1... | collective-permute-start | bytes 786440 | tf_op jit(solution)/shard_map/ppermute | solution.py:31
  89.8 19.6 %collective-permute-start.25 = (bf16[512,256]{1,0:T(8,128)(2,1)S(1)}, bf16[512,256]{1,0:T(8,128)(2,1)S(1)}, u32[]{:S(2)}, u32[]{:S(2)}) collective-permute-start(bf16[512,256]{1,0:T(8,128)(2,1)S(1)} %collective-permute-done.24.refs_12_), channel_id=1, source_target_pairs={{0,4},{4,0},{8,12},{12,8},{1,5},{5,1},{9,13},{13,9},{2,6},{6,2},{1... | collective-permute-start | bytes 786440 | tf_op jit(solution)/shard_map/ppermute | solution.py:31
  92.5 20.0 %collective-permute-start.26 = (bf16[256,256]{1,0:T(8,128)(2,1)}, bf16[256,256]{1,0:T(8,128)(2,1)S(1)}, u32[]{:S(2)}, u32[]{:S(2)}) collective-permute-start(bf16[256,256]{1,0:T(8,128)(2,1)} %shard_map.133.refs_6_.refs_0_), channel_id=1, source_target_pairs={{0,1},{1,0},{2,3},{3,2},{4,5},{5,4},{6,7},{7,6},{8,9},{9,8},{10,11... | collective-permute-start | bytes 393224 | tf_op jit(solution)/shard_map/ppermute | solution.py:31
  94.4 17.6 %collective-permute-start.27 = (bf16[256,256]{1,0:T(8,128)(2,1)}, bf16[256,256]{1,0:T(8,128)(2,1)S(1)}, u32[]{:S(2)}, u32[]{:S(2)}) collective-permute-start(bf16[256,256]{1,0:T(8,128)(2,1)} %shard_map.133.refs_6_.refs_0_), channel_id=1, source_target_pairs={{0,2},{1,3},{2,0},{3,1},{4,6},{5,7},{6,4},{7,5},{8,10},{9,11},{10,... | collective-permute-start | bytes 393224 | tf_op jit(solution)/shard_map/ppermute | solution.py:31
  100.7 18.9 %collective-permute-start.18 = (bf16[384,256]{1,0:T(8,128)(2,1)}, bf16[384,256]{1,0:T(8,128)(2,1)S(1)}, u32[]{:S(2)}, u32[]{:S(2)}) collective-permute-start(bf16[384,256]{1,0:T(8,128)(2,1)} %shard_map.137.refs_0_), channel_id=1, source_target_pairs={{0,2},{1,3},{2,0},{3,1},{4,6},{5,7},{6,4},{7,5},{8,10},{9,11},{10,... | collective-permute-start | bytes 589832 | tf_op jit(solution)/shard_map/ppermute | solution.py:31
  109.3 3.6 %collective-permute-start.14 = (bf16[128,256]{1,0:T(8,128)(2,1)}, bf16[128,256]{1,0:T(8,128)(2,1)S(1)}, u32[]{:S(2)}, u32[]{:S(2)}) collective-permute-start(bf16[128,256]{1,0:T(8,128)(2,1)} %get-tuple-element.31), channel_id=1, source_target_pairs={{0,4},{4,0},{8,12},{12,8},{1,5},{5,1},{9,13},{13,9},{2,6},{6,2},{1... | collective-permute-start | bytes 196616 | tf_op jit(solution)/shard_map/ppermute | solution.py:31
  109.4 11.8 %collective-permute-start.30 = (bf16[256,256]{1,0:T(8,128)(2,1)S(1)}, bf16[256,256]{1,0:T(8,128)(2,1)S(1)}, u32[]{:S(2)}, u32[]{:S(2)}) collective-permute-start(bf16[256,256]{1,0:T(8,128)(2,1)S(1)} %copy-done), channel_id=1, source_target_pairs={{0,2},{1,3},{2,0},{3,1},{4,6},{5,7},{6,4},{7,5},{8,10},{9,11},{10,... | collective-permute-start | bytes 393224 | tf_op jit(solution)/shard_map/ppermute | solution.py:31
  112.0 11.5 %collective-permute-start.28 = (bf16[256,256]{1,0:T(8,128)(2,1)S(1)}, bf16[256,256]{1,0:T(8,128)(2,1)S(1)}, u32[]{:S(2)}, u32[]{:S(2)}) collective-permute-start(bf16[256,256]{1,0:T(8,128)(2,1)S(1)} %collective-permute-done.27.refs_2_), channel_id=1, source_target_pairs={{0,1},{1,0},{2,3},{3,2},{4,5},{5,4},{6,7},{7,6},{8,9},{9,8},{10,11... | collective-permute-start | bytes 393224 | tf_op jit(solution)/shard_map/ppermute | solution.py:31
  112.5 5.0 %collective-permute-start.15 = (bf16[128,256]{1,0:T(8,128)(2,1)}, bf16[128,256]{1,0:T(8,128)(2,1)S(1)}, u32[]{:S(2)}, u32[]{:S(2)}) collective-permute-start(bf16[128,256]{1,0:T(8,128)(2,1)} %get-tuple-element.32), channel_id=1, source_target_pairs={{0,8},{4,12},{8,0},{12,4},{1,9},{5,13},{9,1},{13,5},{2,10},{6,14},... | collective-permute-start | bytes 196616 | tf_op jit(solution)/shard_map/ppermute | solution.py:31
  112.9 6.2 %collective-permute-start.16 = (bf16[128,256]{1,0:T(8,128)(2,1)}, bf16[128,256]{1,0:T(8,128)(2,1)S(1)}, u32[]{:S(2)}, u32[]{:S(2)}) collective-permute-start(bf16[128,256]{1,0:T(8,128)(2,1)} %get-tuple-element.33), channel_id=1, source_target_pairs={{0,12},{4,8},{8,4},{12,0},{1,13},{5,9},{9,5},{13,1},{2,14},{6,10},... | collective-permute-start | bytes 196616 | tf_op jit(solution)/shard_map/ppermute | solution.py:31
  117.5 6.6 %collective-permute-start.29 = (bf16[256,256]{1,0:T(8,128)(2,1)S(1)}, bf16[256,256]{1,0:T(8,128)(2,1)S(1)}, u32[]{:S(2)}, u32[]{:S(2)}) collective-permute-start(bf16[256,256]{1,0:T(8,128)(2,1)S(1)} %copy-done), channel_id=1, source_target_pairs={{0,1},{1,0},{2,3},{3,2},{4,5},{5,4},{6,7},{7,6},{8,9},{9,8},{10,11... | collective-permute-start | bytes 393224 | tf_op jit(solution)/shard_map/ppermute | solution.py:31
  119.1 25.1 %collective-permute-start.17 = (bf16[384,256]{1,0:T(8,128)(2,1)S(1)}, bf16[384,256]{1,0:T(8,128)(2,1)S(1)}, u32[]{:S(2)}, u32[]{:S(2)}) collective-permute-start(bf16[384,256]{1,0:T(8,128)(2,1)S(1)} %copy-done.2), channel_id=1, source_target_pairs={{0,1},{1,0},{2,3},{3,2},{4,5},{5,4},{6,7},{7,6},{8,9},{9,8},{10,11... | collective-permute-start | bytes 589832 | tf_op jit(solution)/shard_map/ppermute | solution.py:31
  119.6 24.6 %collective-permute-start.19 = (bf16[384,256]{1,0:T(8,128)(2,1)S(1)}, bf16[384,256]{1,0:T(8,128)(2,1)S(1)}, u32[]{:S(2)}, u32[]{:S(2)}) collective-permute-start(bf16[384,256]{1,0:T(8,128)(2,1)S(1)} %collective-permute-done.18.refs_2_), channel_id=1, source_target_pairs={{0,1},{1,0},{2,3},{3,2},{4,5},{5,4},{6,7},{7,6},{8,9},{9,8},{10,11... | collective-permute-start | bytes 589832 | tf_op jit(solution)/shard_map/ppermute | solution.py:31
  121.2 15.4 %collective-permute-start.31 = (bf16[256,256]{1,0:T(8,128)(2,1)S(1)}, bf16[256,256]{1,0:T(8,128)(2,1)S(1)}, u32[]{:S(2)}, u32[]{:S(2)}) collective-permute-start(bf16[256,256]{1,0:T(8,128)(2,1)S(1)} %collective-permute-done.30.refs_6_), channel_id=1, source_target_pairs={{0,1},{1,0},{2,3},{3,2},{4,5},{5,4},{6,7},{7,6},{8,9},{9,8},{10,11... | collective-permute-start | bytes 393224 | tf_op jit(solution)/shard_map/ppermute | solution.py:31
  123.5 12.0 %collective-permute-start.21 = (bf16[128,256]{1,0:T(8,128)(2,1)}, bf16[128,256]{1,0:T(8,128)(2,1)S(1)}, u32[]{:S(2)}, u32[]{:S(2)}) collective-permute-start(bf16[128,256]{1,0:T(8,128)(2,1)} %shard_map.139.refs_4_), channel_id=1, source_target_pairs={{0,2},{1,3},{2,0},{3,1},{4,6},{5,7},{6,4},{7,5},{8,10},{9,11},{10,... | collective-permute-start | bytes 196616 | tf_op jit(solution)/shard_map/ppermute | solution.py:31
  124.2 20.0 %collective-permute-start.20 = (bf16[128,256]{1,0:T(8,128)(2,1)}, bf16[128,256]{1,0:T(8,128)(2,1)S(1)}, u32[]{:S(2)}, u32[]{:S(2)}) collective-permute-start(bf16[128,256]{1,0:T(8,128)(2,1)} %shard_map.139.refs_4_), channel_id=1, source_target_pairs={{0,1},{1,0},{2,3},{3,2},{4,5},{5,4},{6,7},{7,6},{8,9},{9,8},{10,11... | collective-permute-start | bytes 196616 | tf_op jit(solution)/shard_map/ppermute | solution.py:31
  135.6 8.6 %collective-permute-start.22 = (bf16[128,256]{1,0:T(8,128)(2,1)S(1)}, bf16[128,256]{1,0:T(8,128)(2,1)S(1)}, u32[]{:S(2)}, u32[]{:S(2)}) collective-permute-start(bf16[128,256]{1,0:T(8,128)(2,1)S(1)} %collective-permute-done.21.refs_6_), channel_id=1, source_target_pairs={{0,1},{1,0},{2,3},{3,2},{4,5},{5,4},{6,7},{7,6},{8,9},{9,8},{10,11... | collective-permute-start | bytes 196616 | tf_op jit(solution)/shard_map/ppermute | solution.py:31
  158.8 8.4 %collective-permute-start.33 = (bf16[1,512,256]{2,1,0:T(8,128)(2,1)S(1)}, bf16[1,512,256]{2,1,0:T(8,128)(2,1)S(1)}, u32[]{:S(2)}, u32[]{:S(2)}) collective-permute-start(bf16[1,512,256]{2,1,0:T(8,128)(2,1)S(1)} %slice.18), channel_id=1, source_target_pairs={{0,8},{4,12},{8,0},{12,4},{1,9},{5,13},{9,1},{13,5},{2,10},{6,14},... | collective-permute-start | bytes 786440 | tf_op jit(solution)/shard_map/ppermute | solution.py:31
  (43 other events, 514.1 us)

commit v3 on v2

--- a/solution.py
+++ b/solution.py
@@ -42,7 +42,6 @@
     users = len(counts)
     take = max(counts)
     total = sum(counts) * half_rows
-    group = max(1, 256 // (take * half_rows))
     n_after = len(after)
 
     def kern(len_ref, place_ref, *refs):
@@ -57,18 +56,19 @@
 
                 @pl.when(left > 0)
                 def _():
-                    k = k_ref[0]
-                    row = lax.broadcasted_iota(jnp.int32, (hist_rows, HEAD), 0)
-                    v = jnp.where(row < left, v_ref[0], jnp.zeros((hist_rows, HEAD), BF16))
-                    for i in range(0, n, group):
-                        some = q_refs[i : i + group]
-                        q = [r[0, :rows, :] for r in some]
-                        q = q[0] if len(q) == 1 else jnp.concatenate(q, axis=0)
-                        s = qk(q, k)
+                    q = [r[0, :rows, :] for r in q_refs]
+                    q = q[0] if n == 1 else jnp.concatenate(q, axis=0)
+                    tile = min(hist_rows, 1024 if n * rows <= 256 else 256)
+                    o = jnp.zeros((n * rows, HEAD), F32)
+                    for t in range(0, hist_rows, tile):
+                        row = t + lax.broadcasted_iota(jnp.int32, (tile, HEAD), 0)
+                        v = jnp.where(row < left, v_ref[0, t : t + tile], jnp.zeros((tile, HEAD), BF16))
+                        s = qk(q, k_ref[0, t : t + tile])
                         w = (s + s * jnp.tanh(s * HALF)).astype(BF16)
-                        o = jnp.dot(w, v, preferred_element_type=F32) * HALF
-                        for m, o_ref in enumerate(o_refs[i : i + group]):
-                            o_ref[at : at + rows, :] = o[m * rows : (m + 1) * rows].astype(o_ref.dtype)
+                        o = o + jnp.dot(w, v, preferred_element_type=F32)
+                    o = o * HALF
+                    for m, o_ref in enumerate(o_refs):
+                        o_ref[at : at + rows, :] = o[m * rows : (m + 1) * rows].astype(o_ref.dtype)
 
                 @pl.when(left <= 0)
                 def _():
@@ -102,7 +102,7 @@
     )(hist_len, place, *[q for q, _ in queries], keys, values, *after)
 
 
-def gate_events(own, own_at, others, tile, tiles, gate_at, gain, gate):
+def gate_events(own, own_at, others, rows, gate_at, gain, gate):
     n = len(others)
     width = own.shape[1]
 
@@ -118,14 +118,14 @@
             ).astype(BF16)
 
     def at(offset):
-        return pl.BlockSpec((tile, width), lambda i: (offset + i, 0))
-
-    return pl.pallas_call(
-        kern,
-        grid=(tiles,),
-        in_specs=[at(own_at)] + [at(0)] * n + [full((1, width)), at(gate_at)],
-        out_specs=at(0),
-        out_shape=jax.ShapeDtypeStruct((tile * tiles, width), BF16),
+        return pl.BlockSpec((pl.Element(rows), pl.Element(width)), lambda i: (offset, 0))
+
+    return pl.pallas_call(
+        kern,
+        grid=(1,),
+        in_specs=[at(own_at)] + [full((rows, width))] * n + [full((1, width)), at(gate_at)],
+        out_specs=full((rows, width)),
+        out_shape=jax.ShapeDtypeStruct((rows, width), BF16),
     )(own, *others, gain, gate)
 
 
@@ -141,57 +141,73 @@
     return user, first
 
 
-def cand_sums(users, n_users, chunks, cands, cand_count, place, column, key_weight, value_weight, earlier):
+def project(e_refs, n_hd, sizes, col_ref, wk, wv, k_ref, v_ref, at):
+    part = wk.shape[0] // n_hd
+    for c, size in enumerate(sizes):
+        k = jnp.zeros((size, wk.shape[1]), F32)
+        v = jnp.zeros((size, wk.shape[1]), F32)
+        for j in range(n_hd):
+            from_row = pl.ds(pl.multiple_of((col_ref[0] ^ j) * part, part), part)
+            e = e_refs[c * n_hd + j][...]
+            k += jnp.dot(e, wk[from_row, :], preferred_element_type=F32)
+            v += jnp.dot(e, wv[from_row, :], preferred_element_type=F32)
+        k_ref[at : at + size, :] = k.astype(BF16)
+        v_ref[at : at + size, :] = v.astype(BF16)
+        at += size
+
+
+def early_keys(chunks, column, key_weight, value_weight):
+    n_hd = len(chunks[0])
+    flat = [p for c in chunks for p in c]
+    sizes = [c[0].shape[0] for c in chunks]
+    shape = (sum(sizes), key_weight.shape[1])
+
+    def kern(col_ref, *refs):
+        project(refs[: len(flat)], n_hd, sizes, col_ref, *refs[len(flat) :], 0)
+
+    return pl.pallas_call(
+        kern,
+        grid_spec=pltpu.PrefetchScalarGridSpec(
+            num_scalar_prefetch=1,
+            grid=(1,),
+            in_specs=[full(e.shape) for e in flat] + [full(key_weight.shape)] * 2,
+            out_specs=[full(shape)] * 2,
+        ),
+        out_shape=[jax.ShapeDtypeStruct(shape, BF16)] * 2,
+        name="early_keys",
+    )(column, *flat, key_weight, value_weight)
+
+
+def cand_sums(n_users, early, chunks, cands, cand_count, place, column, key_weight, value_weight):
     n = len(cands)
     n_hd = len(chunks[0])
-    part = chunks[0][0].shape[1]
     width = key_weight.shape[1]
-    rows = sum(c[0].shape[0] for c in chunks) // len(users)
+    flat = [p for c in chunks for p in c]
+    sizes = [c[0].shape[0] for c in chunks]
+    done = early[0].shape[0]
+    rows = (done + sum(sizes)) // n_users
     blocks = cands[0].shape[0] // BLOCK
-    flat = [p for c in chunks for p in c]
-    lo, hi = users[0], users[-1]
 
     def kern(count_ref, place_ref, col_ref, *refs):
-        e_refs = refs[: len(flat)]
-        wk, wv = refs[len(flat) : len(flat) + 2]
-        q_refs = refs[len(flat) + 2 : len(flat) + 2 + n]
-        early = refs[len(flat) + 2 + n : -4]
+        e_refs, refs = refs[: len(flat)], refs[len(flat) :]
+        wk, wv, early_k, early_v = refs[:4]
+        q_refs = refs[4 : 4 + n]
         keep_ref, send_ref, k_ref, v_ref = refs[-4:]
-        at = 0
-        for c in range(len(chunks)):
-            size = chunks[c][0].shape[0]
-            k = jnp.zeros((size, width), F32)
-            v = jnp.zeros((size, width), F32)
-            for j in range(n_hd):
-                from_row = pl.ds(pl.multiple_of((col_ref[0] ^ j) * part, part), part)
-                e = e_refs[c * n_hd + j][...]
-                k += jnp.dot(e, wk[from_row, :], preferred_element_type=F32)
-                v += jnp.dot(e, wv[from_row, :], preferred_element_type=F32)
-            k_ref[at : at + size, :] = k.astype(BF16)
-            v_ref[at : at + size, :] = v.astype(BF16)
-            at += size
+        k_ref[:done, :] = early_k[...]
+        v_ref[:done, :] = early_v[...]
+        project(e_refs, n_hd, sizes, col_ref, wk, wv, k_ref, v_ref, done)
         for j in range(n):
             o_ref = send_ref if j & 1 else keep_ref
             for i in range(blocks):
                 user, _ = user_of((place_ref[0] ^ j) * blocks + i, count_ref, n_users)
-                mine = (user >= lo) & (user <= hi)
                 rws = slice(i * BLOCK, (i + 1) * BLOCK)
-
-                @pl.when(mine)
-                def _(j=j, o_ref=o_ref, user=user, rws=rws):
-                    own = pl.ds(pl.multiple_of((user - lo) * rows, rows), rows)
-                    for h in range(width // HEAD):
-                        cols = slice(h * HEAD, (h + 1) * HEAD)
-                        t = qk(q_refs[j][rws, cols], k_ref[own, cols]) * HALF
-                        w = (t + t * jnp.tanh(t)).astype(BF16)
-                        o = jnp.dot(w, v_ref[own, cols], preferred_element_type=F32)
-                        o_ref[j // 2, rws, cols] = o.astype(o_ref.dtype)
-
-                if early:
-
-                    @pl.when(jnp.logical_not(mine))
-                    def _(j=j, o_ref=o_ref, rws=rws):
-                        o_ref[j // 2, rws, :] = early[j & 1][j // 2, rws, :]
+                own = pl.ds(pl.multiple_of(user * rows, rows), rows)
+                for h in range(width // HEAD):
+                    cols = slice(h * HEAD, (h + 1) * HEAD)
+                    t = qk(q_refs[j][rws, cols], k_ref[own, cols]) * HALF
+                    w = (t + t * jnp.tanh(t)).astype(BF16)
+                    o = jnp.dot(w, v_ref[own, cols], preferred_element_type=F32)
+                    o_ref[j // 2, rws, cols] = o.astype(o_ref.dtype)
 
     shape = (max(n // 2, 1), blocks * BLOCK, width)
     return pl.pallas_call(
@@ -201,13 +217,14 @@
             grid=(1,),
             in_specs=[full(e.shape) for e in flat]
             + [full(key_weight.shape)] * 2
-            + [full(c.shape) for c in cands]
-            + [full(shape) for _ in earlier],
+            + [full(early[0].shape)] * 2
+            + [full(c.shape) for c in cands],
             out_specs=[full(shape)] * 2,
-            scratch_shapes=[pltpu.VMEM((rows * len(users), width), BF16)] * 2,
+            scratch_shapes=[pltpu.VMEM((rows * n_users, width), BF16)] * 2,
         ),
         out_shape=[jax.ShapeDtypeStruct(shape, F32), jax.ShapeDtypeStruct(shape, BF16)],
-    )(cand_count, place, column, *flat, key_weight, value_weight, *cands, *earlier)
+        name="cand_sums",
+    )(cand_count, place, column, *flat, key_weight, value_weight, *early, *cands)
 
 
 def gate_cands(own, others, cand_count, place, gain, gate):
@@ -217,26 +234,27 @@
 
     def kern(count_ref, place_ref, *refs):
         p_refs, gain_ref, gate_ref, o_ref = refs[:n], refs[n], refs[n + 1], refs[n + 2]
-        i = pl.program_id(0)
-        block = place_ref[0] * (rows // BLOCK) + i
-        user, first = user_of(block, count_ref, n_users)
-        limit = count_ref[user] - (block - first) * BLOCK
-        live = lax.broadcasted_iota(jnp.int32, (BLOCK, HEAD), 0) < limit
-        for h in range(width // HEAD):
-            cols = slice(h * HEAD, (h + 1) * HEAD)
-            total = p_refs[0][0, :, cols].astype(F32)
-            for p in p_refs[1:]:
-                total = total + p[0, :, cols].astype(F32)
-            out = head_norm(total, gain_ref[:, cols]) * gate_ref[:, cols].astype(F32)
-            o_ref[:, cols] = jnp.where(live, out, 0.0).astype(BF16)
-
-    part = pl.BlockSpec((1, BLOCK, width), lambda i, *_: (0, i, 0))
-    block = pl.BlockSpec((BLOCK, width), lambda i, *_: (i, 0))
+        for i in range(rows // BLOCK):
+            rws = slice(i * BLOCK, (i + 1) * BLOCK)
+            block = place_ref[0] * (rows // BLOCK) + i
+            user, first = user_of(block, count_ref, n_users)
+            limit = count_ref[user] - (block - first) * BLOCK
+            live = lax.broadcasted_iota(jnp.int32, (BLOCK, HEAD), 0) < limit
+            for h in range(width // HEAD):
+                cols = slice(h * HEAD, (h + 1) * HEAD)
+                total = p_refs[0][0, rws, cols].astype(F32)
+                for p in p_refs[1:]:
+                    total = total + p[0, rws, cols].astype(F32)
+                out = head_norm(total, gain_ref[:, cols]) * gate_ref[rws, cols].astype(F32)
+                o_ref[rws, cols] = jnp.where(live, out, 0.0).astype(BF16)
+
+    part = pl.BlockSpec((1, rows, width), lambda i, *_: (0, 0, 0))
+    block = full((rows, width))
     return pl.pallas_call(
         kern,
         grid_spec=pltpu.PrefetchScalarGridSpec(
             num_scalar_prefetch=2,
-            grid=(rows // BLOCK,),
+            grid=(1,),
             in_specs=[part] * n + [full((1, width)), block],
             out_specs=block,
         ),
@@ -287,9 +305,9 @@
 
         own01 = attend(0, (2, 2), half, 0, [(new_queries, 0)], True, *hist, ())[0]
 
-        def reduce(own, own_at, outs, tiles, gate_at):
+        def reduce(own, own_at, outs, halves, gate_at):
             others = [swap(o, "ev", n_ev, j + 1) for j, o in enumerate(outs)]
-            return gate_events(own, own_at, others, half, tiles, gate_at, event_gain, gates)
+            return gate_events(own, own_at * half, others, halves * half, gate_at * half, event_gain, gates)
 
 
         out0 = attend(0, (2,), half, 0, [(q, 0) for q in early_q[1:]], False, *hist, (own01,))
@@ -302,9 +320,10 @@
         gated3 = reduce(out3[0], 0, out3[1:], 1, 7)
         gated = [gated0, gated1, gated2, gated3]
         all_columns = [gather_pieces(g, "hd", n_hd) for g in gated]
-        common = (cands, cand_count, place, column, key_weight, value_weight)
-        first = cand_sums((0, 1), n_users, all_columns[:2], *common, ())
-        keep, send = cand_sums((2, 3), n_users, all_columns[2:], *common, first)
+        early = early_keys(all_columns[:2], column, key_weight, value_weight)
+        keep, send = cand_sums(
+            n_users, early, all_columns[2:], cands, cand_count, place, column, key_weight, value_weight
+        )
         if n_ev == 1:
             cand_out = gate_cands(keep, [], cand_count, place, cand_gain, cand_gate)
         else:

time: 173 us -> 160 us (0.925)
  Pallas kernels: 86.8 us -> 77 us
  waiting for transfers between devices: 46.9 us -> 41.4 us
  starting transfers between devices: 26.7 us -> 29.3 us
    pallas_call x2 -> x1, Pallas kernels: 17.3 us -> 5.68 us  [cand_sums(): pl.pallas_call(kern, grid_spec=pltpu.PrefetchScalarGridSpec(num_scalar_pr...]
    ppermute x34, waiting for transfers between devices: 46.9 us -> 41.4 us  [swap(): return lax.ppermute(x, axis, [(i, i ^ j) for i in range(size)])]
    ppermute x34, starting transfers between devices: 26.7 us -> 29.3 us  [swap(): return lax.ppermute(x, axis, [(i, i ^ j) for i in range(size)])]
    pallas_call x4 -> x5, Pallas kernels: 9.08 us -> 11.4 us  [the longest x4 8.29 us: gate_events(): pl.pallas_call(kern, grid=(1,), in_specs=[at(own_at)] + [full((rows, widt...]
    unnamed x82 -> x80, local copies, waits for them, and re-layouts: 6 us -> 5.69 us
  transfers between devices with their start and end apart: 34 -> 34, of which waited for: 11 -> 12; matrix products, arithmetic and copies ran while one was open for 2% -> 2% of each run, Pallas kernels for 42% -> 36%
where the time goes in v3:
time: 160 us; the launch traced here: 159 us
  Pallas kernels  77 us (48%)
  waiting for transfers between devices  41.4 us (26%)
  starting transfers between devices  29.3 us (18%)
  local copies, waits for them, and re-layouts  7.5 us (5%)
  other arithmetic  3.06 us (2%)
    pallas_call x5, Pallas kernels, attend(): pl.pallas_call(kern, grid_spec=pltpu.PrefetchScalarGridSpec(num_scalar_pr...  56.8 us
    ppermute x34, waiting for transfers between devices, swap(): return lax.ppermute(x, axis, [(i, i ^ j) for i in range(size)])  41.4 us
    ppermute x34, starting transfers between devices, swap(): return lax.ppermute(x, axis, [(i, i ^ j) for i in range(size)])  29.3 us
    pallas_call x4, Pallas kernels, gate_events(): pl.pallas_call(kern, grid=(1,), in_specs=[at(own_at)] + [full((rows, widt...  8.29 us
    unnamed x80, local copies, waits for them, and re-layouts  5.69 us
    pallas_call x1, Pallas kernels, cand_sums(): pl.pallas_call(kern, grid_spec=pltpu.PrefetchScalarGridSpec(num_scalar_pr...  5.68 us
  transfers between devices with their start and end apart: 34, of which 12 were waited for; matrix products, arithmetic and copies ran while one was open for 2% of the time, Pallas kernels for 36%

profile of v3, /device:TPU:0, one launch (start us, length us, event | category | flops | bytes accessed | tf_op | source)
XLA Modules:
  0.0 159.2 jit_solution(17015010702860787156)
XLA Ops:
  1.5 3.1 %collective-permute-start.1 = (bf16[1,256,256]{2,1,0:T(8,128)(2,1)S(1)}, bf16[1,256,256]{2,1,0:T(8,128)(2,1)S(1)}, u32[]{:S(2)}, u32[]{:S(2)}) collective-permute-start(bf16[1,256,256]{2,1,0:T(8,128)(2,1)S(1)} %slice.12), channel_id=1, source_target_pairs={{0,8},{4,12},{8,0},{12,4},{1,9},{5,13},{9,1},{13,5},{2,10},{6,14},... | collective-permute-start | bytes 393224 | tf_op jit(solution)/shard_map/ppermute | solution.py:31
  4.7 4.3 %collective-permute-done.1.refs_1_ = bf16[1,256,256]{2,1,0:T(8,128)(2,1)S(1)} collective-permute-done((bf16[1,256,256]{2,1,0:T(8,128)(2,1)S(1)}, bf16[1,256,256]{2,1,0:T(8,128)(2,1)S(1)}, u32[]{:S(2)}, u32[]{:S(2)}) %collective-permute-start.1) | collective-permute-done | bytes 131104 | tf_op jit(solution)/shard_map/ppermute | solution.py:31
  9.0 9.1 %shard_map.131.refs_5_.own_ref = f32[512,256]{1,0:T(8,128)} custom-call(s32[4]{0:T(128)} %len_ref.9, s32[1]{0:T(128)} %bitcast.place_ref, bf16[4,256,256]{2,1,0:T(8,128)(2,1)} %refs_0_.5, bf16[4,4096,256]{2,1,0:T(8,128)(2,1)} %refs_4_.7, bf16[4,4096,256]{2,1,0:T(8,128)(2,1)} %refs_5_.3), custom_call_target="tpu_custom_call" | custom-call | flops 4294967296 | bytes 8388608 | tf_op jit(solution)/shard_map/pallas_call | solution.py:88
  20.9 10.5 %shard_map.132 = (bf16[256,256]{1,0:T(8,128)(2,1)}, bf16[256,256]{1,0:T(8,128)(2,1)}, bf16[256,256]{1,0:T(8,128)(2,1)}) custom-call(s32[4]{0:T(128)} %len_ref.9, s32[1]{0:T(128)} %bitcast.place_ref, bf16[4,256,256]{2,1,0:T(8,128)(2,1)} %copy-done.6, bf16[1,256,256]{2,1,0:T(8,128)(2,1)} %copy-done.38, bf16[1,256,256]{2,1,0:T(8,128)(2,1)} %copy-done.39, ...), custom_call_target="tpu_custom_call" | custom-call | flops 6442450944 | bytes 4194304 | tf_op jit(solution)/shard_map/pallas_call | solution.py:88
  31.5 1.8 %collective-permute-start.5 = (bf16[256,256]{1,0:T(8,128)(2,1)}, bf16[256,256]{1,0:T(8,128)(2,1)S(1)}, u32[]{:S(2)}, u32[]{:S(2)}) collective-permute-start(bf16[256,256]{1,0:T(8,128)(2,1)} %get-tuple-element.22), channel_id=1, source_target_pairs={{0,12},{4,8},{8,4},{12,0},{1,13},{5,9},{9,5},{13,1},{2,14},{6,10},... | collective-permute-start | bytes 393224 | tf_op jit(solution)/shard_map/ppermute | solution.py:31
  33.3 4.8 %collective-permute-done.4.refs_1_ = bf16[256,256]{1,0:T(8,128)(2,1)S(1)} collective-permute-done((bf16[256,256]{1,0:T(8,128)(2,1)}, bf16[256,256]{1,0:T(8,128)(2,1)S(1)}, u32[]{:S(2)}, u32[]{:S(2)}) %collective-permute-start.4) | collective-permute-done | bytes 131104 | tf_op jit(solution)/shard_map/ppermute | solution.py:31
  38.1 1.7 %collective-permute-done.5.refs_2_ = bf16[256,256]{1,0:T(8,128)(2,1)S(1)} collective-permute-done((bf16[256,256]{1,0:T(8,128)(2,1)}, bf16[256,256]{1,0:T(8,128)(2,1)S(1)}, u32[]{:S(2)}, u32[]{:S(2)}) %collective-permute-start.5) | collective-permute-done | bytes 131104 | tf_op jit(solution)/shard_map/ppermute | solution.py:31
  40.4 2.1 %shard_map.133.refs_6_.refs_0_ = bf16[256,256]{1,0:T(8,128)(2,1)} custom-call(f32[512,256]{1,0:T(8,128)} %shard_map.131.refs_5_.own_ref, bf16[256,256]{1,0:T(8,128)(2,1)} %copy-done.27, bf16[256,256]{1,0:T(8,128)(2,1)} %copy-done.29, bf16[256,256]{1,0:T(8,128)(2,1)} %copy-done.30, f32[1,256]{1,0:T(1,128)} %bitcast.11, bf16[1024,256]{1,0:T(8,128)(2,1)} %bitcast.6), custom_call_target="tpu_custom_call" | custom-call | tf_op jit(solution)/shard_map/pallas_call | solution.py:123
  43.3 10.5 %shard_map.134 = (bf16[256,256]{1,0:T(8,128)(2,1)}, bf16[256,256]{1,0:T(8,128)(2,1)}, bf16[256,256]{1,0:T(8,128)(2,1)}) custom-call(s32[4]{0:T(128)} %len_ref.9, s32[1]{0:T(128)} %bitcast.place_ref, bf16[4,256,256]{2,1,0:T(8,128)(2,1)} %copy-done.6, bf16[4,256,256]{2,1,0:T(8,128)(2,1)} %copy-done.5, bf16[4,256,256]{2,1,0:T(8,128)(2,1)} %copy-done.7, ...), custom_call_target="tpu_custom_call" | custom-call | flops 6442450944 | bytes 4194304 | tf_op jit(solution)/shard_map/pallas_call | solution.py:88
  54.5 18.5 %shard_map.136 = (f32[384,256]{1,0:T(8,128)}, bf16[384,256]{1,0:T(8,128)(2,1)}, bf16[384,256]{1,0:T(8,128)(2,1)}, bf16[384,256]{1,0:T(8,128)(2,1)}) custom-call(s32[4]{0:T(128)} %len_ref.9, s32[1]{0:T(128)} %bitcast.place_ref, bf16[4,256,256]{2,1,0:T(8,128)(2,1)} %refs_0_.5, bf16[4,256,256]{2,1,0:T(8,128)(2,1)} %copy-done.6, bf16[4,256,256]{2,1,0:T(8,128)(2,1)} %copy-done.5, ...), custom_call_target="tpu_custom_call" | custom-call | flops 12884901888 | bytes 8388608 | tf_op jit(solution)/shard_map/pallas_call | solution.py:88
  73.1 1.7 %collective-permute-start.12 = (bf16[384,256]{1,0:T(8,128)(2,1)}, bf16[384,256]{1,0:T(8,128)(2,1)S(1)}, u32[]{:S(2)}, u32[]{:S(2)}) collective-permute-start(bf16[384,256]{1,0:T(8,128)(2,1)} %get-tuple-element.28), channel_id=1, source_target_pairs={{0,8},{4,12},{8,0},{12,4},{1,9},{5,13},{9,1},{13,5},{2,10},{6,14},... | collective-permute-start | bytes 589832 | tf_op jit(solution)/shard_map/ppermute | solution.py:31
  76.4 2.8 %collective-permute-start.24 = (bf16[256,256]{1,0:T(8,128)(2,1)}, bf16[256,256]{1,0:T(8,128)(2,1)S(1)}, u32[]{:S(2)}, u32[]{:S(2)}) collective-permute-start(bf16[256,256]{1,0:T(8,128)(2,1)} %shard_map.133.refs_6_.refs_0_), channel_id=1, source_target_pairs={{0,2},{1,3},{2,0},{3,1},{4,6},{5,7},{6,4},{7,5},{8,10},{9,11},{10,... | collective-permute-start | bytes 393224 | tf_op jit(solution)/shard_map/ppermute | solution.py:31
  79.2 8.3 %collective-permute-done.9.refs_1_ = bf16[256,256]{1,0:T(8,128)(2,1)S(1)} collective-permute-done((bf16[256,256]{1,0:T(8,128)(2,1)S(1)}, bf16[256,256]{1,0:T(8,128)(2,1)S(1)}, u32[]{:S(2)}, u32[]{:S(2)}) %collective-permute-start.9) | collective-permute-done | bytes 131104 | tf_op jit(solution)/shard_map/ppermute | solution.py:31
  89.0 2.0 %shard_map.135.refs_6_.refs_4_ = bf16[256,256]{1,0:T(8,128)(2,1)} custom-call(f32[512,256]{1,0:T(8,128)} %shard_map.131.refs_5_.own_ref, bf16[256,256]{1,0:T(8,128)(2,1)} %copy-done.25, bf16[256,256]{1,0:T(8,128)(2,1)} %copy-done.28, bf16[256,256]{1,0:T(8,128)(2,1)} %copy-done.26, f32[1,256]{1,0:T(1,128)} %bitcast.12, bf16[1024,256]{1,0:T(8,128)(2,1)} %bitcast.7), custom_call_target="tpu_custom_call" | custom-call | tf_op jit(solution)/shard_map/pallas_call | solution.py:123
  91.1 1.9 %collective-permute-start.23 = (bf16[256,256]{1,0:T(8,128)(2,1)}, bf16[256,256]{1,0:T(8,128)(2,1)S(1)}, u32[]{:S(2)}, u32[]{:S(2)}) collective-permute-start(bf16[256,256]{1,0:T(8,128)(2,1)} %shard_map.133.refs_6_.refs_0_), channel_id=1, source_target_pairs={{0,1},{1,0},{2,3},{3,2},{4,5},{5,4},{6,7},{7,6},{8,9},{9,8},{10,11... | collective-permute-start | bytes 393224 | tf_op jit(solution)/shard_map/ppermute | solution.py:31
  93.9 2.4 %shard_map.137.refs_0_ = bf16[384,256]{1,0:T(8,128)(2,1)} custom-call(f32[384,256]{1,0:T(8,128)} %get-tuple-element.26.own_ref.refs_7_, bf16[384,256]{1,0:T(8,128)(2,1)} %copy-done.16, bf16[384,256]{1,0:T(8,128)(2,1)} %copy-done.17, bf16[384,256]{1,0:T(8,128)(2,1)} %copy-done.18, f32[1,256]{1,0:T(1,128)} %bitcast.13, bf16[1024,256]{1,0:T(8,128)(2,1)} %bitcast.8), custom_call_target="tpu_custom_call" | custom-call | tf_op jit(solution)/shard_map/pallas_call | solution.py:123
  96.3 2.8 %collective-permute-start.18 = (bf16[384,256]{1,0:T(8,128)(2,1)}, bf16[384,256]{1,0:T(8,128)(2,1)S(1)}, u32[]{:S(2)}, u32[]{:S(2)}) collective-permute-start(bf16[384,256]{1,0:T(8,128)(2,1)} %shard_map.137.refs_0_), channel_id=1, source_target_pairs={{0,2},{1,3},{2,0},{3,1},{4,6},{5,7},{6,4},{7,5},{8,10},{9,11},{10,... | collective-permute-start | bytes 589832 | tf_op jit(solution)/shard_map/ppermute | solution.py:31
  99.1 8.2 %shard_map.138 = (f32[128,256]{1,0:T(8,128)}, bf16[128,256]{1,0:T(8,128)(2,1)}, bf16[128,256]{1,0:T(8,128)(2,1)}, bf16[128,256]{1,0:T(8,128)(2,1)}) custom-call(s32[4]{0:T(128)} %len_ref.9, s32[1]{0:T(128)} %bitcast.place_ref, bf16[4,256,256]{2,1,0:T(8,128)(2,1)} %refs_0_.5, bf16[4,256,256]{2,1,0:T(8,128)(2,1)} %copy-done.6, bf16[4,256,256]{2,1,0:T(8,128)(2,1)} %copy-done.5, ...), custom_call_target="tpu_custom_call" | custom-call | flops 4294967296 | bytes 4194304 | tf_op jit(solution)/shard_map/pallas_call | solution.py:88
  108.8 1.6 collective-permute-start.26
  110.4 1.7 %collective-permute-done.15.refs_1_ = bf16[128,256]{1,0:T(8,128)(2,1)S(1)} collective-permute-done((bf16[128,256]{1,0:T(8,128)(2,1)}, bf16[128,256]{1,0:T(8,128)(2,1)S(1)}, u32[]{:S(2)}, u32[]{:S(2)}) %collective-permute-start.15) | collective-permute-done | bytes 65568 | tf_op jit(solution)/shard_map/ppermute | solution.py:31
  112.1 5.4 %collective-permute-done.27.refs_6_ = bf16[256,256]{1,0:T(8,128)(2,1)S(1)} collective-permute-done((bf16[256,256]{1,0:T(8,128)(2,1)S(1)}, bf16[256,256]{1,0:T(8,128)(2,1)S(1)}, u32[]{:S(2)}, u32[]{:S(2)}) %collective-permute-start.27) | collective-permute-done | bytes 131104 | tf_op jit(solution)/shard_map/ppermute | solution.py:31
  117.5 2.1 %collective-permute-start.17 = (bf16[384,256]{1,0:T(8,128)(2,1)S(1)}, bf16[384,256]{1,0:T(8,128)(2,1)S(1)}, u32[]{:S(2)}, u32[]{:S(2)}) collective-permute-start(bf16[384,256]{1,0:T(8,128)(2,1)S(1)} %copy-done.2), channel_id=1, source_target_pairs={{0,1},{1,0},{2,3},{3,2},{4,5},{5,4},{6,7},{7,6},{8,9},{9,8},{10,11... | collective-permute-start | bytes 589832 | tf_op jit(solution)/shard_map/ppermute | solution.py:31
  119.7 1.8 %shard_map.139.refs_4_ = bf16[128,256]{1,0:T(8,128)(2,1)} custom-call(f32[128,256]{1,0:T(8,128)} %get-tuple-element.30.own_ref, bf16[128,256]{1,0:T(8,128)(2,1)} %copy-done.34, bf16[128,256]{1,0:T(8,128)(2,1)} %copy-done.35, bf16[128,256]{1,0:T(8,128)(2,1)} %copy-done.36, f32[1,256]{1,0:T(1,128)} %bitcast.14, bf16[1024,256]{1,0:T(8,128)(2,1)} %bitcast.9), custom_call_target="tpu_custom_call" | custom-call | tf_op jit(solution)/shard_map/pallas_call | solution.py:123
  121.5 1.8 %collective-permute-start.21 = (bf16[128,256]{1,0:T(8,128)(2,1)}, bf16[128,256]{1,0:T(8,128)(2,1)S(1)}, u32[]{:S(2)}, u32[]{:S(2)}) collective-permute-start(bf16[128,256]{1,0:T(8,128)(2,1)} %shard_map.139.refs_4_), channel_id=1, source_target_pairs={{0,2},{1,3},{2,0},{3,1},{4,6},{5,7},{6,4},{7,5},{8,10},{9,11},{10,... | collective-permute-start | bytes 196616 | tf_op jit(solution)/shard_map/ppermute | solution.py:31
  123.3 6.6 %collective-permute-done.21.refs_6_ = bf16[128,256]{1,0:T(8,128)(2,1)S(1)} collective-permute-done((bf16[128,256]{1,0:T(8,128)(2,1)}, bf16[128,256]{1,0:T(8,128)(2,1)S(1)}, u32[]{:S(2)}, u32[]{:S(2)}) %collective-permute-start.21) | collective-permute-done | bytes 65568 | tf_op jit(solution)/shard_map/ppermute | solution.py:31
  129.9 2.8 %collective-permute-start.20 = (bf16[128,256]{1,0:T(8,128)(2,1)}, bf16[128,256]{1,0:T(8,128)(2,1)S(1)}, u32[]{:S(2)}, u32[]{:S(2)}) collective-permute-start(bf16[128,256]{1,0:T(8,128)(2,1)} %shard_map.139.refs_4_), channel_id=1, source_target_pairs={{0,1},{1,0},{2,3},{3,2},{4,5},{5,4},{6,7},{7,6},{8,9},{9,8},{10,11... | collective-permute-start | bytes 196616 | tf_op jit(solution)/shard_map/ppermute | solution.py:31
  133.4 3.1 %early_keys.1 = (bf16[512,256]{1,0:T(8,128)(2,1)}, bf16[512,256]{1,0:T(8,128)(2,1)}) custom-call(s32[1]{0:T(128)} %bitcast.4.col_ref, bf16[256,256]{1,0:T(8,128)(2,1)} %shard_map.133.refs_6_.refs_0_, bf16[256,256]{1,0:T(8,128)(2,1)} %copy-done.20, bf16[256,256]{1,0:T(8,128)(2,1)} %copy-done.19, bf16[256,256]{1,0:T(8,128)(2,1)} %copy-done.21, ...), custom_call_target="tpu_custom_call" | custom-call | tf_op jit(solution)/shard_map/early_keys/pallas_call | solution.py:168
  137.8 5.7 %cand_sums.1 = (f32[2,512,256]{2,1,0:T(8,128)}, bf16[2,512,256]{2,1,0:T(8,128)(2,1)}) custom-call(s32[4]{0:T(128)} %count_ref.3, s32[1]{0:T(128)} %bitcast.place_ref, s32[1]{0:T(128)} %bitcast.4.col_ref, bf16[384,256]{1,0:T(8,128)(2,1)} %shard_map.137.refs_0_, bf16[384,256]{1,0:T(8,128)(2,1)} %copy-done.14, bf16[384,256]{1,0:T(8,128)(2,1)} %copy-done.13, ...), custom_call_target="tpu_custom_call" | custom-call | tf_op jit(solution)/shard_map/cand_sums/pallas_call | solution.py:213
  143.5 2.1 %collective-permute-done.32 = bf16[2,512,256]{2,1,0:T(8,128)(2,1)S(1)} collective-permute-done((bf16[2,512,256]{2,1,0:T(8,128)(2,1)}, bf16[2,512,256]{2,1,0:T(8,128)(2,1)S(1)}, u32[]{:S(2)}, u32[]{:S(2)}) %collective-permute-start.32) | collective-permute-done | bytes 524320 | tf_op jit(solution)/shard_map/ppermute | solution.py:31
  148.4 1.7 %pad_maximum_fusion = bf16[1024,256]{1,0:T(8,128)(2,1)} fusion(bf16[128,256]{1,0:T(8,128)(2,1)S(1)} %copy-done.4, bf16[384,256]{1,0:T(8,128)(2,1)S(1)} %copy-done.3, bf16[256,256]{1,0:T(8,128)(2,1)S(1)} %copy-done.1, bf16[256,256]{1,0:T(8,128)(2,1)} %shard_map.133.refs_6_.refs_0_), kind=kLoop, calls=%fused_computation.2 | loop fusion | flops 2097152 | bytes 1048576 | tf_op jit(solution)/shard_map/concatenate | solution.py:338
  151.0 4.4 %collective-permute-done.33.refs_1_ = bf16[1,512,256]{2,1,0:T(8,128)(2,1)S(1)} collective-permute-done((bf16[1,512,256]{2,1,0:T(8,128)(2,1)S(1)}, bf16[1,512,256]{2,1,0:T(8,128)(2,1)S(1)}, u32[]{:S(2)}, u32[]{:S(2)}) %collective-permute-start.33) | collective-permute-done | bytes 262176 | tf_op jit(solution)/shard_map/ppermute | solution.py:31
  156.1 3.1 %gate_cands.1 = bf16[512,256]{1,0:T(8,128)(2,1)} custom-call(s32[4]{0:T(128)} %count_ref.3, s32[1]{0:T(128)} %bitcast.place_ref, f32[1,512,256]{2,1,0:T(8,128)} %slice.15.refs_0_, bf16[1,512,256]{2,1,0:T(8,128)(2,1)} %copy-done.12, f32[1,256]{1,0:T(1,128)} %bitcast.15, bf16[512,256]{1,0:T(8,128)(2,1)} %refs_3_.5), custom_call_target="tpu_custom_call" | custom-call | tf_op jit(solution)/shard_map/gate_cands/pallas_call | solution.py:253
  (133 shorter events, 18.0 us)
Async XLA Ops:
  1.5 7.4 %collective-permute-start.1 = (bf16[1,256,256]{2,1,0:T(8,128)(2,1)S(1)}, bf16[1,256,256]{2,1,0:T(8,128)(2,1)S(1)}, u32[]{:S(2)}, u32[]{:S(2)}) collective-permute-start(bf16[1,256,256]{2,1,0:T(8,128)(2,1)S(1)} %slice.12), channel_id=1, source_target_pairs={{0,8},{4,12},{8,0},{12,4},{1,9},{5,13},{9,1},{13,5},{2,10},{6,14},... | collective-permute-start | bytes 393224 | tf_op jit(solution)/shard_map/ppermute | solution.py:31
  4.6 14.7 %collective-permute-start.6 = (bf16[4,256,256]{2,1,0:T(8,128)(2,1)}, bf16[4,256,256]{2,1,0:T(8,128)(2,1)S(1)}, u32[]{:S(2)}, u32[]{:S(2)}) collective-permute-start(bf16[4,256,256]{2,1,0:T(8,128)(2,1)} %refs_0_.5), channel_id=1, source_target_pairs={{0,8},{4,12},{8,0},{12,4},{1,9},{5,13},{9,1},{13,5},{2,10},{6,14},... | collective-permute-start | bytes 1572872 | tf_op jit(solution)/shard_map/ppermute | solution.py:31
  4.7 14.7 %collective-permute-start = (bf16[4,256,256]{2,1,0:T(8,128)(2,1)}, bf16[4,256,256]{2,1,0:T(8,128)(2,1)S(1)}, u32[]{:S(2)}, u32[]{:S(2)}) collective-permute-start(bf16[4,256,256]{2,1,0:T(8,128)(2,1)} %refs_0_.5), channel_id=1, source_target_pairs={{0,4},{4,0},{8,12},{12,8},{1,5},{5,1},{9,13},{13,9},{2,6},{6,2},{1... | collective-permute-start | bytes 1572872 | tf_op jit(solution)/shard_map/ppermute | solution.py:31
  9.0 10.4 %collective-permute-start.2 = (bf16[1,256,256]{2,1,0:T(8,128)(2,1)S(1)}, bf16[1,256,256]{2,1,0:T(8,128)(2,1)S(1)}, u32[]{:S(2)}, u32[]{:S(2)}) collective-permute-start(bf16[1,256,256]{2,1,0:T(8,128)(2,1)S(1)} %collective-permute-done.1.refs_1_), channel_id=1, source_target_pairs={{0,4},{4,0},{8,12},{12,8},{1,5},{5,1},{9,13},{13,9},{2,6},{6,2},{1... | collective-permute-start | bytes 393224 | tf_op jit(solution)/shard_map/ppermute | solution.py:31
  19.3 23.1 %collective-permute-start.7 = (bf16[4,256,256]{2,1,0:T(8,128)(2,1)S(1)}, bf16[4,256,256]{2,1,0:T(8,128)(2,1)S(1)}, u32[]{:S(2)}, u32[]{:S(2)}) collective-permute-start(bf16[4,256,256]{2,1,0:T(8,128)(2,1)S(1)} %collective-permute-done.6.refs_1_.refs_2_), channel_id=1, source_target_pairs={{0,4},{4,0},{8,12},{12,8},{1,5},{5,1},{9,13},{13,9},{2,6},{6,2},{1... | collective-permute-start | bytes 1572872 | tf_op jit(solution)/shard_map/ppermute | solution.py:31
  31.4 6.6 %collective-permute-start.4 = (bf16[256,256]{1,0:T(8,128)(2,1)}, bf16[256,256]{1,0:T(8,128)(2,1)S(1)}, u32[]{:S(2)}, u32[]{:S(2)}) collective-permute-start(bf16[256,256]{1,0:T(8,128)(2,1)} %get-tuple-element.21), channel_id=1, source_target_pairs={{0,8},{4,12},{8,0},{12,4},{1,9},{5,13},{9,1},{13,5},{2,10},{6,14},... | collective-permute-start | bytes 393224 | tf_op jit(solution)/shard_map/ppermute | solution.py:31
  31.5 8.3 %collective-permute-start.5 = (bf16[256,256]{1,0:T(8,128)(2,1)}, bf16[256,256]{1,0:T(8,128)(2,1)S(1)}, u32[]{:S(2)}, u32[]{:S(2)}) collective-permute-start(bf16[256,256]{1,0:T(8,128)(2,1)} %get-tuple-element.22), channel_id=1, source_target_pairs={{0,12},{4,8},{8,4},{12,0},{1,13},{5,9},{9,5},{13,1},{2,14},{6,10},... | collective-permute-start | bytes 393224 | tf_op jit(solution)/shard_map/ppermute | solution.py:31
  53.8 21.1 %collective-permute-start.8 = (bf16[256,256]{1,0:T(8,128)(2,1)}, bf16[256,256]{1,0:T(8,128)(2,1)S(1)}, u32[]{:S(2)}, u32[]{:S(2)}) collective-permute-start(bf16[256,256]{1,0:T(8,128)(2,1)} %get-tuple-element.23.refs_7_), channel_id=1, source_target_pairs={{0,4},{4,0},{8,12},{12,8},{1,5},{5,1},{9,13},{13,9},{2,6},{6,2},{1... | collective-permute-start | bytes 393224 | tf_op jit(solution)/shard_map/ppermute | solution.py:31
  54.1 22.3 %collective-permute-start.10 = (bf16[256,256]{1,0:T(8,128)(2,1)}, bf16[256,256]{1,0:T(8,128)(2,1)S(1)}, u32[]{:S(2)}, u32[]{:S(2)}) collective-permute-start(bf16[256,256]{1,0:T(8,128)(2,1)} %get-tuple-element.25), channel_id=1, source_target_pairs={{0,12},{4,8},{8,4},{12,0},{1,13},{5,9},{9,5},{13,1},{2,14},{6,10},... | collective-permute-start | bytes 393224 | tf_op jit(solution)/shard_map/ppermute | solution.py:31
  73.0 18.1 %collective-permute-start.11 = (bf16[384,256]{1,0:T(8,128)(2,1)}, bf16[384,256]{1,0:T(8,128)(2,1)S(1)}, u32[]{:S(2)}, u32[]{:S(2)}) collective-permute-start(bf16[384,256]{1,0:T(8,128)(2,1)} %get-tuple-element.27), channel_id=1, source_target_pairs={{0,4},{4,0},{8,12},{12,8},{1,5},{5,1},{9,13},{13,9},{2,6},{6,2},{1... | collective-permute-start | bytes 589832 | tf_op jit(solution)/shard_map/ppermute | solution.py:31
  73.1 19.9 %collective-permute-start.12 = (bf16[384,256]{1,0:T(8,128)(2,1)}, bf16[384,256]{1,0:T(8,128)(2,1)S(1)}, u32[]{:S(2)}, u32[]{:S(2)}) collective-permute-start(bf16[384,256]{1,0:T(8,128)(2,1)} %get-tuple-element.28), channel_id=1, source_target_pairs={{0,8},{4,12},{8,0},{12,4},{1,9},{5,13},{9,1},{13,5},{2,10},{6,14},... | collective-permute-start | bytes 589832 | tf_op jit(solution)/shard_map/ppermute | solution.py:31
  74.8 18.4 %collective-permute-start.13 = (bf16[384,256]{1,0:T(8,128)(2,1)}, bf16[384,256]{1,0:T(8,128)(2,1)S(1)}, u32[]{:S(2)}, u32[]{:S(2)}) collective-permute-start(bf16[384,256]{1,0:T(8,128)(2,1)} %get-tuple-element.29), channel_id=1, source_target_pairs={{0,12},{4,8},{8,4},{12,0},{1,13},{5,9},{9,5},{13,1},{2,14},{6,10},... | collective-permute-start | bytes 589832 | tf_op jit(solution)/shard_map/ppermute | solution.py:31
  74.9 12.7 %collective-permute-start.9 = (bf16[256,256]{1,0:T(8,128)(2,1)S(1)}, bf16[256,256]{1,0:T(8,128)(2,1)S(1)}, u32[]{:S(2)}, u32[]{:S(2)}) collective-permute-start(bf16[256,256]{1,0:T(8,128)(2,1)S(1)} %copy-done.37), channel_id=1, source_target_pairs={{0,8},{4,12},{8,0},{12,4},{1,9},{5,13},{9,1},{13,5},{2,10},{6,14},... | collective-permute-start | bytes 393224 | tf_op jit(solution)/shard_map/ppermute | solution.py:31
  76.4 14.7 %collective-permute-start.24 = (bf16[256,256]{1,0:T(8,128)(2,1)}, bf16[256,256]{1,0:T(8,128)(2,1)S(1)}, u32[]{:S(2)}, u32[]{:S(2)}) collective-permute-start(bf16[256,256]{1,0:T(8,128)(2,1)} %shard_map.133.refs_6_.refs_0_), channel_id=1, source_target_pairs={{0,2},{1,3},{2,0},{3,1},{4,6},{5,7},{6,4},{7,5},{8,10},{9,11},{10,... | collective-permute-start | bytes 393224 | tf_op jit(solution)/shard_map/ppermute | solution.py:31
  87.6 19.7 %collective-permute-start.30 = (bf16[512,256]{1,0:T(8,128)(2,1)S(1)}, bf16[512,256]{1,0:T(8,128)(2,1)S(1)}, u32[]{:S(2)}, u32[]{:S(2)}) collective-permute-start(bf16[512,256]{1,0:T(8,128)(2,1)S(1)} %copy-done.8), channel_id=1, source_target_pairs={{0,8},{4,12},{8,0},{12,4},{1,9},{5,13},{9,1},{13,5},{2,10},{6,14},... | collective-permute-start | bytes 786440 | tf_op jit(solution)/shard_map/ppermute | solution.py:31
  91.1 16.3 %collective-permute-start.29 = (bf16[512,256]{1,0:T(8,128)(2,1)S(1)}, bf16[512,256]{1,0:T(8,128)(2,1)S(1)}, u32[]{:S(2)}, u32[]{:S(2)}) collective-permute-start(bf16[512,256]{1,0:T(8,128)(2,1)S(1)} %copy-done.8), channel_id=1, source_target_pairs={{0,4},{4,0},{8,12},{12,8},{1,5},{5,1},{9,13},{13,9},{2,6},{6,2},{1... | collective-permute-start | bytes 786440 | tf_op jit(solution)/shard_map/ppermute | solution.py:31
  91.1 17.0 %collective-permute-start.23 = (bf16[256,256]{1,0:T(8,128)(2,1)}, bf16[256,256]{1,0:T(8,128)(2,1)S(1)}, u32[]{:S(2)}, u32[]{:S(2)}) collective-permute-start(bf16[256,256]{1,0:T(8,128)(2,1)} %shard_map.133.refs_6_.refs_0_), channel_id=1, source_target_pairs={{0,1},{1,0},{2,3},{3,2},{4,5},{5,4},{6,7},{7,6},{8,9},{9,8},{10,11... | collective-permute-start | bytes 393224 | tf_op jit(solution)/shard_map/ppermute | solution.py:31
  93.0 15.4 %collective-permute-start.25 = (bf16[256,256]{1,0:T(8,128)(2,1)S(1)}, bf16[256,256]{1,0:T(8,128)(2,1)S(1)}, u32[]{:S(2)}, u32[]{:S(2)}) collective-permute-start(bf16[256,256]{1,0:T(8,128)(2,1)S(1)} %collective-permute-done.24.refs_2_), channel_id=1, source_target_pairs={{0,1},{1,0},{2,3},{3,2},{4,5},{5,4},{6,7},{7,6},{8,9},{9,8},{10,11... | collective-permute-start | bytes 393224 | tf_op jit(solution)/shard_map/ppermute | solution.py:31
  96.3 23.3 %collective-permute-start.18 = (bf16[384,256]{1,0:T(8,128)(2,1)}, bf16[384,256]{1,0:T(8,128)(2,1)S(1)}, u32[]{:S(2)}, u32[]{:S(2)}) collective-permute-start(bf16[384,256]{1,0:T(8,128)(2,1)} %shard_map.137.refs_0_), channel_id=1, source_target_pairs={{0,2},{1,3},{2,0},{3,1},{4,6},{5,7},{6,4},{7,5},{8,10},{9,11},{10,... | collective-permute-start | bytes 589832 | tf_op jit(solution)/shard_map/ppermute | solution.py:31
  107.4 4.7 %collective-permute-start.15 = (bf16[128,256]{1,0:T(8,128)(2,1)}, bf16[128,256]{1,0:T(8,128)(2,1)S(1)}, u32[]{:S(2)}, u32[]{:S(2)}) collective-permute-start(bf16[128,256]{1,0:T(8,128)(2,1)} %get-tuple-element.32), channel_id=1, source_target_pairs={{0,8},{4,12},{8,0},{12,4},{1,9},{5,13},{9,1},{13,5},{2,10},{6,14},... | collective-permute-start | bytes 196616 | tf_op jit(solution)/shard_map/ppermute | solution.py:31
  108.1 9.4 %collective-permute-start.27 = (bf16[256,256]{1,0:T(8,128)(2,1)S(1)}, bf16[256,256]{1,0:T(8,128)(2,1)S(1)}, u32[]{:S(2)}, u32[]{:S(2)}) collective-permute-start(bf16[256,256]{1,0:T(8,128)(2,1)S(1)} %copy-done), channel_id=1, source_target_pairs={{0,2},{1,3},{2,0},{3,1},{4,6},{5,7},{6,4},{7,5},{8,10},{9,11},{10,... | collective-permute-start | bytes 393224 | tf_op jit(solution)/shard_map/ppermute | solution.py:31
  108.4 28.1 %collective-permute-start.31 = (bf16[512,256]{1,0:T(8,128)(2,1)S(1)}, bf16[512,256]{1,0:T(8,128)(2,1)S(1)}, u32[]{:S(2)}, u32[]{:S(2)}) collective-permute-start(bf16[512,256]{1,0:T(8,128)(2,1)S(1)} %collective-permute-done.30.refs_14_), channel_id=1, source_target_pairs={{0,4},{4,0},{8,12},{12,8},{1,5},{5,1},{9,13},{13,9},{2,6},{6,2},{1... | collective-permute-start | bytes 786440 | tf_op jit(solution)/shard_map/ppermute | solution.py:31
  108.8 12.7 %collective-permute-start.26 = (bf16[256,256]{1,0:T(8,128)(2,1)S(1)}, bf16[256,256]{1,0:T(8,128)(2,1)S(1)}, u32[]{:S(2)}, u32[]{:S(2)}) collective-permute-start(bf16[256,256]{1,0:T(8,128)(2,1)S(1)} %copy-done), channel_id=1, source_target_pairs={{0,1},{1,0},{2,3},{3,2},{4,5},{5,4},{6,7},{7,6},{8,9},{9,8},{10,11... | collective-permute-start | bytes 393224 | tf_op jit(solution)/shard_map/ppermute | solution.py:31
  112.1 5.4 %collective-permute-start.16 = (bf16[128,256]{1,0:T(8,128)(2,1)}, bf16[128,256]{1,0:T(8,128)(2,1)S(1)}, u32[]{:S(2)}, u32[]{:S(2)}) collective-permute-start(bf16[128,256]{1,0:T(8,128)(2,1)} %get-tuple-element.33), channel_id=1, source_target_pairs={{0,12},{4,8},{8,4},{12,0},{1,13},{5,9},{9,5},{13,1},{2,14},{6,10},... | collective-permute-start | bytes 196616 | tf_op jit(solution)/shard_map/ppermute | solution.py:31
  117.4 15.3 %collective-permute-start.28 = (bf16[256,256]{1,0:T(8,128)(2,1)S(1)}, bf16[256,256]{1,0:T(8,128)(2,1)S(1)}, u32[]{:S(2)}, u32[]{:S(2)}) collective-permute-start(bf16[256,256]{1,0:T(8,128)(2,1)S(1)} %collective-permute-done.27.refs_6_), channel_id=1, source_target_pairs={{0,1},{1,0},{2,3},{3,2},{4,5},{5,4},{6,7},{7,6},{8,9},{9,8},{10,11... | collective-permute-start | bytes 393224 | tf_op jit(solution)/shard_map/ppermute | solution.py:31
  117.5 19.5 %collective-permute-start.17 = (bf16[384,256]{1,0:T(8,128)(2,1)S(1)}, bf16[384,256]{1,0:T(8,128)(2,1)S(1)}, u32[]{:S(2)}, u32[]{:S(2)}) collective-permute-start(bf16[384,256]{1,0:T(8,128)(2,1)S(1)} %copy-done.2), channel_id=1, source_target_pairs={{0,1},{1,0},{2,3},{3,2},{4,5},{5,4},{6,7},{7,6},{8,9},{9,8},{10,11... | collective-permute-start | bytes 589832 | tf_op jit(solution)/shard_map/ppermute | solution.py:31
  119.5 17.5 %collective-permute-start.19 = (bf16[384,256]{1,0:T(8,128)(2,1)S(1)}, bf16[384,256]{1,0:T(8,128)(2,1)S(1)}, u32[]{:S(2)}, u32[]{:S(2)}) collective-permute-start(bf16[384,256]{1,0:T(8,128)(2,1)S(1)} %collective-permute-done.18.refs_2_), channel_id=1, source_target_pairs={{0,1},{1,0},{2,3},{3,2},{4,5},{5,4},{6,7},{7,6},{8,9},{9,8},{10,11... | collective-permute-start | bytes 589832 | tf_op jit(solution)/shard_map/ppermute | solution.py:31
  121.5 8.4 %collective-permute-start.21 = (bf16[128,256]{1,0:T(8,128)(2,1)}, bf16[128,256]{1,0:T(8,128)(2,1)S(1)}, u32[]{:S(2)}, u32[]{:S(2)}) collective-permute-start(bf16[128,256]{1,0:T(8,128)(2,1)} %shard_map.139.refs_4_), channel_id=1, source_target_pairs={{0,2},{1,3},{2,0},{3,1},{4,6},{5,7},{6,4},{7,5},{8,10},{9,11},{10,... | collective-permute-start | bytes 196616 | tf_op jit(solution)/shard_map/ppermute | solution.py:31
  129.9 6.7 %collective-permute-start.20 = (bf16[128,256]{1,0:T(8,128)(2,1)}, bf16[128,256]{1,0:T(8,128)(2,1)S(1)}, u32[]{:S(2)}, u32[]{:S(2)}) collective-permute-start(bf16[128,256]{1,0:T(8,128)(2,1)} %shard_map.139.refs_4_), channel_id=1, source_target_pairs={{0,1},{1,0},{2,3},{3,2},{4,5},{5,4},{6,7},{7,6},{8,9},{9,8},{10,11... | collective-permute-start | bytes 196616 | tf_op jit(solution)/shard_map/ppermute | solution.py:31
  132.7 4.3 %collective-permute-start.22 = (bf16[128,256]{1,0:T(8,128)(2,1)S(1)}, bf16[128,256]{1,0:T(8,128)(2,1)S(1)}, u32[]{:S(2)}, u32[]{:S(2)}) collective-permute-start(bf16[128,256]{1,0:T(8,128)(2,1)S(1)} %collective-permute-done.21.refs_6_), channel_id=1, source_target_pairs={{0,1},{1,0},{2,3},{3,2},{4,5},{5,4},{6,7},{7,6},{8,9},{9,8},{10,11... | collective-permute-start | bytes 196616 | tf_op jit(solution)/shard_map/ppermute | solution.py:31
  143.5 2.1 %collective-permute-start.32 = (bf16[2,512,256]{2,1,0:T(8,128)(2,1)}, bf16[2,512,256]{2,1,0:T(8,128)(2,1)S(1)}, u32[]{:S(2)}, u32[]{:S(2)}) collective-permute-start(bf16[2,512,256]{2,1,0:T(8,128)(2,1)} %get-tuple-element.37), channel_id=1, source_target_pairs={{0,4},{4,0},{8,12},{12,8},{1,5},{5,1},{9,13},{13,9},{2,6},{6,2},{1... | collective-permute-start | bytes 1572872 | tf_op jit(solution)/shard_map/ppermute | solution.py:31
  147.0 8.4 %collective-permute-start.33 = (bf16[1,512,256]{2,1,0:T(8,128)(2,1)S(1)}, bf16[1,512,256]{2,1,0:T(8,128)(2,1)S(1)}, u32[]{:S(2)}, u32[]{:S(2)}) collective-permute-start(bf16[1,512,256]{2,1,0:T(8,128)(2,1)S(1)} %slice.18), channel_id=1, source_target_pairs={{0,8},{4,12},{8,0},{12,4},{1,9},{5,13},{9,1},{13,5},{2,10},{6,14},... | collective-permute-start | bytes 786440 | tf_op jit(solution)/shard_map/ppermute | solution.py:31
  (42 other events, 491.1 us)

commit v4 on v3

--- a/solution.py
+++ b/solution.py
@@ -14,6 +14,8 @@
 BF16 = jnp.bfloat16
 F32 = jnp.float32
 ANY = pl.BlockSpec(memory_space=pl.ANY)
+SMALL = pltpu.CompilerParams(vmem_limit_bytes=12 << 20)
+LARGE = pltpu.CompilerParams(vmem_limit_bytes=20 << 20)
 
 
 def qk(q, k):
@@ -99,6 +101,7 @@
             transcendentals=n * total * hist_rows * width // HEAD,
             bytes_accessed=4 * users * hist_rows * width,
         ),
+        compiler_params=LARGE,
     )(hist_len, place, *[q for q, _ in queries], keys, values, *after)
 
 
@@ -126,6 +129,7 @@
         in_specs=[at(own_at)] + [full((rows, width))] * n + [full((1, width)), at(gate_at)],
         out_specs=full((rows, width)),
         out_shape=jax.ShapeDtypeStruct((rows, width), BF16),
+        compiler_params=SMALL,
     )(own, *others, gain, gate)
 
 
@@ -174,6 +178,7 @@
             out_specs=[full(shape)] * 2,
         ),
         out_shape=[jax.ShapeDtypeStruct(shape, BF16)] * 2,
+        compiler_params=SMALL,
         name="early_keys",
     )(column, *flat, key_weight, value_weight)
 
@@ -223,6 +228,7 @@
             scratch_shapes=[pltpu.VMEM((rows * n_users, width), BF16)] * 2,
         ),
         out_shape=[jax.ShapeDtypeStruct(shape, F32), jax.ShapeDtypeStruct(shape, BF16)],
+        compiler_params=SMALL,
         name="cand_sums",
     )(cand_count, place, column, *flat, key_weight, value_weight, *early, *cands)
 
@@ -259,6 +265,7 @@
             out_specs=block,
         ),
         out_shape=jax.ShapeDtypeStruct((rows, width), BF16),
+        compiler_params=SMALL,
         name="gate_cands",
     )(cand_count, place, own, *others, gain, gate)
 
@@ -297,13 +304,17 @@
         event_gain = event_gain.reshape(1, width)
         cand_gain = cand_gain.reshape(1, width)
         gates = event_gate.reshape(n_users * rows, width)
+        new_in_hbm, *kv_in_hbm = [
+            pltpu.with_memory_space_constraint(x, pltpu.HBM) for x in (new_queries, hist_keys, hist_values)
+        ]
         early_q = gather_pieces(new_queries[:1], "ev", n_ev, skip=(1,))
         queries = gather_pieces(new_queries, "ev", n_ev)
         early_q[1] = queries[1]
+        queries[0] = new_in_hbm
         cands = gather_pieces(cand_queries, "ev", n_ev)
-        hist = (hist_len, place, hist_keys, hist_values)
-
-        own01 = attend(0, (2, 2), half, 0, [(new_queries, 0)], True, *hist, ())[0]
+        hist = (hist_len, place, *kv_in_hbm)
+
+        own01 = attend(0, (2, 2), half, 0, [(new_in_hbm, 0)], True, *hist, ())[0]
 
         def reduce(own, own_at, outs, halves, gate_at):
             others = [swap(o, "ev", n_ev, j + 1) for j, o in enumerate(outs)]

time: 160 us -> 144 us (0.900)
  Pallas kernels: 77 us -> 60.2 us
  other arithmetic: 3.06 us -> 0.95 us
  waiting for transfers between devices: 41.4 us -> 43.2 us
    pallas_call x4, Pallas kernels: 8.29 us -> 1.06 us  [gate_events(): pl.pallas_call(kern, grid=(1,), in_specs=[at(own_at)] + [full((rows, widt...]
    pallas_call x5, Pallas kernels: 56.8 us -> 52.9 us  [attend(): pl.pallas_call(kern, grid_spec=pltpu.PrefetchScalarGridSpec(num_scalar_pr...]
    pallas_call x1, Pallas kernels: 3.14 us -> 0.71 us  [early_keys(): pl.pallas_call(kern, grid_spec=pltpu.PrefetchScalarGridSpec(num_scalar_pr...]
    pallas_call x1, Pallas kernels: 5.68 us -> 3.63 us  [cand_sums(): pl.pallas_call(kern, grid_spec=pltpu.PrefetchScalarGridSpec(num_scalar_pr...]
    ppermute x34, waiting for transfers between devices: 41.4 us -> 43.2 us  [swap(): return lax.ppermute(x, axis, [(i, i ^ j) for i in range(size)])]
    unnamed x80 -> x42, local copies, waits for them, and re-layouts: 5.69 us -> 7.45 us
  transfers between devices with their start and end apart: 34 -> 34, of which waited for: 12 -> 11; matrix products, arithmetic and copies ran while one was open for 2% -> 1% of each run, Pallas kernels for 36% -> 31%
where the time goes in v4:
time: 144 us; the launch traced here: 143 us
  Pallas kernels  60.2 us (42%)
  waiting for transfers between devices  43.2 us (30%)
  starting transfers between devices  29.5 us (20%)
  local copies, waits for them, and re-layouts  8.43 us (6%)
    pallas_call x5, Pallas kernels, attend(): pl.pallas_call(kern, grid_spec=pltpu.PrefetchScalarGridSpec(num_scalar_pr...  52.9 us
    ppermute x34, waiting for transfers between devices, swap(): return lax.ppermute(x, axis, [(i, i ^ j) for i in range(size)])  43.2 us
    ppermute x34, starting transfers between devices, swap(): return lax.ppermute(x, axis, [(i, i ^ j) for i in range(size)])  29.5 us
    unnamed x42, local copies, waits for them, and re-layouts  7.45 us
    pallas_call x1, Pallas kernels, cand_sums(): pl.pallas_call(kern, grid_spec=pltpu.PrefetchScalarGridSpec(num_scalar_pr...  3.63 us
  transfers between devices with their start and end apart: 34, of which 11 were waited for; matrix products, arithmetic and copies ran while one was open for 1% of the time, Pallas kernels for 31%

profile of v4, /device:TPU:0, one launch (start us, length us, event | category | flops | bytes accessed | tf_op | source)
XLA Modules:
  0.0 143.3 jit_solution(7099651963585035352)
XLA Ops:
  0.6 0.9 slice.12
  1.5 3.1 %collective-permute-start.1 = (bf16[1,256,256]{2,1,0:T(8,128)(2,1)S(1)}, bf16[1,256,256]{2,1,0:T(8,128)(2,1)S(1)}, u32[]{:S(2)}, u32[]{:S(2)}) collective-permute-start(bf16[1,256,256]{2,1,0:T(8,128)(2,1)S(1)} %slice.12), channel_id=1, source_target_pairs={{0,8},{4,12},{8,0},{12,4},{1,9},{5,13},{9,1},{13,5},{2,10},{6,14},... | collective-permute-start | bytes 393224 | tf_op jit(solution)/shard_map/ppermute | solution.py:33
  4.7 4.3 %collective-permute-done.1.refs_1_ = bf16[1,256,256]{2,1,0:T(8,128)(2,1)S(1)} collective-permute-done((bf16[1,256,256]{2,1,0:T(8,128)(2,1)S(1)}, bf16[1,256,256]{2,1,0:T(8,128)(2,1)S(1)}, u32[]{:S(2)}, u32[]{:S(2)}) %collective-permute-start.1) | collective-permute-done | bytes 131104 | tf_op jit(solution)/shard_map/ppermute | solution.py:33
  9.6 8.3 %shard_map.131.refs_5_.own_ref = f32[512,256]{1,0:T(8,128)S(1)} custom-call(s32[4]{0:T(128)S(1)} %copy-done.18, s32[1]{0:T(128)} %bitcast.place_ref, bf16[4,256,256]{2,1,0:T(8,128)(2,1)} %refs_0_.5, bf16[4,4096,256]{2,1,0:T(8,128)(2,1)} %refs_4_.7, bf16[4,4096,256]{2,1,0:T(8,128)(2,1)} %refs_5_.3), custom_call_target="tpu_custom_call" | custom-call | flops 4294967296 | bytes 8388608 | tf_op jit(solution)/shard_map/pallas_call | solution.py:90
  17.9 1.4 %collective-permute-done.6.refs_1_.refs_2_ = bf16[4,256,256]{2,1,0:T(8,128)(2,1)S(1)} collective-permute-done((bf16[4,256,256]{2,1,0:T(8,128)(2,1)}, bf16[4,256,256]{2,1,0:T(8,128)(2,1)S(1)}, u32[]{:S(2)}, u32[]{:S(2)}) %collective-permute-start.6) | collective-permute-done | bytes 524320 | tf_op jit(solution)/shard_map/ppermute | solution.py:33
  19.4 9.7 %shard_map.132 = (bf16[256,256]{1,0:T(8,128)(2,1)S(1)}, bf16[256,256]{1,0:T(8,128)(2,1)S(1)}, bf16[256,256]{1,0:T(8,128)(2,1)S(1)}) custom-call(s32[4]{0:T(128)S(1)} %copy-done.18, s32[1]{0:T(128)} %bitcast.place_ref, bf16[4,256,256]{2,1,0:T(8,128)(2,1)S(1)} %collective-permute-done.refs_0_.refs_1_, bf16[1,256,256]{2,1,0:T(8,128)(2,1)S(1)} %collective-permute-done.1.refs_1_, ...), custom_call_target="tpu_custom_call" | custom-call | flops 6442450944 | bytes 4194304 | tf_op jit(solution)/shard_map/pallas_call | solution.py:90
  29.2 1.8 %collective-permute-start.5 = (bf16[256,256]{1,0:T(8,128)(2,1)S(1)}, bf16[256,256]{1,0:T(8,128)(2,1)S(1)}, u32[]{:S(2)}, u32[]{:S(2)}) collective-permute-start(bf16[256,256]{1,0:T(8,128)(2,1)S(1)} %get-tuple-element.22), channel_id=1, source_target_pairs={{0,12},{4,8},{8,4},{12,0},{1,13},{5,9},{9,5},{13,1},{2,14},{6,10},... | collective-permute-start | bytes 393224 | tf_op jit(solution)/shard_map/ppermute | solution.py:33
  31.0 4.6 %collective-permute-done.4.refs_1_ = bf16[256,256]{1,0:T(8,128)(2,1)S(1)} collective-permute-done((bf16[256,256]{1,0:T(8,128)(2,1)S(1)}, bf16[256,256]{1,0:T(8,128)(2,1)S(1)}, u32[]{:S(2)}, u32[]{:S(2)}) %collective-permute-start.4) | collective-permute-done | bytes 131104 | tf_op jit(solution)/shard_map/ppermute | solution.py:33
  35.6 1.7 %collective-permute-done.5.refs_2_ = bf16[256,256]{1,0:T(8,128)(2,1)S(1)} collective-permute-done((bf16[256,256]{1,0:T(8,128)(2,1)S(1)}, bf16[256,256]{1,0:T(8,128)(2,1)S(1)}, u32[]{:S(2)}, u32[]{:S(2)}) %collective-permute-start.5) | collective-permute-done | bytes 131104 | tf_op jit(solution)/shard_map/ppermute | solution.py:33
  37.6 9.7 %shard_map.134 = (bf16[256,256]{1,0:T(8,128)(2,1)S(1)}, bf16[256,256]{1,0:T(8,128)(2,1)S(1)}, bf16[256,256]{1,0:T(8,128)(2,1)S(1)}) custom-call(s32[4]{0:T(128)S(1)} %copy-done.18, s32[1]{0:T(128)} %bitcast.place_ref, bf16[4,256,256]{2,1,0:T(8,128)(2,1)S(1)} %collective-permute-done.refs_0_.refs_1_, ...), custom_call_target="tpu_custom_call" | custom-call | flops 6442450944 | bytes 4194304 | tf_op jit(solution)/shard_map/pallas_call | solution.py:90
  48.0 17.7 %shard_map.136 = (f32[384,256]{1,0:T(8,128)S(1)}, bf16[384,256]{1,0:T(8,128)(2,1)S(1)}, bf16[384,256]{1,0:T(8,128)(2,1)S(1)}, bf16[384,256]{1,0:T(8,128)(2,1)S(1)}) custom-call(s32[4]{0:T(128)S(1)} %copy-done.18, s32[1]{0:T(128)} %bitcast.place_ref, bf16[4,256,256]{2,1,0:T(8,128)(2,1)} %refs_0_.5, ...), custom_call_target="tpu_custom_call" | custom-call | flops 12884901888 | bytes 8388608 | tf_op jit(solution)/shard_map/pallas_call | solution.py:90
  65.9 1.7 %collective-permute-start.12 = (bf16[384,256]{1,0:T(8,128)(2,1)S(1)}, bf16[384,256]{1,0:T(8,128)(2,1)S(1)}, u32[]{:S(2)}, u32[]{:S(2)}) collective-permute-start(bf16[384,256]{1,0:T(8,128)(2,1)S(1)} %get-tuple-element.28), channel_id=1, source_target_pairs={{0,8},{4,12},{8,0},{12,4},{1,9},{5,13},{9,1},{13,5},{2,10},{6,14},... | collective-permute-start | bytes 589832 | tf_op jit(solution)/shard_map/ppermute | solution.py:33
  67.6 1.5 %collective-permute-start.9 = (bf16[256,256]{1,0:T(8,128)(2,1)S(1)}, bf16[256,256]{1,0:T(8,128)(2,1)S(1)}, u32[]{:S(2)}, u32[]{:S(2)}) collective-permute-start(bf16[256,256]{1,0:T(8,128)(2,1)S(1)} %get-tuple-element.24), channel_id=1, source_target_pairs={{0,8},{4,12},{8,0},{12,4},{1,9},{5,13},{9,1},{13,5},{2,10},{6,14},... | collective-permute-start | bytes 393224 | tf_op jit(solution)/shard_map/ppermute | solution.py:33
  69.1 2.8 %collective-permute-start.24 = (bf16[256,256]{1,0:T(8,128)(2,1)S(1)}, bf16[256,256]{1,0:T(8,128)(2,1)S(1)}, u32[]{:S(2)}, u32[]{:S(2)}) collective-permute-start(bf16[256,256]{1,0:T(8,128)(2,1)S(1)} %shard_map.133.refs_6_.refs_0_), channel_id=1, source_target_pairs={{0,2},{1,3},{2,0},{3,1},{4,6},{5,7},{6,4},{7,5},{8,10},{9,11},{10,... | collective-permute-start | bytes 393224 | tf_op jit(solution)/shard_map/ppermute | solution.py:33
  71.9 8.2 %collective-permute-done.9.refs_1_ = bf16[256,256]{1,0:T(8,128)(2,1)S(1)} collective-permute-done((bf16[256,256]{1,0:T(8,128)(2,1)S(1)}, bf16[256,256]{1,0:T(8,128)(2,1)S(1)}, u32[]{:S(2)}, u32[]{:S(2)}) %collective-permute-start.9) | collective-permute-done | bytes 131104 | tf_op jit(solution)/shard_map/ppermute | solution.py:33
  80.1 1.5 %collective-permute-start.30 = (bf16[512,256]{1,0:T(8,128)(2,1)S(1)}, bf16[512,256]{1,0:T(8,128)(2,1)S(1)}, u32[]{:S(2)}, u32[]{:S(2)}) collective-permute-start(bf16[512,256]{1,0:T(8,128)(2,1)S(1)} %copy-done.3), channel_id=1, source_target_pairs={{0,8},{4,12},{8,0},{12,4},{1,9},{5,13},{9,1},{13,5},{2,10},{6,14},... | collective-permute-start | bytes 786440 | tf_op jit(solution)/shard_map/ppermute | solution.py:33
  82.0 1.9 %collective-permute-start.23 = (bf16[256,256]{1,0:T(8,128)(2,1)S(1)}, bf16[256,256]{1,0:T(8,128)(2,1)S(1)}, u32[]{:S(2)}, u32[]{:S(2)}) collective-permute-start(bf16[256,256]{1,0:T(8,128)(2,1)S(1)} %shard_map.133.refs_6_.refs_0_), channel_id=1, source_target_pairs={{0,1},{1,0},{2,3},{3,2},{4,5},{5,4},{6,7},{7,6},{8,9},{9,8},{10,11... | collective-permute-start | bytes 393224 | tf_op jit(solution)/shard_map/ppermute | solution.py:33
  84.5 2.9 %collective-permute-start.18 = (bf16[384,256]{1,0:T(8,128)(2,1)S(1)}, bf16[384,256]{1,0:T(8,128)(2,1)S(1)}, u32[]{:S(2)}, u32[]{:S(2)}) collective-permute-start(bf16[384,256]{1,0:T(8,128)(2,1)S(1)} %shard_map.137.refs_0_), channel_id=1, source_target_pairs={{0,2},{1,3},{2,0},{3,1},{4,6},{5,7},{6,4},{7,5},{8,10},{9,11},{10,... | collective-permute-start | bytes 589832 | tf_op jit(solution)/shard_map/ppermute | solution.py:33
  87.3 7.6 %shard_map.138 = (f32[128,256]{1,0:T(8,128)S(1)}, bf16[128,256]{1,0:T(8,128)(2,1)S(1)}, bf16[128,256]{1,0:T(8,128)(2,1)S(1)}, bf16[128,256]{1,0:T(8,128)(2,1)S(1)}) custom-call(s32[4]{0:T(128)S(1)} %copy-done.18, s32[1]{0:T(128)} %bitcast.place_ref, bf16[4,256,256]{2,1,0:T(8,128)(2,1)} %refs_0_.5, ...), custom_call_target="tpu_custom_call" | custom-call | flops 4294967296 | bytes 4194304 | tf_op jit(solution)/shard_map/pallas_call | solution.py:90
  96.3 1.6 %collective-permute-start.26 = (bf16[256,256]{1,0:T(8,128)(2,1)S(1)}, bf16[256,256]{1,0:T(8,128)(2,1)S(1)}, u32[]{:S(2)}, u32[]{:S(2)}) collective-permute-start(bf16[256,256]{1,0:T(8,128)(2,1)S(1)} %shard_map.135.refs_6_.refs_4_), channel_id=1, source_target_pairs={{0,1},{1,0},{2,3},{3,2},{4,5},{5,4},{6,7},{7,6},{8,9},{9,8},{10,11... | collective-permute-start | bytes 393224 | tf_op jit(solution)/shard_map/ppermute | solution.py:33
  97.9 1.7 %collective-permute-done.15.refs_1_ = bf16[128,256]{1,0:T(8,128)(2,1)S(1)} collective-permute-done((bf16[128,256]{1,0:T(8,128)(2,1)S(1)}, bf16[128,256]{1,0:T(8,128)(2,1)S(1)}, u32[]{:S(2)}, u32[]{:S(2)}) %collective-permute-start.15) | collective-permute-done | bytes 65568 | tf_op jit(solution)/shard_map/ppermute | solution.py:33
  99.6 5.4 %collective-permute-done.27.refs_6_ = bf16[256,256]{1,0:T(8,128)(2,1)S(1)} collective-permute-done((bf16[256,256]{1,0:T(8,128)(2,1)S(1)}, bf16[256,256]{1,0:T(8,128)(2,1)S(1)}, u32[]{:S(2)}, u32[]{:S(2)}) %collective-permute-start.27) | collective-permute-done | bytes 131104 | tf_op jit(solution)/shard_map/ppermute | solution.py:33
  105.0 2.0 %collective-permute-start.17 = (bf16[384,256]{1,0:T(8,128)(2,1)S(1)}, bf16[384,256]{1,0:T(8,128)(2,1)S(1)}, u32[]{:S(2)}, u32[]{:S(2)}) collective-permute-start(bf16[384,256]{1,0:T(8,128)(2,1)S(1)} %shard_map.137.refs_0_), channel_id=1, source_target_pairs={{0,1},{1,0},{2,3},{3,2},{4,5},{5,4},{6,7},{7,6},{8,9},{9,8},{10,11... | collective-permute-start | bytes 589832 | tf_op jit(solution)/shard_map/ppermute | solution.py:33
  108.0 1.7 %collective-permute-start.21 = (bf16[128,256]{1,0:T(8,128)(2,1)S(1)}, bf16[128,256]{1,0:T(8,128)(2,1)}, u32[]{:S(2)}, u32[]{:S(2)}) collective-permute-start(bf16[128,256]{1,0:T(8,128)(2,1)S(1)} %shard_map.139.refs_4_), channel_id=1, source_target_pairs={{0,2},{1,3},{2,0},{3,1},{4,6},{5,7},{6,4},{7,5},{8,10},{9,11},{10,... | collective-permute-start | bytes 196616 | tf_op jit(solution)/shard_map/ppermute | solution.py:33
  109.7 7.6 %collective-permute-done.21.refs_6_ = bf16[128,256]{1,0:T(8,128)(2,1)} collective-permute-done((bf16[128,256]{1,0:T(8,128)(2,1)S(1)}, bf16[128,256]{1,0:T(8,128)(2,1)}, u32[]{:S(2)}, u32[]{:S(2)}) %collective-permute-start.21) | collective-permute-done | bytes 65568 | tf_op jit(solution)/shard_map/ppermute | solution.py:33
  117.3 3.0 %collective-permute-start.20 = (bf16[128,256]{1,0:T(8,128)(2,1)S(1)}, bf16[128,256]{1,0:T(8,128)(2,1)}, u32[]{:S(2)}, u32[]{:S(2)}) collective-permute-start(bf16[128,256]{1,0:T(8,128)(2,1)S(1)} %shard_map.139.refs_4_), channel_id=1, source_target_pairs={{0,1},{1,0},{2,3},{3,2},{4,5},{5,4},{6,7},{7,6},{8,9},{9,8},{10,11... | collective-permute-start | bytes 196616 | tf_op jit(solution)/shard_map/ppermute | solution.py:33
  123.8 0.9 copy-done.12
  127.3 3.6 %cand_sums.1 = (f32[2,512,256]{2,1,0:T(8,128)S(1)}, bf16[2,512,256]{2,1,0:T(8,128)(2,1)S(1)}) custom-call(s32[4]{0:T(128)S(1)} %copy-done.19, s32[1]{0:T(128)} %bitcast.place_ref, s32[1]{0:T(128)} %bitcast.4.col_ref, bf16[384,256]{1,0:T(8,128)(2,1)S(1)} %shard_map.137.refs_0_, bf16[384,256]{1,0:T(8,128)(2,1)S(1)} %collective-permute-done.17.refs_1_, ...), custom_call_target="tpu_custom_call" | custom-call | tf_op jit(solution)/shard_map/cand_sums/pallas_call | solution.py:218
  131.0 1.9 %collective-permute-done.32 = bf16[2,512,256]{2,1,0:T(8,128)(2,1)S(1)} collective-permute-done((bf16[2,512,256]{2,1,0:T(8,128)(2,1)S(1)}, bf16[2,512,256]{2,1,0:T(8,128)(2,1)S(1)}, u32[]{:S(2)}, u32[]{:S(2)}) %collective-permute-start.32) | collective-permute-done | bytes 524320 | tf_op jit(solution)/shard_map/ppermute | solution.py:33
  133.1 1.5 %collective-permute-start.33 = (bf16[1,512,256]{2,1,0:T(8,128)(2,1)S(1)}, bf16[1,512,256]{2,1,0:T(8,128)(2,1)S(1)}, u32[]{:S(2)}, u32[]{:S(2)}) collective-permute-start(bf16[1,512,256]{2,1,0:T(8,128)(2,1)S(1)} %slice.18), channel_id=1, source_target_pairs={{0,8},{4,12},{8,0},{12,4},{1,9},{5,13},{9,1},{13,5},{2,10},{6,14},... | collective-permute-start | bytes 786440 | tf_op jit(solution)/shard_map/ppermute | solution.py:33
  135.5 6.0 %collective-permute-done.33.refs_1_ = bf16[1,512,256]{2,1,0:T(8,128)(2,1)S(1)} collective-permute-done((bf16[1,512,256]{2,1,0:T(8,128)(2,1)S(1)}, bf16[1,512,256]{2,1,0:T(8,128)(2,1)S(1)}, u32[]{:S(2)}, u32[]{:S(2)}) %collective-permute-start.33) | collective-permute-done | bytes 262176 | tf_op jit(solution)/shard_map/ppermute | solution.py:33
  141.5 1.9 %gate_cands.1 = bf16[512,256]{1,0:T(8,128)(2,1)} custom-call(s32[4]{0:T(128)S(1)} %copy-done.19, s32[1]{0:T(128)} %bitcast.place_ref, f32[1,512,256]{2,1,0:T(8,128)S(1)} %slice.15.refs_0_, bf16[1,512,256]{2,1,0:T(8,128)(2,1)S(1)} %collective-permute-done.33.refs_1_, f32[1,256]{1,0:T(1,128)S(1)} %bitcast.14, bf16[512,256]{1,0:T(8,128)(2,1)S(1)} %copy-done.4), custom_call_target="tpu_custom_call" | custom-call | tf_op jit(solution)/shard_map/gate_cands/pallas_call | solution.py:259
  (95 shorter events, 12.3 us)
Async XLA Ops:
  1.5 7.4 %collective-permute-start.1 = (bf16[1,256,256]{2,1,0:T(8,128)(2,1)S(1)}, bf16[1,256,256]{2,1,0:T(8,128)(2,1)S(1)}, u32[]{:S(2)}, u32[]{:S(2)}) collective-permute-start(bf16[1,256,256]{2,1,0:T(8,128)(2,1)S(1)} %slice.12), channel_id=1, source_target_pairs={{0,8},{4,12},{8,0},{12,4},{1,9},{5,13},{9,1},{13,5},{2,10},{6,14},... | collective-permute-start | bytes 393224 | tf_op jit(solution)/shard_map/ppermute | solution.py:33
  4.6 14.7 %collective-permute-start.6 = (bf16[4,256,256]{2,1,0:T(8,128)(2,1)}, bf16[4,256,256]{2,1,0:T(8,128)(2,1)S(1)}, u32[]{:S(2)}, u32[]{:S(2)}) collective-permute-start(bf16[4,256,256]{2,1,0:T(8,128)(2,1)} %refs_0_.5), channel_id=1, source_target_pairs={{0,8},{4,12},{8,0},{12,4},{1,9},{5,13},{9,1},{13,5},{2,10},{6,14},... | collective-permute-start | bytes 1572872 | tf_op jit(solution)/shard_map/ppermute | solution.py:33
  4.7 14.7 %collective-permute-start = (bf16[4,256,256]{2,1,0:T(8,128)(2,1)}, bf16[4,256,256]{2,1,0:T(8,128)(2,1)S(1)}, u32[]{:S(2)}, u32[]{:S(2)}) collective-permute-start(bf16[4,256,256]{2,1,0:T(8,128)(2,1)} %refs_0_.5), channel_id=1, source_target_pairs={{0,4},{4,0},{8,12},{12,8},{1,5},{5,1},{9,13},{13,9},{2,6},{6,2},{1... | collective-permute-start | bytes 1572872 | tf_op jit(solution)/shard_map/ppermute | solution.py:33
  9.0 10.4 %collective-permute-start.2 = (bf16[1,256,256]{2,1,0:T(8,128)(2,1)S(1)}, bf16[1,256,256]{2,1,0:T(8,128)(2,1)S(1)}, u32[]{:S(2)}, u32[]{:S(2)}) collective-permute-start(bf16[1,256,256]{2,1,0:T(8,128)(2,1)S(1)} %collective-permute-done.1.refs_1_), channel_id=1, source_target_pairs={{0,4},{4,0},{8,12},{12,8},{1,5},{5,1},{9,13},{13,9},{2,6},{6,2},{1... | collective-permute-start | bytes 393224 | tf_op jit(solution)/shard_map/ppermute | solution.py:33
  19.3 18.2 %collective-permute-start.7 = (bf16[4,256,256]{2,1,0:T(8,128)(2,1)S(1)}, bf16[4,256,256]{2,1,0:T(8,128)(2,1)S(1)}, u32[]{:S(2)}, u32[]{:S(2)}) collective-permute-start(bf16[4,256,256]{2,1,0:T(8,128)(2,1)S(1)} %collective-permute-done.6.refs_1_.refs_2_), channel_id=1, source_target_pairs={{0,4},{4,0},{8,12},{12,8},{1,5},{5,1},{9,13},{13,9},{2,6},{6,2},{1... | collective-permute-start | bytes 1572872 | tf_op jit(solution)/shard_map/ppermute | solution.py:33
  29.1 6.4 %collective-permute-start.4 = (bf16[256,256]{1,0:T(8,128)(2,1)S(1)}, bf16[256,256]{1,0:T(8,128)(2,1)S(1)}, u32[]{:S(2)}, u32[]{:S(2)}) collective-permute-start(bf16[256,256]{1,0:T(8,128)(2,1)S(1)} %get-tuple-element.21), channel_id=1, source_target_pairs={{0,8},{4,12},{8,0},{12,4},{1,9},{5,13},{9,1},{13,5},{2,10},{6,14},... | collective-permute-start | bytes 393224 | tf_op jit(solution)/shard_map/ppermute | solution.py:33
  29.2 8.1 %collective-permute-start.5 = (bf16[256,256]{1,0:T(8,128)(2,1)S(1)}, bf16[256,256]{1,0:T(8,128)(2,1)S(1)}, u32[]{:S(2)}, u32[]{:S(2)}) collective-permute-start(bf16[256,256]{1,0:T(8,128)(2,1)S(1)} %get-tuple-element.22), channel_id=1, source_target_pairs={{0,12},{4,8},{8,4},{12,0},{1,13},{5,9},{9,5},{13,1},{2,14},{6,10},... | collective-permute-start | bytes 393224 | tf_op jit(solution)/shard_map/ppermute | solution.py:33
  47.3 20.3 %collective-permute-start.8 = (bf16[256,256]{1,0:T(8,128)(2,1)S(1)}, bf16[256,256]{1,0:T(8,128)(2,1)S(1)}, u32[]{:S(2)}, u32[]{:S(2)}) collective-permute-start(bf16[256,256]{1,0:T(8,128)(2,1)S(1)} %get-tuple-element.23.refs_7_), channel_id=1, source_target_pairs={{0,4},{4,0},{8,12},{12,8},{1,5},{5,1},{9,13},{13,9},{2,6},{6,2},{1... | collective-permute-start | bytes 393224 | tf_op jit(solution)/shard_map/ppermute | solution.py:33
  47.7 21.4 %collective-permute-start.10 = (bf16[256,256]{1,0:T(8,128)(2,1)S(1)}, bf16[256,256]{1,0:T(8,128)(2,1)S(1)}, u32[]{:S(2)}, u32[]{:S(2)}) collective-permute-start(bf16[256,256]{1,0:T(8,128)(2,1)S(1)} %get-tuple-element.25), channel_id=1, source_target_pairs={{0,12},{4,8},{8,4},{12,0},{1,13},{5,9},{9,5},{13,1},{2,14},{6,10},... | collective-permute-start | bytes 393224 | tf_op jit(solution)/shard_map/ppermute | solution.py:33
  65.7 16.2 %collective-permute-start.11 = (bf16[384,256]{1,0:T(8,128)(2,1)S(1)}, bf16[384,256]{1,0:T(8,128)(2,1)S(1)}, u32[]{:S(2)}, u32[]{:S(2)}) collective-permute-start(bf16[384,256]{1,0:T(8,128)(2,1)S(1)} %get-tuple-element.27), channel_id=1, source_target_pairs={{0,4},{4,0},{8,12},{12,8},{1,5},{5,1},{9,13},{13,9},{2,6},{6,2},{1... | collective-permute-start | bytes 589832 | tf_op jit(solution)/shard_map/ppermute | solution.py:33
  65.9 17.9 %collective-permute-start.12 = (bf16[384,256]{1,0:T(8,128)(2,1)S(1)}, bf16[384,256]{1,0:T(8,128)(2,1)S(1)}, u32[]{:S(2)}, u32[]{:S(2)}) collective-permute-start(bf16[384,256]{1,0:T(8,128)(2,1)S(1)} %get-tuple-element.28), channel_id=1, source_target_pairs={{0,8},{4,12},{8,0},{12,4},{1,9},{5,13},{9,1},{13,5},{2,10},{6,14},... | collective-permute-start | bytes 589832 | tf_op jit(solution)/shard_map/ppermute | solution.py:33
  67.6 16.4 %collective-permute-start.13 = (bf16[384,256]{1,0:T(8,128)(2,1)S(1)}, bf16[384,256]{1,0:T(8,128)(2,1)S(1)}, u32[]{:S(2)}, u32[]{:S(2)}) collective-permute-start(bf16[384,256]{1,0:T(8,128)(2,1)S(1)} %get-tuple-element.29), channel_id=1, source_target_pairs={{0,12},{4,8},{8,4},{12,0},{1,13},{5,9},{9,5},{13,1},{2,14},{6,10},... | collective-permute-start | bytes 589832 | tf_op jit(solution)/shard_map/ppermute | solution.py:33
  67.6 12.5 %collective-permute-start.9 = (bf16[256,256]{1,0:T(8,128)(2,1)S(1)}, bf16[256,256]{1,0:T(8,128)(2,1)S(1)}, u32[]{:S(2)}, u32[]{:S(2)}) collective-permute-start(bf16[256,256]{1,0:T(8,128)(2,1)S(1)} %get-tuple-element.24), channel_id=1, source_target_pairs={{0,8},{4,12},{8,0},{12,4},{1,9},{5,13},{9,1},{13,5},{2,10},{6,14},... | collective-permute-start | bytes 393224 | tf_op jit(solution)/shard_map/ppermute | solution.py:33
  69.1 12.7 %collective-permute-start.24 = (bf16[256,256]{1,0:T(8,128)(2,1)S(1)}, bf16[256,256]{1,0:T(8,128)(2,1)S(1)}, u32[]{:S(2)}, u32[]{:S(2)}) collective-permute-start(bf16[256,256]{1,0:T(8,128)(2,1)S(1)} %shard_map.133.refs_6_.refs_0_), channel_id=1, source_target_pairs={{0,2},{1,3},{2,0},{3,1},{4,6},{5,7},{6,4},{7,5},{8,10},{9,11},{10,... | collective-permute-start | bytes 393224 | tf_op jit(solution)/shard_map/ppermute | solution.py:33
  80.1 14.9 %collective-permute-start.30 = (bf16[512,256]{1,0:T(8,128)(2,1)S(1)}, bf16[512,256]{1,0:T(8,128)(2,1)S(1)}, u32[]{:S(2)}, u32[]{:S(2)}) collective-permute-start(bf16[512,256]{1,0:T(8,128)(2,1)S(1)} %copy-done.3), channel_id=1, source_target_pairs={{0,8},{4,12},{8,0},{12,4},{1,9},{5,13},{9,1},{13,5},{2,10},{6,14},... | collective-permute-start | bytes 786440 | tf_op jit(solution)/shard_map/ppermute | solution.py:33
  81.9 13.2 %collective-permute-start.29 = (bf16[512,256]{1,0:T(8,128)(2,1)S(1)}, bf16[512,256]{1,0:T(8,128)(2,1)S(1)}, u32[]{:S(2)}, u32[]{:S(2)}) collective-permute-start(bf16[512,256]{1,0:T(8,128)(2,1)S(1)} %copy-done.3), channel_id=1, source_target_pairs={{0,4},{4,0},{8,12},{12,8},{1,5},{5,1},{9,13},{13,9},{2,6},{6,2},{1... | collective-permute-start | bytes 786440 | tf_op jit(solution)/shard_map/ppermute | solution.py:33
  82.0 13.7 %collective-permute-start.23 = (bf16[256,256]{1,0:T(8,128)(2,1)S(1)}, bf16[256,256]{1,0:T(8,128)(2,1)S(1)}, u32[]{:S(2)}, u32[]{:S(2)}) collective-permute-start(bf16[256,256]{1,0:T(8,128)(2,1)S(1)} %shard_map.133.refs_6_.refs_0_), channel_id=1, source_target_pairs={{0,1},{1,0},{2,3},{3,2},{4,5},{5,4},{6,7},{7,6},{8,9},{9,8},{10,11... | collective-permute-start | bytes 393224 | tf_op jit(solution)/shard_map/ppermute | solution.py:33
  83.8 12.0 %collective-permute-start.25 = (bf16[256,256]{1,0:T(8,128)(2,1)S(1)}, bf16[256,256]{1,0:T(8,128)(2,1)S(1)}, u32[]{:S(2)}, u32[]{:S(2)}) collective-permute-start(bf16[256,256]{1,0:T(8,128)(2,1)S(1)} %collective-permute-done.24.refs_2_), channel_id=1, source_target_pairs={{0,1},{1,0},{2,3},{3,2},{4,5},{5,4},{6,7},{7,6},{8,9},{9,8},{10,11... | collective-permute-start | bytes 393224 | tf_op jit(solution)/shard_map/ppermute | solution.py:33
  84.5 22.6 %collective-permute-start.18 = (bf16[384,256]{1,0:T(8,128)(2,1)S(1)}, bf16[384,256]{1,0:T(8,128)(2,1)S(1)}, u32[]{:S(2)}, u32[]{:S(2)}) collective-permute-start(bf16[384,256]{1,0:T(8,128)(2,1)S(1)} %shard_map.137.refs_0_), channel_id=1, source_target_pairs={{0,2},{1,3},{2,0},{3,1},{4,6},{5,7},{6,4},{7,5},{8,10},{9,11},{10,... | collective-permute-start | bytes 589832 | tf_op jit(solution)/shard_map/ppermute | solution.py:33
  95.1 4.5 %collective-permute-start.15 = (bf16[128,256]{1,0:T(8,128)(2,1)S(1)}, bf16[128,256]{1,0:T(8,128)(2,1)S(1)}, u32[]{:S(2)}, u32[]{:S(2)}) collective-permute-start(bf16[128,256]{1,0:T(8,128)(2,1)S(1)} %get-tuple-element.32), channel_id=1, source_target_pairs={{0,8},{4,12},{8,0},{12,4},{1,9},{5,13},{9,1},{13,5},{2,10},{6,14},... | collective-permute-start | bytes 196616 | tf_op jit(solution)/shard_map/ppermute | solution.py:33
  95.7 9.3 %collective-permute-start.27 = (bf16[256,256]{1,0:T(8,128)(2,1)S(1)}, bf16[256,256]{1,0:T(8,128)(2,1)S(1)}, u32[]{:S(2)}, u32[]{:S(2)}) collective-permute-start(bf16[256,256]{1,0:T(8,128)(2,1)S(1)} %shard_map.135.refs_6_.refs_4_), channel_id=1, source_target_pairs={{0,2},{1,3},{2,0},{3,1},{4,6},{5,7},{6,4},{7,5},{8,10},{9,11},{10,... | collective-permute-start | bytes 393224 | tf_op jit(solution)/shard_map/ppermute | solution.py:33
  95.8 31.4 %collective-permute-start.31 = (bf16[512,256]{1,0:T(8,128)(2,1)S(1)}, bf16[512,256]{1,0:T(8,128)(2,1)S(1)}, u32[]{:S(2)}, u32[]{:S(2)}) collective-permute-start(bf16[512,256]{1,0:T(8,128)(2,1)S(1)} %collective-permute-done.30.refs_14_), channel_id=1, source_target_pairs={{0,4},{4,0},{8,12},{12,8},{1,5},{5,1},{9,13},{13,9},{2,6},{6,2},{1... | collective-permute-start | bytes 786440 | tf_op jit(solution)/shard_map/ppermute | solution.py:33
  96.3 11.0 %collective-permute-start.26 = (bf16[256,256]{1,0:T(8,128)(2,1)S(1)}, bf16[256,256]{1,0:T(8,128)(2,1)S(1)}, u32[]{:S(2)}, u32[]{:S(2)}) collective-permute-start(bf16[256,256]{1,0:T(8,128)(2,1)S(1)} %shard_map.135.refs_6_.refs_4_), channel_id=1, source_target_pairs={{0,1},{1,0},{2,3},{3,2},{4,5},{5,4},{6,7},{7,6},{8,9},{9,8},{10,11... | collective-permute-start | bytes 393224 | tf_op jit(solution)/shard_map/ppermute | solution.py:33
  99.6 5.4 %collective-permute-start.16 = (bf16[128,256]{1,0:T(8,128)(2,1)S(1)}, bf16[128,256]{1,0:T(8,128)(2,1)S(1)}, u32[]{:S(2)}, u32[]{:S(2)}) collective-permute-start(bf16[128,256]{1,0:T(8,128)(2,1)S(1)} %get-tuple-element.33), channel_id=1, source_target_pairs={{0,12},{4,8},{8,4},{12,0},{1,13},{5,9},{9,5},{13,1},{2,14},{6,10},... | collective-permute-start | bytes 196616 | tf_op jit(solution)/shard_map/ppermute | solution.py:33
  105.0 15.4 %collective-permute-start.28 = (bf16[256,256]{1,0:T(8,128)(2,1)S(1)}, bf16[256,256]{1,0:T(8,128)(2,1)S(1)}, u32[]{:S(2)}, u32[]{:S(2)}) collective-permute-start(bf16[256,256]{1,0:T(8,128)(2,1)S(1)} %collective-permute-done.27.refs_6_), channel_id=1, source_target_pairs={{0,1},{1,0},{2,3},{3,2},{4,5},{5,4},{6,7},{7,6},{8,9},{9,8},{10,11... | collective-permute-start | bytes 393224 | tf_op jit(solution)/shard_map/ppermute | solution.py:33
  105.0 22.2 %collective-permute-start.17 = (bf16[384,256]{1,0:T(8,128)(2,1)S(1)}, bf16[384,256]{1,0:T(8,128)(2,1)S(1)}, u32[]{:S(2)}, u32[]{:S(2)}) collective-permute-start(bf16[384,256]{1,0:T(8,128)(2,1)S(1)} %shard_map.137.refs_0_), channel_id=1, source_target_pairs={{0,1},{1,0},{2,3},{3,2},{4,5},{5,4},{6,7},{7,6},{8,9},{9,8},{10,11... | collective-permute-start | bytes 589832 | tf_op jit(solution)/shard_map/ppermute | solution.py:33
  107.1 20.2 %collective-permute-start.19 = (bf16[384,256]{1,0:T(8,128)(2,1)S(1)}, bf16[384,256]{1,0:T(8,128)(2,1)}, u32[]{:S(2)}, u32[]{:S(2)}) collective-permute-start(bf16[384,256]{1,0:T(8,128)(2,1)S(1)} %collective-permute-done.18.refs_2_), channel_id=1, source_target_pairs={{0,1},{1,0},{2,3},{3,2},{4,5},{5,4},{6,7},{7,6},{8,9},{9,8},{10,11... | collective-permute-start | bytes 589832 | tf_op jit(solution)/shard_map/ppermute | solution.py:33
  108.0 9.3 %collective-permute-start.21 = (bf16[128,256]{1,0:T(8,128)(2,1)S(1)}, bf16[128,256]{1,0:T(8,128)(2,1)}, u32[]{:S(2)}, u32[]{:S(2)}) collective-permute-start(bf16[128,256]{1,0:T(8,128)(2,1)S(1)} %shard_map.139.refs_4_), channel_id=1, source_target_pairs={{0,2},{1,3},{2,0},{3,1},{4,6},{5,7},{6,4},{7,5},{8,10},{9,11},{10,... | collective-permute-start | bytes 196616 | tf_op jit(solution)/shard_map/ppermute | solution.py:33
  117.3 9.9 %collective-permute-start.20 = (bf16[128,256]{1,0:T(8,128)(2,1)S(1)}, bf16[128,256]{1,0:T(8,128)(2,1)}, u32[]{:S(2)}, u32[]{:S(2)}) collective-permute-start(bf16[128,256]{1,0:T(8,128)(2,1)S(1)} %shard_map.139.refs_4_), channel_id=1, source_target_pairs={{0,1},{1,0},{2,3},{3,2},{4,5},{5,4},{6,7},{7,6},{8,9},{9,8},{10,11... | collective-permute-start | bytes 196616 | tf_op jit(solution)/shard_map/ppermute | solution.py:33
  121.0 6.2 %collective-permute-start.22 = (bf16[128,256]{1,0:T(8,128)(2,1)}, bf16[128,256]{1,0:T(8,128)(2,1)}, u32[]{:S(2)}, u32[]{:S(2)}) collective-permute-start(bf16[128,256]{1,0:T(8,128)(2,1)} %collective-permute-done.21.refs_6_), channel_id=1, source_target_pairs={{0,1},{1,0},{2,3},{3,2},{4,5},{5,4},{6,7},{7,6},{8,9},{9,8},{10,11... | collective-permute-start | bytes 196616 | tf_op jit(solution)/shard_map/ppermute | solution.py:33
  130.9 2.0 %collective-permute-start.32 = (bf16[2,512,256]{2,1,0:T(8,128)(2,1)S(1)}, bf16[2,512,256]{2,1,0:T(8,128)(2,1)S(1)}, u32[]{:S(2)}, u32[]{:S(2)}) collective-permute-start(bf16[2,512,256]{2,1,0:T(8,128)(2,1)S(1)} %get-tuple-element.37), channel_id=1, source_target_pairs={{0,4},{4,0},{8,12},{12,8},{1,5},{5,1},{9,13},{13,9},{2,6},{6,2},{1... | collective-permute-start | bytes 1572872 | tf_op jit(solution)/shard_map/ppermute | solution.py:33
  133.1 8.4 %collective-permute-start.33 = (bf16[1,512,256]{2,1,0:T(8,128)(2,1)S(1)}, bf16[1,512,256]{2,1,0:T(8,128)(2,1)S(1)}, u32[]{:S(2)}, u32[]{:S(2)}) collective-permute-start(bf16[1,512,256]{2,1,0:T(8,128)(2,1)S(1)} %slice.18), channel_id=1, source_target_pairs={{0,8},{4,12},{8,0},{12,4},{1,9},{5,13},{9,1},{13,5},{2,10},{6,14},... | collective-permute-start | bytes 786440 | tf_op jit(solution)/shard_map/ppermute | solution.py:33
  (23 other events, 366.3 us)

commit v5 on v4

--- a/solution.py
+++ b/solution.py
@@ -37,7 +37,7 @@
     return pl.BlockSpec(shape, lambda *_: (0,) * len(shape))
 
 
-def attend(first_user, counts, half_rows, start, queries, own_first, hist_len, place, keys, values, after):
+def attend(first_user, counts, half_rows, start, queries, own_first, hist_len, place, keys, values, after, resident=True):
     n = len(queries)
     width = queries[0][0].shape[2]
     hist_rows = keys.shape[1]
@@ -64,8 +64,12 @@
                     o = jnp.zeros((n * rows, HEAD), F32)
                     for t in range(0, hist_rows, tile):
                         row = t + lax.broadcasted_iota(jnp.int32, (tile, HEAD), 0)
-                        v = jnp.where(row < left, v_ref[0, t : t + tile], jnp.zeros((tile, HEAD), BF16))
-                        s = qk(q, k_ref[0, t : t + tile])
+                        part = (0, slice(t, t + tile), slice(None))
+                        if resident:
+                            head = pl.multiple_of(pl.program_id(0) * HEAD, HEAD)
+                            part = (first_user + g, slice(t, t + tile), pl.ds(head, HEAD))
+                        v = jnp.where(row < left, v_ref[part], jnp.zeros((tile, HEAD), BF16))
+                        s = qk(q, k_ref[part])
                         w = (s + s * jnp.tanh(s * HALF)).astype(BF16)
                         o = o + jnp.dot(w, v, preferred_element_type=F32)
                     o = o * HALF
@@ -86,6 +90,8 @@
         return pl.BlockSpec((1, take * half_rows, HEAD), lambda h, g, *_: (offset + g, start, h))
 
     hist = pl.BlockSpec((1, hist_rows, HEAD), lambda h, g, *_: (first_user + g, 0, h))
+    if resident:
+        hist = pl.BlockSpec(memory_space=pltpu.VMEM)
     kinds = [F32 if own_first and i == 0 else BF16 for i in range(n)]
     return pl.pallas_call(
         kern,
@@ -312,9 +318,9 @@
         early_q[1] = queries[1]
         queries[0] = new_in_hbm
         cands = gather_pieces(cand_queries, "ev", n_ev)
-        hist = (hist_len, place, *kv_in_hbm)
-
-        own01 = attend(0, (2, 2), half, 0, [(new_in_hbm, 0)], True, *hist, ())[0]
+        hist = (hist_len, place, *[pltpu.with_memory_space_constraint(x, pltpu.VMEM) for x in (hist_keys, hist_values)])
+
+        own01 = attend(0, (2, 2), half, 0, [(new_in_hbm, 0)], True, hist_len, place, *kv_in_hbm, (), resident=False)[0]
 
         def reduce(own, own_at, outs, halves, gate_at):
             others = [swap(o, "ev", n_ev, j + 1) for j, o in enumerate(outs)]

time: 144 us -> 140 us (0.972)
  Pallas kernels: 60.2 us -> 57 us
    pallas_call x5, Pallas kernels: 52.9 us -> 49.7 us  [attend(): pl.pallas_call(kern, grid_spec=pltpu.PrefetchScalarGridSpec(num_scalar_pr...]
    unnamed x42 -> x46, local copies, waits for them, and re-layouts: 7.45 us -> 7.43 us
where the time goes in v5:
time: 140 us; the launch traced here: 139 us
  Pallas kernels  57 us (41%)
  waiting for transfers between devices  42.1 us (30%)
  starting transfers between devices  29.9 us (21%)
  local copies, waits for them, and re-layouts  8.41 us (6%)
    pallas_call x5, Pallas kernels, attend(): pl.pallas_call(kern, grid_spec=pltpu.PrefetchScalarGridSpec(num_scalar_pr...  49.7 us
    ppermute x34, waiting for transfers between devices, swap(): return lax.ppermute(x, axis, [(i, i ^ j) for i in range(size)])  42.1 us
    ppermute x34, starting transfers between devices, swap(): return lax.ppermute(x, axis, [(i, i ^ j) for i in range(size)])  29.9 us
    unnamed x46, local copies, waits for them, and re-layouts  7.43 us
    pallas_call x1, Pallas kernels, cand_sums(): pl.pallas_call(kern, grid_spec=pltpu.PrefetchScalarGridSpec(num_scalar_pr...  3.63 us
  transfers between devices with their start and end apart: 34, of which 11 were waited for; matrix products, arithmetic and copies ran while one was open for 1% of the time, Pallas kernels for 31%

profile of v5, /device:TPU:0, one launch (start us, length us, event | category | flops | bytes accessed | tf_op | source)
XLA Modules:
  0.0 139.3 jit_solution(9354037816802316315)
XLA Ops:
  0.6 0.9 slice.12
  1.5 3.1 %collective-permute-start.1 = (bf16[1,256,256]{2,1,0:T(8,128)(2,1)S(1)}, bf16[1,256,256]{2,1,0:T(8,128)(2,1)S(1)}, u32[]{:S(2)}, u32[]{:S(2)}) collective-permute-start(bf16[1,256,256]{2,1,0:T(8,128)(2,1)S(1)} %slice.12), channel_id=1, source_target_pairs={{0,8},{4,12},{8,0},{12,4},{1,9},{5,13},{9,1},{13,5},{2,10},{6,14},... | collective-permute-start | bytes 393224 | tf_op jit(solution)/shard_map/ppermute | solution.py:33
  4.7 4.3 %collective-permute-done.1.refs_1_ = bf16[1,256,256]{2,1,0:T(8,128)(2,1)S(1)} collective-permute-done((bf16[1,256,256]{2,1,0:T(8,128)(2,1)S(1)}, bf16[1,256,256]{2,1,0:T(8,128)(2,1)S(1)}, u32[]{:S(2)}, u32[]{:S(2)}) %collective-permute-start.1) | collective-permute-done | bytes 131104 | tf_op jit(solution)/shard_map/ppermute | solution.py:33
  9.6 9.2 %shard_map.131.refs_5_.own_ref = f32[512,256]{1,0:T(8,128)S(1)} custom-call(s32[4]{0:T(128)S(1)} %copy-done.20, s32[1]{0:T(128)} %bitcast.place_ref, bf16[4,256,256]{2,1,0:T(8,128)(2,1)} %refs_0_.5, bf16[4,4096,256]{2,1,0:T(8,128)(2,1)} %refs_4_.7, bf16[4,4096,256]{2,1,0:T(8,128)(2,1)} %refs_5_.3), custom_call_target="tpu_custom_call" | custom-call | flops 4294967296 | bytes 8388608 | tf_op jit(solution)/shard_map/pallas_call | solution.py:96
  19.4 8.3 %shard_map.132 = (bf16[256,256]{1,0:T(8,128)(2,1)S(1)}, bf16[256,256]{1,0:T(8,128)(2,1)S(1)}, bf16[256,256]{1,0:T(8,128)(2,1)S(1)}) custom-call(s32[4]{0:T(128)S(1)} %copy-done.20, s32[1]{0:T(128)} %bitcast.place_ref, bf16[4,256,256]{2,1,0:T(8,128)(2,1)S(1)} %collective-permute-done.refs_0_.refs_1_, bf16[1,256,256]{2,1,0:T(8,128)(2,1)S(1)} %collective-permute-done.1.refs_1_, ...), custom_call_target="tpu_custom_call" | custom-call | flops 6442450944 | bytes 4194304 | tf_op jit(solution)/shard_map/pallas_call | solution.py:96
  27.8 1.8 %collective-permute-start.5 = (bf16[256,256]{1,0:T(8,128)(2,1)S(1)}, bf16[256,256]{1,0:T(8,128)(2,1)S(1)}, u32[]{:S(2)}, u32[]{:S(2)}) collective-permute-start(bf16[256,256]{1,0:T(8,128)(2,1)S(1)} %get-tuple-element.22), channel_id=1, source_target_pairs={{0,12},{4,8},{8,4},{12,0},{1,13},{5,9},{9,5},{13,1},{2,14},{6,10},... | collective-permute-start | bytes 393224 | tf_op jit(solution)/shard_map/ppermute | solution.py:33
  29.6 4.6 %collective-permute-done.4.refs_1_ = bf16[256,256]{1,0:T(8,128)(2,1)S(1)} collective-permute-done((bf16[256,256]{1,0:T(8,128)(2,1)S(1)}, bf16[256,256]{1,0:T(8,128)(2,1)S(1)}, u32[]{:S(2)}, u32[]{:S(2)}) %collective-permute-start.4) | collective-permute-done | bytes 131104 | tf_op jit(solution)/shard_map/ppermute | solution.py:33
  34.2 1.7 %collective-permute-done.5.refs_2_ = bf16[256,256]{1,0:T(8,128)(2,1)S(1)} collective-permute-done((bf16[256,256]{1,0:T(8,128)(2,1)S(1)}, bf16[256,256]{1,0:T(8,128)(2,1)S(1)}, u32[]{:S(2)}, u32[]{:S(2)}) %collective-permute-start.5) | collective-permute-done | bytes 131104 | tf_op jit(solution)/shard_map/ppermute | solution.py:33
  36.2 8.3 %shard_map.134 = (bf16[256,256]{1,0:T(8,128)(2,1)S(1)}, bf16[256,256]{1,0:T(8,128)(2,1)S(1)}, bf16[256,256]{1,0:T(8,128)(2,1)S(1)}) custom-call(s32[4]{0:T(128)S(1)} %copy-done.20, s32[1]{0:T(128)} %bitcast.place_ref, bf16[4,256,256]{2,1,0:T(8,128)(2,1)S(1)} %collective-permute-done.refs_0_.refs_1_, ...), custom_call_target="tpu_custom_call" | custom-call | flops 6442450944 | bytes 4194304 | tf_op jit(solution)/shard_map/pallas_call | solution.py:96
  45.2 17.0 %shard_map.136 = (f32[384,256]{1,0:T(8,128)S(1)}, bf16[384,256]{1,0:T(8,128)(2,1)S(1)}, bf16[384,256]{1,0:T(8,128)(2,1)S(1)}, bf16[384,256]{1,0:T(8,128)(2,1)S(1)}) custom-call(s32[4]{0:T(128)S(1)} %copy-done.20, s32[1]{0:T(128)} %bitcast.place_ref, bf16[4,256,256]{2,1,0:T(8,128)(2,1)} %refs_0_.5, ...), custom_call_target="tpu_custom_call" | custom-call | flops 12884901888 | bytes 8388608 | tf_op jit(solution)/shard_map/pallas_call | solution.py:96
  62.4 1.7 %collective-permute-start.12 = (bf16[384,256]{1,0:T(8,128)(2,1)S(1)}, bf16[384,256]{1,0:T(8,128)(2,1)S(1)}, u32[]{:S(2)}, u32[]{:S(2)}) collective-permute-start(bf16[384,256]{1,0:T(8,128)(2,1)S(1)} %get-tuple-element.28), channel_id=1, source_target_pairs={{0,8},{4,12},{8,0},{12,4},{1,9},{5,13},{9,1},{13,5},{2,10},{6,14},... | collective-permute-start | bytes 589832 | tf_op jit(solution)/shard_map/ppermute | solution.py:33
  64.2 1.5 %collective-permute-start.9 = (bf16[256,256]{1,0:T(8,128)(2,1)S(1)}, bf16[256,256]{1,0:T(8,128)(2,1)S(1)}, u32[]{:S(2)}, u32[]{:S(2)}) collective-permute-start(bf16[256,256]{1,0:T(8,128)(2,1)S(1)} %get-tuple-element.24), channel_id=1, source_target_pairs={{0,8},{4,12},{8,0},{12,4},{1,9},{5,13},{9,1},{13,5},{2,10},{6,14},... | collective-permute-start | bytes 393224 | tf_op jit(solution)/shard_map/ppermute | solution.py:33
  65.7 2.8 %collective-permute-start.24 = (bf16[256,256]{1,0:T(8,128)(2,1)S(1)}, bf16[256,256]{1,0:T(8,128)(2,1)S(1)}, u32[]{:S(2)}, u32[]{:S(2)}) collective-permute-start(bf16[256,256]{1,0:T(8,128)(2,1)S(1)} %shard_map.133.refs_6_.refs_0_), channel_id=1, source_target_pairs={{0,2},{1,3},{2,0},{3,1},{4,6},{5,7},{6,4},{7,5},{8,10},{9,11},{10,... | collective-permute-start | bytes 393224 | tf_op jit(solution)/shard_map/ppermute | solution.py:33
  68.5 8.2 %collective-permute-done.9.refs_1_ = bf16[256,256]{1,0:T(8,128)(2,1)S(1)} collective-permute-done((bf16[256,256]{1,0:T(8,128)(2,1)S(1)}, bf16[256,256]{1,0:T(8,128)(2,1)S(1)}, u32[]{:S(2)}, u32[]{:S(2)}) %collective-permute-start.9) | collective-permute-done | bytes 131104 | tf_op jit(solution)/shard_map/ppermute | solution.py:33
  76.7 1.5 %collective-permute-start.30 = (bf16[512,256]{1,0:T(8,128)(2,1)S(1)}, bf16[512,256]{1,0:T(8,128)(2,1)S(1)}, u32[]{:S(2)}, u32[]{:S(2)}) collective-permute-start(bf16[512,256]{1,0:T(8,128)(2,1)S(1)} %copy-done.5), channel_id=1, source_target_pairs={{0,8},{4,12},{8,0},{12,4},{1,9},{5,13},{9,1},{13,5},{2,10},{6,14},... | collective-permute-start | bytes 786440 | tf_op jit(solution)/shard_map/ppermute | solution.py:33
  78.5 1.9 %collective-permute-start.23 = (bf16[256,256]{1,0:T(8,128)(2,1)S(1)}, bf16[256,256]{1,0:T(8,128)(2,1)S(1)}, u32[]{:S(2)}, u32[]{:S(2)}) collective-permute-start(bf16[256,256]{1,0:T(8,128)(2,1)S(1)} %shard_map.133.refs_6_.refs_0_), channel_id=1, source_target_pairs={{0,1},{1,0},{2,3},{3,2},{4,5},{5,4},{6,7},{7,6},{8,9},{9,8},{10,11... | collective-permute-start | bytes 393224 | tf_op jit(solution)/shard_map/ppermute | solution.py:33
  81.0 2.9 %collective-permute-start.18 = (bf16[384,256]{1,0:T(8,128)(2,1)S(1)}, bf16[384,256]{1,0:T(8,128)(2,1)S(1)}, u32[]{:S(2)}, u32[]{:S(2)}) collective-permute-start(bf16[384,256]{1,0:T(8,128)(2,1)S(1)} %shard_map.137.refs_0_), channel_id=1, source_target_pairs={{0,2},{1,3},{2,0},{3,1},{4,6},{5,7},{6,4},{7,5},{8,10},{9,11},{10,... | collective-permute-start | bytes 589832 | tf_op jit(solution)/shard_map/ppermute | solution.py:33
  83.9 6.9 %shard_map.138 = (f32[128,256]{1,0:T(8,128)S(1)}, bf16[128,256]{1,0:T(8,128)(2,1)S(1)}, bf16[128,256]{1,0:T(8,128)(2,1)S(1)}, bf16[128,256]{1,0:T(8,128)(2,1)S(1)}) custom-call(s32[4]{0:T(128)S(1)} %copy-done.20, s32[1]{0:T(128)} %bitcast.place_ref, bf16[4,256,256]{2,1,0:T(8,128)(2,1)} %refs_0_.5, ...), custom_call_target="tpu_custom_call" | custom-call | flops 4294967296 | bytes 4194304 | tf_op jit(solution)/shard_map/pallas_call | solution.py:96
  92.1 1.6 %collective-permute-start.26 = (bf16[256,256]{1,0:T(8,128)(2,1)S(1)}, bf16[256,256]{1,0:T(8,128)(2,1)S(1)}, u32[]{:S(2)}, u32[]{:S(2)}) collective-permute-start(bf16[256,256]{1,0:T(8,128)(2,1)S(1)} %shard_map.135.refs_6_.refs_4_), channel_id=1, source_target_pairs={{0,1},{1,0},{2,3},{3,2},{4,5},{5,4},{6,7},{7,6},{8,9},{9,8},{10,11... | collective-permute-start | bytes 393224 | tf_op jit(solution)/shard_map/ppermute | solution.py:33
  93.7 1.7 %collective-permute-done.15.refs_1_ = bf16[128,256]{1,0:T(8,128)(2,1)S(1)} collective-permute-done((bf16[128,256]{1,0:T(8,128)(2,1)S(1)}, bf16[128,256]{1,0:T(8,128)(2,1)S(1)}, u32[]{:S(2)}, u32[]{:S(2)}) %collective-permute-start.15) | collective-permute-done | bytes 65568 | tf_op jit(solution)/shard_map/ppermute | solution.py:33
  95.4 5.4 %collective-permute-done.27.refs_6_ = bf16[256,256]{1,0:T(8,128)(2,1)S(1)} collective-permute-done((bf16[256,256]{1,0:T(8,128)(2,1)S(1)}, bf16[256,256]{1,0:T(8,128)(2,1)S(1)}, u32[]{:S(2)}, u32[]{:S(2)}) %collective-permute-start.27) | collective-permute-done | bytes 131104 | tf_op jit(solution)/shard_map/ppermute | solution.py:33
  100.8 2.0 %collective-permute-start.17 = (bf16[384,256]{1,0:T(8,128)(2,1)S(1)}, bf16[384,256]{1,0:T(8,128)(2,1)S(1)}, u32[]{:S(2)}, u32[]{:S(2)}) collective-permute-start(bf16[384,256]{1,0:T(8,128)(2,1)S(1)} %shard_map.137.refs_0_), channel_id=1, source_target_pairs={{0,1},{1,0},{2,3},{3,2},{4,5},{5,4},{6,7},{7,6},{8,9},{9,8},{10,11... | collective-permute-start | bytes 589832 | tf_op jit(solution)/shard_map/ppermute | solution.py:33
  103.8 2.1 %collective-permute-start.21 = (bf16[128,256]{1,0:T(8,128)(2,1)S(1)}, bf16[128,256]{1,0:T(8,128)(2,1)}, u32[]{:S(2)}, u32[]{:S(2)}) collective-permute-start(bf16[128,256]{1,0:T(8,128)(2,1)S(1)} %shard_map.139.refs_4_), channel_id=1, source_target_pairs={{0,2},{1,3},{2,0},{3,1},{4,6},{5,7},{6,4},{7,5},{8,10},{9,11},{10,... | collective-permute-start | bytes 196616 | tf_op jit(solution)/shard_map/ppermute | solution.py:33
  105.9 7.3 %collective-permute-done.21.refs_6_ = bf16[128,256]{1,0:T(8,128)(2,1)} collective-permute-done((bf16[128,256]{1,0:T(8,128)(2,1)S(1)}, bf16[128,256]{1,0:T(8,128)(2,1)}, u32[]{:S(2)}, u32[]{:S(2)}) %collective-permute-start.21) | collective-permute-done | bytes 65568 | tf_op jit(solution)/shard_map/ppermute | solution.py:33
  113.2 3.2 %collective-permute-start.20 = (bf16[128,256]{1,0:T(8,128)(2,1)S(1)}, bf16[128,256]{1,0:T(8,128)(2,1)}, u32[]{:S(2)}, u32[]{:S(2)}) collective-permute-start(bf16[128,256]{1,0:T(8,128)(2,1)S(1)} %shard_map.139.refs_4_), channel_id=1, source_target_pairs={{0,1},{1,0},{2,3},{3,2},{4,5},{5,4},{6,7},{7,6},{8,9},{9,8},{10,11... | collective-permute-start | bytes 196616 | tf_op jit(solution)/shard_map/ppermute | solution.py:33
  118.0 0.9 copy-done.10
  121.6 0.9 copy-done.18
  123.3 3.6 %cand_sums.1 = (f32[2,512,256]{2,1,0:T(8,128)S(1)}, bf16[2,512,256]{2,1,0:T(8,128)(2,1)S(1)}) custom-call(s32[4]{0:T(128)S(1)} %copy-done.21, s32[1]{0:T(128)} %bitcast.place_ref, s32[1]{0:T(128)} %bitcast.4.col_ref, bf16[384,256]{1,0:T(8,128)(2,1)S(1)} %shard_map.137.refs_0_, bf16[384,256]{1,0:T(8,128)(2,1)S(1)} %collective-permute-done.17.refs_1_, ...), custom_call_target="tpu_custom_call" | custom-call | tf_op jit(solution)/shard_map/cand_sums/pallas_call | solution.py:224
  127.0 1.9 %collective-permute-done.32 = bf16[2,512,256]{2,1,0:T(8,128)(2,1)S(1)} collective-permute-done((bf16[2,512,256]{2,1,0:T(8,128)(2,1)S(1)}, bf16[2,512,256]{2,1,0:T(8,128)(2,1)S(1)}, u32[]{:S(2)}, u32[]{:S(2)}) %collective-permute-start.32) | collective-permute-done | bytes 524320 | tf_op jit(solution)/shard_map/ppermute | solution.py:33
  129.1 1.3 collective-permute-start.33
  131.3 6.2 %collective-permute-done.33.refs_1_ = bf16[1,512,256]{2,1,0:T(8,128)(2,1)S(1)} collective-permute-done((bf16[1,512,256]{2,1,0:T(8,128)(2,1)S(1)}, bf16[1,512,256]{2,1,0:T(8,128)(2,1)S(1)}, u32[]{:S(2)}, u32[]{:S(2)}) %collective-permute-start.33) | collective-permute-done | bytes 262176 | tf_op jit(solution)/shard_map/ppermute | solution.py:33
  137.5 1.9 %gate_cands.1 = bf16[512,256]{1,0:T(8,128)(2,1)} custom-call(s32[4]{0:T(128)S(1)} %copy-done.21, s32[1]{0:T(128)} %bitcast.place_ref, f32[1,512,256]{2,1,0:T(8,128)S(1)} %slice.15.refs_0_, bf16[1,512,256]{2,1,0:T(8,128)(2,1)S(1)} %collective-permute-done.33.refs_1_, f32[1,256]{1,0:T(1,128)S(1)} %bitcast.14, bf16[512,256]{1,0:T(8,128)(2,1)S(1)} %copy-done.6), custom_call_target="tpu_custom_call" | custom-call | tf_op jit(solution)/shard_map/gate_cands/pallas_call | solution.py:265
  (99 shorter events, 11.9 us)
Async XLA Ops:
  1.5 7.4 %collective-permute-start.1 = (bf16[1,256,256]{2,1,0:T(8,128)(2,1)S(1)}, bf16[1,256,256]{2,1,0:T(8,128)(2,1)S(1)}, u32[]{:S(2)}, u32[]{:S(2)}) collective-permute-start(bf16[1,256,256]{2,1,0:T(8,128)(2,1)S(1)} %slice.12), channel_id=1, source_target_pairs={{0,8},{4,12},{8,0},{12,4},{1,9},{5,13},{9,1},{13,5},{2,10},{6,14},... | collective-permute-start | bytes 393224 | tf_op jit(solution)/shard_map/ppermute | solution.py:33
  4.6 14.7 %collective-permute-start.6 = (bf16[4,256,256]{2,1,0:T(8,128)(2,1)}, bf16[4,256,256]{2,1,0:T(8,128)(2,1)S(1)}, u32[]{:S(2)}, u32[]{:S(2)}) collective-permute-start(bf16[4,256,256]{2,1,0:T(8,128)(2,1)} %refs_0_.5), channel_id=1, source_target_pairs={{0,8},{4,12},{8,0},{12,4},{1,9},{5,13},{9,1},{13,5},{2,10},{6,14},... | collective-permute-start | bytes 1572872 | tf_op jit(solution)/shard_map/ppermute | solution.py:33
  4.7 14.7 %collective-permute-start = (bf16[4,256,256]{2,1,0:T(8,128)(2,1)}, bf16[4,256,256]{2,1,0:T(8,128)(2,1)S(1)}, u32[]{:S(2)}, u32[]{:S(2)}) collective-permute-start(bf16[4,256,256]{2,1,0:T(8,128)(2,1)} %refs_0_.5), channel_id=1, source_target_pairs={{0,4},{4,0},{8,12},{12,8},{1,5},{5,1},{9,13},{13,9},{2,6},{6,2},{1... | collective-permute-start | bytes 1572872 | tf_op jit(solution)/shard_map/ppermute | solution.py:33
  9.0 10.4 %collective-permute-start.2 = (bf16[1,256,256]{2,1,0:T(8,128)(2,1)S(1)}, bf16[1,256,256]{2,1,0:T(8,128)(2,1)S(1)}, u32[]{:S(2)}, u32[]{:S(2)}) collective-permute-start(bf16[1,256,256]{2,1,0:T(8,128)(2,1)S(1)} %collective-permute-done.1.refs_1_), channel_id=1, source_target_pairs={{0,4},{4,0},{8,12},{12,8},{1,5},{5,1},{9,13},{13,9},{2,6},{6,2},{1... | collective-permute-start | bytes 393224 | tf_op jit(solution)/shard_map/ppermute | solution.py:33
  19.3 16.8 %collective-permute-start.7 = (bf16[4,256,256]{2,1,0:T(8,128)(2,1)S(1)}, bf16[4,256,256]{2,1,0:T(8,128)(2,1)S(1)}, u32[]{:S(2)}, u32[]{:S(2)}) collective-permute-start(bf16[4,256,256]{2,1,0:T(8,128)(2,1)S(1)} %collective-permute-done.6.refs_1_.refs_2_), channel_id=1, source_target_pairs={{0,4},{4,0},{8,12},{12,8},{1,5},{5,1},{9,13},{13,9},{2,6},{6,2},{1... | collective-permute-start | bytes 1572872 | tf_op jit(solution)/shard_map/ppermute | solution.py:33
  27.8 6.4 %collective-permute-start.4 = (bf16[256,256]{1,0:T(8,128)(2,1)S(1)}, bf16[256,256]{1,0:T(8,128)(2,1)S(1)}, u32[]{:S(2)}, u32[]{:S(2)}) collective-permute-start(bf16[256,256]{1,0:T(8,128)(2,1)S(1)} %get-tuple-element.21), channel_id=1, source_target_pairs={{0,8},{4,12},{8,0},{12,4},{1,9},{5,13},{9,1},{13,5},{2,10},{6,14},... | collective-permute-start | bytes 393224 | tf_op jit(solution)/shard_map/ppermute | solution.py:33
  27.8 8.1 %collective-permute-start.5 = (bf16[256,256]{1,0:T(8,128)(2,1)S(1)}, bf16[256,256]{1,0:T(8,128)(2,1)S(1)}, u32[]{:S(2)}, u32[]{:S(2)}) collective-permute-start(bf16[256,256]{1,0:T(8,128)(2,1)S(1)} %get-tuple-element.22), channel_id=1, source_target_pairs={{0,12},{4,8},{8,4},{12,0},{1,13},{5,9},{9,5},{13,1},{2,14},{6,10},... | collective-permute-start | bytes 393224 | tf_op jit(solution)/shard_map/ppermute | solution.py:33
  44.5 19.7 %collective-permute-start.8 = (bf16[256,256]{1,0:T(8,128)(2,1)S(1)}, bf16[256,256]{1,0:T(8,128)(2,1)S(1)}, u32[]{:S(2)}, u32[]{:S(2)}) collective-permute-start(bf16[256,256]{1,0:T(8,128)(2,1)S(1)} %get-tuple-element.23.refs_7_), channel_id=1, source_target_pairs={{0,4},{4,0},{8,12},{12,8},{1,5},{5,1},{9,13},{13,9},{2,6},{6,2},{1... | collective-permute-start | bytes 393224 | tf_op jit(solution)/shard_map/ppermute | solution.py:33
  44.9 20.7 %collective-permute-start.10 = (bf16[256,256]{1,0:T(8,128)(2,1)S(1)}, bf16[256,256]{1,0:T(8,128)(2,1)S(1)}, u32[]{:S(2)}, u32[]{:S(2)}) collective-permute-start(bf16[256,256]{1,0:T(8,128)(2,1)S(1)} %get-tuple-element.25), channel_id=1, source_target_pairs={{0,12},{4,8},{8,4},{12,0},{1,13},{5,9},{9,5},{13,1},{2,14},{6,10},... | collective-permute-start | bytes 393224 | tf_op jit(solution)/shard_map/ppermute | solution.py:33
  62.3 16.2 %collective-permute-start.11 = (bf16[384,256]{1,0:T(8,128)(2,1)S(1)}, bf16[384,256]{1,0:T(8,128)(2,1)S(1)}, u32[]{:S(2)}, u32[]{:S(2)}) collective-permute-start(bf16[384,256]{1,0:T(8,128)(2,1)S(1)} %get-tuple-element.27), channel_id=1, source_target_pairs={{0,4},{4,0},{8,12},{12,8},{1,5},{5,1},{9,13},{13,9},{2,6},{6,2},{1... | collective-permute-start | bytes 589832 | tf_op jit(solution)/shard_map/ppermute | solution.py:33
  62.4 17.9 %collective-permute-start.12 = (bf16[384,256]{1,0:T(8,128)(2,1)S(1)}, bf16[384,256]{1,0:T(8,128)(2,1)S(1)}, u32[]{:S(2)}, u32[]{:S(2)}) collective-permute-start(bf16[384,256]{1,0:T(8,128)(2,1)S(1)} %get-tuple-element.28), channel_id=1, source_target_pairs={{0,8},{4,12},{8,0},{12,4},{1,9},{5,13},{9,1},{13,5},{2,10},{6,14},... | collective-permute-start | bytes 589832 | tf_op jit(solution)/shard_map/ppermute | solution.py:33
  64.2 16.4 %collective-permute-start.13 = (bf16[384,256]{1,0:T(8,128)(2,1)S(1)}, bf16[384,256]{1,0:T(8,128)(2,1)S(1)}, u32[]{:S(2)}, u32[]{:S(2)}) collective-permute-start(bf16[384,256]{1,0:T(8,128)(2,1)S(1)} %get-tuple-element.29), channel_id=1, source_target_pairs={{0,12},{4,8},{8,4},{12,0},{1,13},{5,9},{9,5},{13,1},{2,14},{6,10},... | collective-permute-start | bytes 589832 | tf_op jit(solution)/shard_map/ppermute | solution.py:33
  64.2 12.5 %collective-permute-start.9 = (bf16[256,256]{1,0:T(8,128)(2,1)S(1)}, bf16[256,256]{1,0:T(8,128)(2,1)S(1)}, u32[]{:S(2)}, u32[]{:S(2)}) collective-permute-start(bf16[256,256]{1,0:T(8,128)(2,1)S(1)} %get-tuple-element.24), channel_id=1, source_target_pairs={{0,8},{4,12},{8,0},{12,4},{1,9},{5,13},{9,1},{13,5},{2,10},{6,14},... | collective-permute-start | bytes 393224 | tf_op jit(solution)/shard_map/ppermute | solution.py:33
  65.7 12.7 %collective-permute-start.24 = (bf16[256,256]{1,0:T(8,128)(2,1)S(1)}, bf16[256,256]{1,0:T(8,128)(2,1)S(1)}, u32[]{:S(2)}, u32[]{:S(2)}) collective-permute-start(bf16[256,256]{1,0:T(8,128)(2,1)S(1)} %shard_map.133.refs_6_.refs_0_), channel_id=1, source_target_pairs={{0,2},{1,3},{2,0},{3,1},{4,6},{5,7},{6,4},{7,5},{8,10},{9,11},{10,... | collective-permute-start | bytes 393224 | tf_op jit(solution)/shard_map/ppermute | solution.py:33
  76.7 14.1 %collective-permute-start.30 = (bf16[512,256]{1,0:T(8,128)(2,1)S(1)}, bf16[512,256]{1,0:T(8,128)(2,1)S(1)}, u32[]{:S(2)}, u32[]{:S(2)}) collective-permute-start(bf16[512,256]{1,0:T(8,128)(2,1)S(1)} %copy-done.5), channel_id=1, source_target_pairs={{0,8},{4,12},{8,0},{12,4},{1,9},{5,13},{9,1},{13,5},{2,10},{6,14},... | collective-permute-start | bytes 786440 | tf_op jit(solution)/shard_map/ppermute | solution.py:33
  78.4 12.5 %collective-permute-start.29 = (bf16[512,256]{1,0:T(8,128)(2,1)S(1)}, bf16[512,256]{1,0:T(8,128)(2,1)S(1)}, u32[]{:S(2)}, u32[]{:S(2)}) collective-permute-start(bf16[512,256]{1,0:T(8,128)(2,1)S(1)} %copy-done.5), channel_id=1, source_target_pairs={{0,4},{4,0},{8,12},{12,8},{1,5},{5,1},{9,13},{13,9},{2,6},{6,2},{1... | collective-permute-start | bytes 786440 | tf_op jit(solution)/shard_map/ppermute | solution.py:33
  78.5 13.0 %collective-permute-start.23 = (bf16[256,256]{1,0:T(8,128)(2,1)S(1)}, bf16[256,256]{1,0:T(8,128)(2,1)S(1)}, u32[]{:S(2)}, u32[]{:S(2)}) collective-permute-start(bf16[256,256]{1,0:T(8,128)(2,1)S(1)} %shard_map.133.refs_6_.refs_0_), channel_id=1, source_target_pairs={{0,1},{1,0},{2,3},{3,2},{4,5},{5,4},{6,7},{7,6},{8,9},{9,8},{10,11... | collective-permute-start | bytes 393224 | tf_op jit(solution)/shard_map/ppermute | solution.py:33
  80.4 11.3 %collective-permute-start.25 = (bf16[256,256]{1,0:T(8,128)(2,1)S(1)}, bf16[256,256]{1,0:T(8,128)(2,1)S(1)}, u32[]{:S(2)}, u32[]{:S(2)}) collective-permute-start(bf16[256,256]{1,0:T(8,128)(2,1)S(1)} %collective-permute-done.24.refs_2_), channel_id=1, source_target_pairs={{0,1},{1,0},{2,3},{3,2},{4,5},{5,4},{6,7},{7,6},{8,9},{9,8},{10,11... | collective-permute-start | bytes 393224 | tf_op jit(solution)/shard_map/ppermute | solution.py:33
  81.0 21.9 %collective-permute-start.18 = (bf16[384,256]{1,0:T(8,128)(2,1)S(1)}, bf16[384,256]{1,0:T(8,128)(2,1)S(1)}, u32[]{:S(2)}, u32[]{:S(2)}) collective-permute-start(bf16[384,256]{1,0:T(8,128)(2,1)S(1)} %shard_map.137.refs_0_), channel_id=1, source_target_pairs={{0,2},{1,3},{2,0},{3,1},{4,6},{5,7},{6,4},{7,5},{8,10},{9,11},{10,... | collective-permute-start | bytes 589832 | tf_op jit(solution)/shard_map/ppermute | solution.py:33
  90.9 4.5 %collective-permute-start.15 = (bf16[128,256]{1,0:T(8,128)(2,1)S(1)}, bf16[128,256]{1,0:T(8,128)(2,1)S(1)}, u32[]{:S(2)}, u32[]{:S(2)}) collective-permute-start(bf16[128,256]{1,0:T(8,128)(2,1)S(1)} %get-tuple-element.32), channel_id=1, source_target_pairs={{0,8},{4,12},{8,0},{12,4},{1,9},{5,13},{9,1},{13,5},{2,10},{6,14},... | collective-permute-start | bytes 196616 | tf_op jit(solution)/shard_map/ppermute | solution.py:33
  91.5 9.3 %collective-permute-start.27 = (bf16[256,256]{1,0:T(8,128)(2,1)S(1)}, bf16[256,256]{1,0:T(8,128)(2,1)S(1)}, u32[]{:S(2)}, u32[]{:S(2)}) collective-permute-start(bf16[256,256]{1,0:T(8,128)(2,1)S(1)} %shard_map.135.refs_6_.refs_4_), channel_id=1, source_target_pairs={{0,2},{1,3},{2,0},{3,1},{4,6},{5,7},{6,4},{7,5},{8,10},{9,11},{10,... | collective-permute-start | bytes 393224 | tf_op jit(solution)/shard_map/ppermute | solution.py:33
  91.6 31.6 %collective-permute-start.31 = (bf16[512,256]{1,0:T(8,128)(2,1)S(1)}, bf16[512,256]{1,0:T(8,128)(2,1)S(1)}, u32[]{:S(2)}, u32[]{:S(2)}) collective-permute-start(bf16[512,256]{1,0:T(8,128)(2,1)S(1)} %collective-permute-done.30.refs_14_), channel_id=1, source_target_pairs={{0,4},{4,0},{8,12},{12,8},{1,5},{5,1},{9,13},{13,9},{2,6},{6,2},{1... | collective-permute-start | bytes 786440 | tf_op jit(solution)/shard_map/ppermute | solution.py:33
  92.1 11.0 %collective-permute-start.26 = (bf16[256,256]{1,0:T(8,128)(2,1)S(1)}, bf16[256,256]{1,0:T(8,128)(2,1)S(1)}, u32[]{:S(2)}, u32[]{:S(2)}) collective-permute-start(bf16[256,256]{1,0:T(8,128)(2,1)S(1)} %shard_map.135.refs_6_.refs_4_), channel_id=1, source_target_pairs={{0,1},{1,0},{2,3},{3,2},{4,5},{5,4},{6,7},{7,6},{8,9},{9,8},{10,11... | collective-permute-start | bytes 393224 | tf_op jit(solution)/shard_map/ppermute | solution.py:33
  95.4 5.5 %collective-permute-start.16 = (bf16[128,256]{1,0:T(8,128)(2,1)S(1)}, bf16[128,256]{1,0:T(8,128)(2,1)S(1)}, u32[]{:S(2)}, u32[]{:S(2)}) collective-permute-start(bf16[128,256]{1,0:T(8,128)(2,1)S(1)} %get-tuple-element.33), channel_id=1, source_target_pairs={{0,12},{4,8},{8,4},{12,0},{1,13},{5,9},{9,5},{13,1},{2,14},{6,10},... | collective-permute-start | bytes 196616 | tf_op jit(solution)/shard_map/ppermute | solution.py:33
  100.8 15.6 %collective-permute-start.28 = (bf16[256,256]{1,0:T(8,128)(2,1)S(1)}, bf16[256,256]{1,0:T(8,128)(2,1)S(1)}, u32[]{:S(2)}, u32[]{:S(2)}) collective-permute-start(bf16[256,256]{1,0:T(8,128)(2,1)S(1)} %collective-permute-done.27.refs_6_), channel_id=1, source_target_pairs={{0,1},{1,0},{2,3},{3,2},{4,5},{5,4},{6,7},{7,6},{8,9},{9,8},{10,11... | collective-permute-start | bytes 393224 | tf_op jit(solution)/shard_map/ppermute | solution.py:33
  100.8 22.4 %collective-permute-start.17 = (bf16[384,256]{1,0:T(8,128)(2,1)S(1)}, bf16[384,256]{1,0:T(8,128)(2,1)S(1)}, u32[]{:S(2)}, u32[]{:S(2)}) collective-permute-start(bf16[384,256]{1,0:T(8,128)(2,1)S(1)} %shard_map.137.refs_0_), channel_id=1, source_target_pairs={{0,1},{1,0},{2,3},{3,2},{4,5},{5,4},{6,7},{7,6},{8,9},{9,8},{10,11... | collective-permute-start | bytes 589832 | tf_op jit(solution)/shard_map/ppermute | solution.py:33
  102.9 20.4 %collective-permute-start.19 = (bf16[384,256]{1,0:T(8,128)(2,1)S(1)}, bf16[384,256]{1,0:T(8,128)(2,1)}, u32[]{:S(2)}, u32[]{:S(2)}) collective-permute-start(bf16[384,256]{1,0:T(8,128)(2,1)S(1)} %collective-permute-done.18.refs_2_), channel_id=1, source_target_pairs={{0,1},{1,0},{2,3},{3,2},{4,5},{5,4},{6,7},{7,6},{8,9},{9,8},{10,11... | collective-permute-start | bytes 589832 | tf_op jit(solution)/shard_map/ppermute | solution.py:33
  103.8 9.4 %collective-permute-start.21 = (bf16[128,256]{1,0:T(8,128)(2,1)S(1)}, bf16[128,256]{1,0:T(8,128)(2,1)}, u32[]{:S(2)}, u32[]{:S(2)}) collective-permute-start(bf16[128,256]{1,0:T(8,128)(2,1)S(1)} %shard_map.139.refs_4_), channel_id=1, source_target_pairs={{0,2},{1,3},{2,0},{3,1},{4,6},{5,7},{6,4},{7,5},{8,10},{9,11},{10,... | collective-permute-start | bytes 196616 | tf_op jit(solution)/shard_map/ppermute | solution.py:33
  113.2 10.1 %collective-permute-start.20 = (bf16[128,256]{1,0:T(8,128)(2,1)S(1)}, bf16[128,256]{1,0:T(8,128)(2,1)}, u32[]{:S(2)}, u32[]{:S(2)}) collective-permute-start(bf16[128,256]{1,0:T(8,128)(2,1)S(1)} %shard_map.139.refs_4_), channel_id=1, source_target_pairs={{0,1},{1,0},{2,3},{3,2},{4,5},{5,4},{6,7},{7,6},{8,9},{9,8},{10,11... | collective-permute-start | bytes 196616 | tf_op jit(solution)/shard_map/ppermute | solution.py:33
  117.0 6.2 %collective-permute-start.22 = (bf16[128,256]{1,0:T(8,128)(2,1)}, bf16[128,256]{1,0:T(8,128)(2,1)}, u32[]{:S(2)}, u32[]{:S(2)}) collective-permute-start(bf16[128,256]{1,0:T(8,128)(2,1)} %collective-permute-done.21.refs_6_), channel_id=1, source_target_pairs={{0,1},{1,0},{2,3},{3,2},{4,5},{5,4},{6,7},{7,6},{8,9},{9,8},{10,11... | collective-permute-start | bytes 196616 | tf_op jit(solution)/shard_map/ppermute | solution.py:33
  126.9 2.0 %collective-permute-start.32 = (bf16[2,512,256]{2,1,0:T(8,128)(2,1)S(1)}, bf16[2,512,256]{2,1,0:T(8,128)(2,1)S(1)}, u32[]{:S(2)}, u32[]{:S(2)}) collective-permute-start(bf16[2,512,256]{2,1,0:T(8,128)(2,1)S(1)} %get-tuple-element.37), channel_id=1, source_target_pairs={{0,4},{4,0},{8,12},{12,8},{1,5},{5,1},{9,13},{13,9},{2,6},{6,2},{1... | collective-permute-start | bytes 1572872 | tf_op jit(solution)/shard_map/ppermute | solution.py:33
  129.1 8.4 %collective-permute-start.33 = (bf16[1,512,256]{2,1,0:T(8,128)(2,1)S(1)}, bf16[1,512,256]{2,1,0:T(8,128)(2,1)S(1)}, u32[]{:S(2)}, u32[]{:S(2)}) collective-permute-start(bf16[1,512,256]{2,1,0:T(8,128)(2,1)S(1)} %slice.18), channel_id=1, source_target_pairs={{0,8},{4,12},{8,0},{12,4},{1,9},{5,13},{9,1},{13,5},{2,10},{6,14},... | collective-permute-start | bytes 786440 | tf_op jit(solution)/shard_map/ppermute | solution.py:33
  (25 other events, 378.9 us)
